TPU v7x, 512 devices: a whole 4x8x8 slice. The times are simulated.
512 devices in a mesh: rows: 32 (over z, x), piv: 16 (over y, core).
Axes of the slice: x: 4, y: 8, z: 8, core: 2. Of those that a mesh axis runs over, the one named last changes fastest.
Arguments:
- ancestor_sol: float32 [1024, 32768], P('piv', 'rows'), may hold values from -6 to 6
- front_map: int32 [256], P('rows'), may hold values from 0 to 255, each once
- lower_panel: float32 [32768, 12288], P('rows', 'piv'), may hold values from -0.03125 to 0.03125
- inverse_factor: float32 [12288, 12288], P('piv', 'rows'), as said below
- right_side: float32 [1024, 12288], P(None, ('piv', 'rows')), may hold values from -6 to 6
- child_start: int32 [128], P('rows'), may hold values from 0 to 12287, as said below
- child_len: int32 [128], P('rows'), may hold values from 1 to 128, as said below
Outputs:
- child_blocks: float32 [1024, 16384], P('piv', 'rows')
Inputs may be any that keep to these rules, and one draw needn't show every extreme that they name: Child block c lies within pivots k * 384 to (k + 1) * 384 - 1, with k = c // 4; child_start[c] + child_len[c] <= (k + 1) * 384. `child_len`: child block 0 is full. inverse_factor is lower triangular with a diagonal in [0.5, 2].
All inputs are finite; a program needn't handle non-finite values.
Results may differ from a plain program's by a relative error of at most 0.000088.
Values sent between devices are 32-bit elements; how exact they have to be, the bound alone decides.
No kernel may reach another device: no remote copies, remote signals or barrier semaphores. Data moves between devices by JAX's collectives and lax.ppermute only.
A program may use at most 64 MiB of HBM per device.

v0:
```python
import jax
import jax.numpy as jnp
from jax import lax
from jax.sharding import Mesh
from jax.sharding import PartitionSpec as P

ROW_BLK = 128
CHILD_BLK = 128
ROWS = ("rows_0", "rows_1")
PIV_ROWS = ("piv", "rows_0", "rows_1")


def scatter_axes(value, axes, dim):
    if not axes:
        return value
    nearer = lax.psum_scatter(value, axes[0], scatter_dimension=dim, tiled=True)
    return scatter_axes(nearer, axes[1:], dim)


def gather_axes(value, axes, dim):
    for axis in reversed(axes):
        value = lax.all_gather(value, axis, axis=dim, tiled=True)
    return value


def in_blocks(value, dim, size):
    lengths = value.shape
    parts = value.reshape(*lengths[:dim], size, lengths[dim] // size, *lengths[dim + 1 :])
    return jnp.moveaxis(parts, dim, 0)


def sent_and_summed(value, axis, dim):
    parts = in_blocks(value, dim, lax.axis_size(axis))
    arrived = lax.all_to_all(parts, axis, split_axis=0, concat_axis=0, tiled=True)
    return arrived.sum(axis=0)


def body(ancestor_sol, front_map, lower_panel, inverse_factor, right_side, child_start, child_len):
    local_srcs = ancestor_sol.shape[0]
    count = front_map.shape[0]
    empty = jnp.zeros((local_srcs, count * ROW_BLK), jnp.float32)
    carry = empty
    piece = lax.all_gather(ancestor_sol, ROWS, axis=1, tiled=True)
    width = piece.shape[1]
    for block in range(count):
        offset = front_map[block] * ROW_BLK
        inside = (offset >= 0) & (offset < width)
        taken = lax.dynamic_slice_in_dim(piece, jnp.clip(offset, 0, width - ROW_BLK), ROW_BLK, 1)
        previous = carry[:, block * ROW_BLK : (block + 1) * ROW_BLK]
        carry = carry.at[:, block * ROW_BLK : (block + 1) * ROW_BLK].set(
            jnp.where(inside, taken, previous)
        )
    boundary = lax.all_gather(carry, "piv", axis=0, tiled=True)
    coupled = jnp.dot(
        boundary, lower_panel, precision=lax.Precision.HIGHEST, preferred_element_type=jnp.float32
    )
    span = inverse_factor.shape[1]
    share = right_side - scatter_axes(coupled, ROWS, 1)
    partial_sol = jnp.dot(
        gather_axes(share, ROWS, 1),
        inverse_factor,
        precision=lax.Precision.HIGHEST,
        preferred_element_type=jnp.float32,
    )
    slots = jnp.arange(CHILD_BLK, dtype=jnp.int32)
    local_first = child_start - lax.axis_index(ROWS) * span
    columns = jnp.clip(local_first[:, None] + slots[None, :], 0, span - 1).reshape(-1)
    valid = (slots[None, :] < child_len[:, None]).reshape(-1)[None, :]
    summed = sent_and_summed(partial_sol, "piv", 0)
    picked = jnp.take(summed, columns, axis=1)
    return jnp.where(valid, picked, jnp.zeros_like(picked))


def solution(mesh):
    torus = Mesh(mesh.devices.reshape(8, 4, mesh.shape["piv"]), ("rows_0", "rows_1", "piv"))
    return jax.shard_map(
        body,
        mesh=torus,
        in_specs=(
            P("piv", ROWS),
            P(ROWS),
            P(ROWS, "piv"),
            P("piv", ROWS),
            P(None, PIV_ROWS),
            P(ROWS),
            P(ROWS),
        ),
        out_specs=P("piv", ROWS),
        check_vma=False,
    )
```

profile of v0, /device:TPU:1, one launch (start us, length us, event | category | flops | bytes accessed | tf_op | source)
XLA Modules:
  0.0 392.0 jit_solution(8113103257739380664)
XLA Ops:
  7.3 1.6 fusion.7
  18.5 100.8 %all-gather.4.cloned.1.call-done = f32[64,32768]{1,0:T(8,128)} async-done(((f32[64,1024]{1,0:T(8,128)}), f32[64,32768]{1,0:T(8,128)}) %all-gather.4.cloned.1.call-update) | async-done | bytes 8388624 | tf_op jit(solution)/shard_map/all_gather | solution.py:43
  119.3 1.5 select_select_fusion.5
  120.9 1.6 select_dynamic-update-slice_fusion
  122.4 1.5 fusion
  123.9 1.5 fusion.1
  125.5 1.5 fusion.2
  127.0 1.5 fusion.3
  128.6 1.5 fusion.4
  130.1 0.9 fusion.5
  131.8 42.2 %all-gather.6.cloned.1.call-done = f32[1024,1024]{1,0:T(8,128)} async-done(((f32[64,1024]{1,0:T(8,128)}), f32[1024,1024]{1,0:T(8,128)}) %all-gather.6.cloned.1.call-update) | async-done | bytes 4194320 | tf_op jit(solution)/shard_map/all_gather | solution.py:53
  174.0 13.0 %fusion.8 = f32[1024,768]{0,1:T(8,128)} fusion(f32[1024,1024]{1,0:T(8,128)} %all-gather.6.cloned.1.call-done, f32[1024,768]{1,0:T(8,128)S(1)} %copy-done), kind=kOutput, calls=%fused_computation.33 | convolution fusion | flops 9663676416 | bytes 10485760 | tf_op jit(solution)/shard_map/dot_general | solution.py:54
  187.1 45.9 %reduce-scatter.3.cloned.1.call-done = f32[1024,96]{0,1:T(8,128)} async-done(((f32[1024,768]{0,1:T(8,128)}), f32[1024,96]{0,1:T(8,128)}) %reduce-scatter.3.cloned.1.call-update) | async-done | bytes 393232 | tf_op jit(solution)/shard_map/reduce_scatter | solution.py:16
  233.0 28.4 %reduce-scatter.5.cloned.1.call-done = f32[1024,24]{0,1:T(8,128)} async-done(((f32[1024,96]{0,1:T(8,128)}), f32[1024,24]{0,1:T(8,128)}) %reduce-scatter.5.cloned.1.call-update) | async-done | bytes 98320 | tf_op jit(solution)/shard_map/reduce_scatter | solution.py:16
  261.5 0.9 sub.11
  262.4 10.4 %all_gather.14 = f32[1024,96]{0,1:T(8,128)} all-gather(f32[1024,24]{0,1:T(8,128)S(1)} %sub.11), channel_id=1, replica_groups=mesh['rows_0'=8,'rows_1'=4,'piv'=16] {'rows_1'}, dimensions={1}, use_global_device_ids=true | all-gather | bytes 491520 | tf_op jit(solution)/shard_map/all_gather | solution.py:22
  272.8 53.3 %all-gather.8.cloned.1.call-done = f32[1024,768]{0,1:T(8,128)} async-done(((f32[1024,96]{0,1:T(8,128)}), f32[1024,768]{0,1:T(8,128)}) %all-gather.8.cloned.1.call-update) | async-done | bytes 3145744 | tf_op jit(solution)/shard_map/all_gather | solution.py:22
  326.1 7.9 %fusion.9 = f32[1024,384]{1,0:T(8,128)} fusion(f32[1024,768]{0,1:T(8,128)} %all-gather.8.cloned.1.call-done, f32[768,384]{1,0:T(8,128)} %param.26), kind=kOutput, calls=%fused_computation.34 | convolution fusion | flops 3623878656 | bytes 5898240 | tf_op jit(solution)/shard_map/dot_general | solution.py:59
  334.0 7.6 %all-to-all-start = ((f32[16,64,384]{2,1,0:T(8,128)}), f32[16,64,384]{2,1,0:T(8,128)}, u32[]{:S(2)}, u32[]{:S(2)}) async-start(f32[16,64,384]{2,1,0:T(8,128)} %bitcast.31), calls=%async_computation.2 | async-start | bytes 3145728 | tf_op jit(solution)/shard_map/all_to_all | solution.py:34
  341.9 38.4 %all-to-all-done = f32[16,64,384]{2,1,0:T(8,128)} async-done(((f32[16,64,384]{2,1,0:T(8,128)}), f32[16,64,384]{2,1,0:T(8,128)}, u32[]{:S(2)}, u32[]{:S(2)}) %all-to-all-start) | async-done | bytes 1572896 | tf_op jit(solution)/shard_map/all_to_all | solution.py:34
  380.2 1.5 reduce_sum.9
  381.9 1.6 gather_fusion
  383.5 1.1 select_bitcast_fusion
  384.7 0.8 copy.10
  (35 shorter events, 6.6 us)
Async XLA Ops:
  6.5 167.4 %copy-start = (f32[1024,768]{1,0:T(8,128)S(1)}, f32[1024,768]{1,0:T(8,128)}, u32[]{:S(2)}) copy-start(f32[1024,768]{1,0:T(8,128)} %param.25) | copy-start | bytes 9437188
  6.5 112.8 %all-gather.4.cloned.1.call-start = ((), (), s32[]{:S(2)}) async-start(), calls=%async_computation.3 | async-start | bytes 8650752 | tf_op jit(solution)/shard_map/all_gather | solution.py:43
  7.3 166.7 %all-gather.6.cloned.1.call-start = ((), (), s32[]{:S(2)}) async-start(), calls=%async_computation.4 | async-start | bytes 4456448 | tf_op jit(solution)/shard_map/all_gather | solution.py:53
  131.0 0.7 copy-start.1
  131.7 101.2 %reduce-scatter.3.cloned.1.call-start = ((), (), s32[]{:S(2)}) async-start(), calls=%async_computation.5 | async-start | bytes 3538944 | tf_op jit(solution)/shard_map/reduce_scatter | solution.py:16
  187.0 74.5 %copy-start.2 = (f32[1024,24]{0,1:T(8,128)S(1)}, f32[1024,24]{0,1:T(8,128)}, u32[]{:S(2)}) copy-start(f32[1024,24]{0,1:T(8,128)} %param.27) | copy-start | bytes 294916
  187.0 74.4 %reduce-scatter.5.cloned.1.call-start = ((), (), s32[]{:S(2)}) async-start(), calls=%async_computation.6 | async-start | bytes 491520 | tf_op jit(solution)/shard_map/reduce_scatter | solution.py:16
  233.0 93.1 %all-gather.8.cloned.1.call-start = ((), (), s32[]{:S(2)}) async-start(), calls=%async_computation.7 | async-start | bytes 3538944 | tf_op jit(solution)/shard_map/all_gather | solution.py:22
  272.8 68.8 %copy-start.3 = (s32[4]{0:T(128)S(1)}, s32[4]{0:T(128)}, u32[]{:S(2)}) copy-start(s32[4]{0:T(128)} %param.28) | copy-start | bytes 52
  272.8 69.0 %copy-start.4 = (s32[4]{0:T(128)S(1)}, s32[4]{0:T(128)}, u32[]{:S(2)}) copy-start(s32[4]{0:T(128)} %param.29) | copy-start | bytes 52
  334.0 46.2 %all-to-all-start = ((f32[16,64,384]{2,1,0:T(8,128)}), f32[16,64,384]{2,1,0:T(8,128)}, u32[]{:S(2)}, u32[]{:S(2)}) async-start(f32[16,64,384]{2,1,0:T(8,128)} %bitcast.31), calls=%async_computation.2 | async-start | bytes 3145728 | tf_op jit(solution)/shard_map/all_to_all | solution.py:34
Sparse Core Ops, SparseCore 0:
  10.5 108.7 all-gather.3
  131.8 42.0 all-gather.5
  187.1 45.7 reduce-scatter.2
  235.6 25.7 reduce-scatter.4
  272.9 53.1 all-gather.7
where the time goes:
time: 393 us; the launch traced here: 392 us
  waiting for transfers between devices  310 us (79%)
  matrix products  21 us (5%)
  other arithmetic  20 us (5%)
  between operations  18.2 us (5%)
  blocking collectives  10.4 us (3%)
  starting transfers between devices  7.75 us (2%)
  local copies, waits for them, and re-layouts  4.88 us (1%)
    all_gather x1, waiting for transfers between devices, body(): piece = lax.all_gather(ancestor_sol, ROWS, axis=1, tiled=True)  101 us
    reduce_scatter x2, waiting for transfers between devices, scatter_axes(): nearer = lax.psum_scatter(value, axes[0], scatter_dimension=dim, tiled=True)  74.3 us
    all_gather x1, waiting for transfers between devices, gather_axes(): value = lax.all_gather(value, axis, axis=dim, tiled=True)  53.3 us
    all_gather x1, waiting for transfers between devices, body(): boundary = lax.all_gather(carry, 'piv', axis=0, tiled=True)  42.2 us
    all_to_all x1, waiting for transfers between devices, sent_and_summed(): lax.all_to_all(parts, axis, split_axis=0, concat_axis=0, tiled=True)  38.4 us
    dot_general x1, matrix products, body(): jnp.dot(boundary, lower_panel, precision=lax.Precision.HIGHEST, preferred...  13 us
    all_gather x1, blocking collectives, gather_axes(): value = lax.all_gather(value, axis, axis=dim, tiled=True)  10.4 us
    scatter x7, other arithmetic, body(): carry.at[:, block * ROW_BLK:(block + 1) * ROW_BLK]  10.1 us
  transfers between devices with their start and end apart: 6, of which 6 were waited for; matrix products, arithmetic and copies ran while one was open for 2% of the time, Pallas kernels for 0%

commit v1 on v0

v1 whole, which is shorter than its diff:
```python
import jax
import jax.numpy as jnp
from jax import lax
from jax.experimental import pallas as pl
from jax.experimental.pallas import tpu as pltpu
from jax.sharding import Mesh
from jax.sharding import PartitionSpec as P

BLK = 128
ROWS = ("z", "x")
PIV = ("y", "c")
VMEM = pl.BlockSpec(memory_space=pltpu.VMEM)
SMEM = pl.BlockSpec(memory_space=pltpu.SMEM)


def exchange(value, axes):
    return lax.all_to_all(value, axes, split_axis=0, concat_axis=0, tiled=True)


def spread(value, axis):
    count = lax.axis_size(axis)
    return exchange(jnp.broadcast_to(value[None], (count, *value.shape)), axis)


def pack_kernel(count, maps, column, sends):
    across = maps.shape[0]
    for dest in range(across):
        for slot in range(count):
            block = maps[dest, slot]
            level = lax.div(block, count * across)
            offset = pl.multiple_of(lax.rem(block, count) * BLK, BLK)
            sends[dest, :, slot * BLK : (slot + 1) * BLK] = column[level, :, pl.ds(offset, BLK)]


def pick_kernel(count, own, arrived, boundary):
    across = arrived.shape[0]
    for slot in range(count):
        origin = lax.rem(lax.div(own[slot], count), across)
        cols = slice(slot * BLK, (slot + 1) * BLK)
        boundary[:, cols] = arrived[origin, :, cols]


def child_kernel(first, length, pieces, children, summed):
    quarters, _, rows, span = pieces.shape
    padded = summed.shape[1]
    for quarter in range(quarters):
        own = slice(quarter * rows, (quarter + 1) * rows)
        summed[own, :span] = jnp.sum(pieces[quarter], axis=0)
    summed[:, span:] = jnp.zeros((quarters * rows, padded - span), jnp.float32)
    lane = lax.broadcasted_iota(jnp.int32, (quarters * rows, BLK), 1)
    for child in range(first.shape[0]):
        offset = jnp.clip(first[child], 0, span - 1)
        tile = lax.div(offset, BLK)
        window = summed[:, pl.ds(pl.multiple_of(tile * BLK, BLK), 2 * BLK)]
        shift = lax.rem(2 * BLK - (offset - tile * BLK), 2 * BLK)
        moved = pltpu.roll(window, shift, 1)[:, :BLK]
        children[:, child * BLK : (child + 1) * BLK] = jnp.where(
            lane < length[child], moved, jnp.zeros_like(moved)
        )


def body(ancestor_sol, front_map, lower_panel, inverse_factor, right_side, child_start, child_len):
    deep, across, tall, cores = (lax.axis_size(a) for a in ("z", "x", "y", "c"))
    srcs, width = ancestor_sol.shape
    count = front_map.shape[0]
    pivots, span = inverse_factor.shape
    total = right_side.shape[0]
    piv_devs = tall * cores
    part = srcs // across
    quarter = total // across
    me = lax.axis_index(ROWS)

    maps = spread(front_map, "x").reshape(across, count)
    column = lax.all_gather(ancestor_sol, "z", axis=0, tiled=False)
    half = pivots // 2
    inverse_lo = spread(inverse_factor[:half], "x")
    own_share = right_side.shape[1]
    place = (
        jnp.arange(pivots, dtype=jnp.int32)[None, :]
        == me * own_share + jnp.arange(own_share, dtype=jnp.int32)[:, None]
    ).astype(jnp.float32)
    ordered = right_side.reshape(piv_devs, across, part, own_share).swapaxes(0, 1)
    placed = jnp.dot(
        ordered.reshape(total, own_share),
        place,
        precision=lax.Precision.HIGHEST,
        preferred_element_type=jnp.float32,
    )
    column, inverse_lo, maps, placed = lax.optimization_barrier((column, inverse_lo, maps, placed))
    sends = pl.pallas_call(
        lambda *refs: pack_kernel(count, *refs),
        out_shape=jax.ShapeDtypeStruct((across, srcs, width), jnp.float32),
        in_specs=[SMEM, VMEM],
        out_specs=VMEM,
        name="pack",
    )(maps, column)
    arrived = exchange(sends, "x")
    boundary = pl.pallas_call(
        lambda *refs: pick_kernel(count, *refs),
        out_shape=jax.ShapeDtypeStruct((srcs, width), jnp.float32),
        in_specs=[SMEM, VMEM],
        out_specs=VMEM,
        name="pick",
    )(front_map, arrived)
    boundary, upper = lax.optimization_barrier((boundary, inverse_factor[half:]))
    inverse_hi = spread(upper, "x")
    full = lax.all_gather(boundary.reshape(across, part, width), PIV, axis=1, tiled=True)
    full, inverse_hi = lax.optimization_barrier((full, inverse_hi))
    share = placed - jnp.dot(
        full.reshape(total, width),
        lower_panel,
        precision=lax.Precision.HIGH,
        preferred_element_type=jnp.float32,
    )
    reduced = exchange(share.reshape(across, quarter, pivots), "x").sum(axis=0)
    reduced = exchange(reduced.reshape(deep, quarter // deep, pivots), "z").sum(axis=0)
    reduced = spread(reduced, "z").reshape(quarter, pivots)
    inverse = jnp.concatenate(
        [inverse_lo.reshape(across, half, span), inverse_hi.reshape(across, half, span)], axis=1
    )
    partial = jnp.stack(
        [
            jnp.dot(
                reduced,
                inverse[group],
                precision=lax.Precision.HIGH,
                preferred_element_type=jnp.float32,
            )
            for group in range(across)
        ]
    )
    partial = partial.reshape(across, tall, cores, part, span)
    core = lax.axis_index("c")
    kept = lax.dynamic_index_in_dim(partial, core, 2, keepdims=False)
    other = lax.dynamic_index_in_dim(partial, 1 - core, 2, keepdims=False)
    kept = kept + lax.ppermute(other, "c", [(0, 1), (1, 0)])
    pieces = exchange(kept.reshape(across * tall, part, span), ("x", "y"))
    return pl.pallas_call(
        child_kernel,
        out_shape=jax.ShapeDtypeStruct((srcs, child_len.shape[0] * BLK), jnp.float32),
        in_specs=[SMEM, SMEM, VMEM],
        out_specs=VMEM,
        scratch_shapes=[pltpu.VMEM((srcs, span + BLK), jnp.float32)],
        name="children",
    )(child_start - me * span, child_len, pieces.reshape(across, tall, part, span))


def solution(mesh):
    piv = mesh.shape["piv"]
    torus = Mesh(mesh.devices.reshape(8, 4, piv // 2, 2), ("z", "x", "y", "c"))
    return jax.shard_map(
        body,
        mesh=torus,
        in_specs=(
            P(PIV, ROWS),
            P(ROWS),
            P(ROWS, PIV),
            P(PIV, ROWS),
            P(None, PIV + ROWS),
            P(ROWS),
            P(ROWS),
        ),
        out_specs=P(PIV, ROWS),
        check_vma=False,
    )
```

time: 393 us -> 293 us (0.75); the launches traced: 392 us -> 288 us
  waiting for transfers between devices: 310 us -> 83.1 us
  blocking collectives: 10.4 us -> 109 us
  local copies, waits for them, and re-layouts: 4.88 us -> 23.6 us
  starting transfers between devices: 7.75 us -> 24.3 us
  other arithmetic: 20 us -> 7.27 us
  Pallas kernels: 0 us -> 6.74 us
  between operations: 18.2 us -> 13.6 us
    all_gather x3 -> x2, waiting for transfers between devices: 196 us -> 30.5 us  [the longest x1 23.2 us: body(): lax.all_gather(boundary.reshape(across, part, width), PIV, axis=1, tiled=...]
    all_to_all x0 -> x4, blocking collectives: none -> 109 us  [exchange(): return lax.all_to_all(value, axes, split_axis=0, concat_axis=0, tiled=True)]
    reduce_scatter x2 -> x0, waiting for transfers between devices: 74.3 us -> none  [scatter_axes(): nearer = lax.psum_scatter(value, axes[0], scatter_dimension=dim, tiled=True)]
    all_to_all x1 -> x4, waiting for transfers between devices: 38.4 us -> 49.7 us  [exchange(): return lax.all_to_all(value, axes, split_axis=0, concat_axis=0, tiled=True)]
    all_to_all x1 -> x4, starting transfers between devices: 7.59 us -> 18.7 us  [exchange(): return lax.all_to_all(value, axes, split_axis=0, concat_axis=0, tiled=True)]
    all_gather x1 -> x0, blocking collectives: 10.4 us -> none  [gather_axes(): value = lax.all_gather(value, axis, axis=dim, tiled=True)]
    scatter x7 -> x0, other arithmetic: 10.1 us -> none  [body(): carry.at[:, block * ROW_BLK:(block + 1) * ROW_BLK]]
    pallas_call x0 -> x3, Pallas kernels: none -> 6.74 us  [the longest x1 2.79 us: body(): pl.pallas_call(lambda *refs: pack_kernel(count, *refs), out_shape=jax.Sha...]
  transfers between devices with their start and end apart: 6 -> 7, of which waited for: 6 -> 7; matrix products, arithmetic and copies ran while one was open for 2% -> 8% of each run, Pallas kernels for 0% -> 0%
where the time goes in v1:
time: 293 us; the launch traced here: 288 us
  blocking collectives  109 us (37%)
  waiting for transfers between devices  83.1 us (28%)
  starting transfers between devices  24.3 us (8%)
  local copies, waits for them, and re-layouts  23.6 us (8%)
  matrix products  20.3 us (7%)
  between operations  13.6 us (5%)
  other arithmetic  7.27 us (2%)
  Pallas kernels  6.74 us (2%)
    all_to_all x4, blocking collectives, exchange(): return lax.all_to_all(value, axes, split_axis=0, concat_axis=0, tiled=True)  109 us
    all_to_all x4, waiting for transfers between devices, exchange(): return lax.all_to_all(value, axes, split_axis=0, concat_axis=0, tiled=True)  49.7 us
    all_gather x1, waiting for transfers between devices, body(): lax.all_gather(boundary.reshape(across, part, width), PIV, axis=1, tiled=...  23.2 us
    all_to_all x4, starting transfers between devices, exchange(): return lax.all_to_all(value, axes, split_axis=0, concat_axis=0, tiled=True)  18.7 us
    dot_general x4, matrix products, body(): jnp.dot(reduced, inverse[group], precision=lax.Precision.HIGH, preferred_...  9.22 us
    dot_general x1, matrix products, body(): jnp.dot(full.reshape(total, width), lower_panel, precision=lax.Precision....  7.89 us
    all_gather x1, waiting for transfers between devices, body(): column = lax.all_gather(ancestor_sol, 'z', axis=0, tiled=False)  7.25 us
    broadcast_in_dim x4, local copies, waits for them, and re-layouts, spread(): return exchange(jnp.broadcast_to(value[None], (count, *value.shape)), axis)  6.34 us
  transfers between devices with their start and end apart: 7, of which 7 were waited for; matrix products, arithmetic and copies ran while one was open for 8% of the time, Pallas kernels for 0%

profile of v1, /device:TPU:1, one launch (start us, length us, event | category | flops | bytes accessed | tf_op | source)
XLA Modules:
  0.0 287.8 jit_solution(2328881857524270252)
XLA Ops:
  8.7 4.8 %all-to-all-start.1 = ((s32[4,1,8]{2,1,0:T(1,128)}), s32[4,1,8]{2,1,0:T(1,128)S(1)}, u32[]{:S(2)}, u32[]{:S(2)}) async-start(s32[4,1,8]{2,1,0:T(1,128)} %broadcast_in_dim.9), calls=%async_computation.1 | async-start | bytes 4096 | tf_op jit(solution)/shard_map/all_to_all | solution.py:17
  13.5 2.4 fusion.1
  17.6 2.7 broadcast_in_dim.8
  20.3 4.5 %all-to-all-start = ((f32[4,384,384]{2,1,0:T(8,128)}), f32[4,384,384]{2,1,0:T(8,128)}, u32[]{:S(2)}, u32[]{:S(2)}) async-start(f32[4,384,384]{2,1,0:T(8,128)} %broadcast_in_dim.8), calls=%async_computation | async-start | bytes 4718592 | tf_op jit(solution)/shard_map/all_to_all | solution.py:17
  30.1 3.2 %convolution_bitcast_fusion = f32[1024,768]{0,1:T(8,128)} fusion(f32[1024,24]{0,1:T(8,128)S(1)} %reshape.71, s32[24]{0:T(128)S(1)} %iota_add_fusion), kind=kOutput, calls=%fused_computation.1 | convolution fusion | flops 226510848 | bytes 3244128 | tf_op jit(solution)/shard_map/dot_general | solution.py:83
  33.3 14.2 %all-to-all-done = f32[4,384,384]{2,1,0:T(8,128)} async-done(((f32[4,384,384]{2,1,0:T(8,128)}), f32[4,384,384]{2,1,0:T(8,128)}, u32[]{:S(2)}, u32[]{:S(2)}) %all-to-all-start) | async-done | bytes 2359328 | tf_op jit(solution)/shard_map/all_to_all | solution.py:17
  47.5 7.2 %all-gather.6.cloned.1.call-done = f32[512,1024]{1,0:T(8,128)} async-done(((f32[64,1024]{1,0:T(8,128)}), f32[512,1024]{1,0:T(8,128)}) %all-gather.6.cloned.1.call-update) | async-done | bytes 2097168 | tf_op jit(solution)/shard_map/all_gather | solution.py:74
  54.7 2.8 pack.1
  57.5 14.1 %all_to_all.44.refs_1_ = f32[4,64,1024]{2,1,0:T(8,128)} all-to-all(f32[4,64,1024]{2,1,0:T(8,128)} %pack.1), channel_id=1, replica_groups=mesh['z'=8,'x'=4,'y'=8,'c'=2] {'x'}, dimensions={0} | all-to-all | bytes 2097152 | tf_op jit(solution)/shard_map/all_to_all | solution.py:17
  74.8 25.9 %all_to_all.45 = f32[4,384,384]{2,1,0:T(8,128)} all-to-all(f32[4,384,384]{2,1,0:T(8,128)S(1)} %broadcast_in_dim.10), channel_id=1, replica_groups=mesh['z'=8,'x'=4,'y'=8,'c'=2] {'x'}, dimensions={0} | all-to-all | bytes 4718592 | tf_op jit(solution)/shard_map/all_to_all | solution.py:17
  100.7 23.2 %all-gather.4.cloned.1.call-done = f32[4,256,1024]{2,1,0:T(8,128)} async-done(((f32[4,16,1024]{2,1,0:T(8,128)}), f32[4,256,1024]{2,1,0:T(8,128)}) %all-gather.4.cloned.1.call-update) | async-done | bytes 4194320 | tf_op jit(solution)/shard_map/all_gather | solution.py:107
  124.0 7.9 %convolution_subtract_fusion = f32[1024,768]{0,1:T(8,128)S(1)} fusion(f32[1024,768]{0,1:T(8,128)} %convolution_bitcast_fusion, f32[1024,1024]{1,0:T(8,128)} %bitcast.70, f32[1024,768]{1,0:T(8,128)S(1)} %copy-done), kind=kOutput, calls=%fused_computation.2 | convolution fusion | flops 4832624640 | bytes 13631488 | tf_op jit(solution)/shard_map/dot_general | solution.py:109
  132.1 41.0 %all_to_all.46 = f32[4,256,768]{1,2,0:T(8,128)} all-to-all(f32[4,256,768]{1,2,0:T(8,128)S(1)} %bitcast.68), channel_id=1, replica_groups=mesh['z'=8,'x'=4,'y'=8,'c'=2] {'x'}, dimensions={0} | all-to-all | bytes 6291456 | tf_op jit(solution)/shard_map/all_to_all | solution.py:17
  173.1 3.1 %reduce_sum.18 = f32[256,768]{0,1:T(8,128)} reduce(f32[4,256,768]{1,2,0:T(8,128)} %all_to_all.46, f32[]{:T(128)} %constant.30.clone.1), dimensions={0}, to_apply=%region_0.0 | reduce | flops 589824 | bytes 3932164 | tf_op jit(solution)/shard_map/reduce_sum | solution.py:115
  178.5 28.0 %all_to_all.47 = f32[8,32,768]{2,1,0:T(8,128)} all-to-all(f32[8,32,768]{2,1,0:T(8,128)} %bitcast.72), channel_id=1, replica_groups=mesh['z'=8,'x'=4,'y'=8,'c'=2] {'z'}, dimensions={0} | all-to-all | bytes 1572864 | tf_op jit(solution)/shard_map/all_to_all | solution.py:17
  208.6 4.2 %all-to-all-start.6 = ((f32[8,32,768]{2,1,0:T(8,128)}), f32[8,32,768]{2,1,0:T(8,128)}, u32[]{:S(2)}, u32[]{:S(2)}) async-start(f32[8,32,768]{2,1,0:T(8,128)} %broadcast_in_dim.11), calls=%async_computation.6 | async-start | bytes 1572864 | tf_op jit(solution)/shard_map/all_to_all | solution.py:17
  212.8 3.4 %constant_dynamic-update-slice_fusion.1 = f32[4,768,384]{2,1,0:T(8,128)} fusion(f32[4,384,384]{2,1,0:T(8,128)} %all-to-all-done), kind=kLoop, calls=%fused_computation.17 | loop fusion | bytes 4718592
  217.8 15.5 %all-to-all-done.6 = f32[8,32,768]{2,1,0:T(8,128)} async-done(((f32[8,32,768]{2,1,0:T(8,128)}), f32[8,32,768]{2,1,0:T(8,128)}, u32[]{:S(2)}, u32[]{:S(2)}) %all-to-all-start.6) | async-done | bytes 786464 | tf_op jit(solution)/shard_map/all_to_all | solution.py:17
  235.6 2.3 convolution_bitcast_fusion.2
  238.0 2.3 convolution_bitcast_fusion.3
  244.8 5.5 %collective-permute-start = (f32[4,8,16,384]{3,2,1,0:T(8,128)}, f32[4,8,16,384]{3,2,1,0:T(8,128)}, u32[]{:S(2)}, u32[]{:S(2)}) collective-permute-start(f32[4,8,16,384]{3,2,1,0:T(8,128)} %dynamic-slice_bitcast_fusion), channel_id=1, source_target_pairs={{0,1},{1,0},{2,3},{3,2},{4,5},{5,4},{6,7},{7,6},{8,9},{9,8},{10,11... | collective-permute-start | bytes 2359304 | tf_op jit(solution)/shard_map/ppermute | solution.py:136
  252.6 2.4 bitcast_add_fusion
  254.9 5.2 %all-to-all-start.7 = ((f32[32,16,384]{2,1,0:T(8,128)}), f32[32,16,384]{2,1,0:T(8,128)}, u32[]{:S(2)}, u32[]{:S(2)}) async-start(f32[32,16,384]{2,1,0:T(8,128)} %bitcast.71), calls=%async_computation.7 | async-start | bytes 1572864 | tf_op jit(solution)/shard_map/all_to_all | solution.py:17
  260.7 18.3 %all-to-all-done.7 = f32[32,16,384]{2,1,0:T(8,128)} async-done(((f32[32,16,384]{2,1,0:T(8,128)}), f32[32,16,384]{2,1,0:T(8,128)}, u32[]{:S(2)}, u32[]{:S(2)}) %all-to-all-start.7) | async-done | bytes 786464 | tf_op jit(solution)/shard_map/all_to_all | solution.py:17
  (36 shorter events, 30.1 us)
Async XLA Ops:
  6.5 117.4 %copy-start = (f32[1024,768]{1,0:T(8,128)S(1)}, f32[1024,768]{1,0:T(8,128)}, u32[]{:S(2)}) copy-start(f32[1024,768]{1,0:T(8,128)} %param.9) | copy-start | bytes 9437188
  6.5 48.2 %all-gather.6.cloned.1.call-start = ((), (), s32[]{:S(2)}) async-start(), calls=%async_computation.9 | async-start | bytes 2359296 | tf_op jit(solution)/shard_map/all_gather | solution.py:74
  8.7 8.9 %all-to-all-start.1 = ((s32[4,1,8]{2,1,0:T(1,128)}), s32[4,1,8]{2,1,0:T(1,128)S(1)}, u32[]{:S(2)}, u32[]{:S(2)}) async-start(s32[4,1,8]{2,1,0:T(1,128)} %broadcast_in_dim.9), calls=%async_computation.1 | async-start | bytes 4096 | tf_op jit(solution)/shard_map/all_to_all | solution.py:17
  17.6 2.7 copy-start.4
  17.6 7.3 %copy-start.3 = (f32[1024,24]{0,1:T(8,128)S(1)}, f32[1024,24]{0,1:T(8,128)}, u32[]{:S(2)}) copy-start(f32[1024,24]{0,1:T(8,128)} %param.11) | copy-start | bytes 294916
  20.3 27.2 %all-to-all-start = ((f32[4,384,384]{2,1,0:T(8,128)}), f32[4,384,384]{2,1,0:T(8,128)}, u32[]{:S(2)}, u32[]{:S(2)}) async-start(f32[4,384,384]{2,1,0:T(8,128)} %broadcast_in_dim.8), calls=%async_computation | async-start | bytes 4718592 | tf_op jit(solution)/shard_map/all_to_all | solution.py:17
  24.8 99.1 %all-gather.4.cloned.1.call-start = ((), (), s32[]{:S(2)}) async-start(), calls=%async_computation.8 | async-start | bytes 4456448 | tf_op jit(solution)/shard_map/all_gather | solution.py:107
  208.6 24.7 %all-to-all-start.6 = ((f32[8,32,768]{2,1,0:T(8,128)}), f32[8,32,768]{2,1,0:T(8,128)}, u32[]{:S(2)}, u32[]{:S(2)}) async-start(f32[8,32,768]{2,1,0:T(8,128)} %broadcast_in_dim.11), calls=%async_computation.6 | async-start | bytes 1572864 | tf_op jit(solution)/shard_map/all_to_all | solution.py:17
  212.8 3.4 %copy-start.1 = (f32[4,384,384]{2,1,0:T(8,128)S(1)}, f32[4,384,384]{2,1,0:T(8,128)}, u32[]{:S(2)}) copy-start(f32[4,384,384]{2,1,0:T(8,128)} %all_to_all.45) | copy-start | bytes 7077892
  242.7 1.2 copy-start.2
  243.9 16.3 %copy-start.5 = (s32[4]{0:T(128)S(1)}, s32[4]{0:T(128)}, u32[]{:S(2)}) copy-start(s32[4]{0:T(128)} %param.12) | copy-start | bytes 52
  244.8 7.7 %collective-permute-start = (f32[4,8,16,384]{3,2,1,0:T(8,128)}, f32[4,8,16,384]{3,2,1,0:T(8,128)}, u32[]{:S(2)}, u32[]{:S(2)}) collective-permute-start(f32[4,8,16,384]{3,2,1,0:T(8,128)} %dynamic-slice_bitcast_fusion), channel_id=1, source_target_pairs={{0,1},{1,0},{2,3},{3,2},{4,5},{5,4},{6,7},{7,6},{8,9},{9,8},{10,11... | collective-permute-start | bytes 2359304 | tf_op jit(solution)/shard_map/ppermute | solution.py:136
  254.9 24.0 %all-to-all-start.7 = ((f32[32,16,384]{2,1,0:T(8,128)}), f32[32,16,384]{2,1,0:T(8,128)}, u32[]{:S(2)}, u32[]{:S(2)}) async-start(f32[32,16,384]{2,1,0:T(8,128)} %bitcast.71), calls=%async_computation.7 | async-start | bytes 1572864 | tf_op jit(solution)/shard_map/all_to_all | solution.py:17
Sparse Core Ops, SparseCore 0:
  9.4 45.2 all-gather.5
  73.7 50.2 all-gather.3

commit v2 on v1

--- a/solution.py
+++ b/solution.py
@@ -38,6 +38,54 @@
         origin = lax.rem(lax.div(own[slot], count), across)
         cols = slice(slot * BLK, (slot + 1) * BLK)
         boundary[:, cols] = arrived[origin, :, cols]
+
+
+def split(value):
+    high = value.astype(jnp.bfloat16)
+    return high, (value - high.astype(jnp.float32)).astype(jnp.bfloat16)
+
+
+def product(left, right):
+    terms = ((0, 0), (0, 1), (1, 0))
+    return sum(jnp.dot(left[i], right[j], preferred_element_type=jnp.float32) for i, j in terms)
+
+
+def couple_kernel(full, panel, placed, share_a, share_b, high, low):
+    @pl.when(pl.program_id(0) == 0)
+    def _():
+        high[...], low[...] = split(panel[...])
+
+    _, devs, part, width = full.shape
+    short = part // 2
+    pivots = panel.shape[1]
+    left = split(full[0].reshape(devs * part, width))
+    result = placed[0].reshape(devs * part, pivots) - product(left, (high[...], low[...]))
+    result = result.reshape(devs, 2, short, pivots)
+    share_a[0] = result[:, 0].reshape(share_a.shape[1:])
+    share_b[:, 0] = result[:, 1].reshape(share_b.shape[0], *share_b.shape[2:])
+
+
+def join_kernel(pieces_a, pieces_b, copies):
+    joined = (jnp.sum(pieces_a[...], axis=0), jnp.sum(pieces_b[...], axis=0))
+    for level in range(copies.shape[0]):
+        for side in range(2):
+            copies[level, side] = joined[side]
+
+
+def solve_kernel(core, reduced, inverse_lo, inverse_hi, kept, other, high, low):
+    @pl.when(pl.program_id(0) == 0)
+    def _():
+        high[...], low[...] = split(reduced[...])
+
+    _, tall, halves, short, span = kept.shape
+    half = inverse_lo.shape[1]
+    result = product((high[:, :half], low[:, :half]), split(inverse_lo[0]))
+    result = result + product((high[:, half:], low[:, half:]), split(inverse_hi[0]))
+    result = result.reshape(tall, halves, 2, short, span)
+    first, second = result[:, :, 0], result[:, :, 1]
+    mine = core[0] == 0
+    kept[0] = jnp.where(mine, first, second)
+    other[0] = jnp.where(mine, second, first)
 
 
 def child_kernel(first, length, pieces, children, summed):
@@ -74,6 +122,26 @@
     column = lax.all_gather(ancestor_sol, "z", axis=0, tiled=False)
     half = pivots // 2
     inverse_lo = spread(inverse_factor[:half], "x")
+    column, inverse_lo, maps = lax.optimization_barrier((column, inverse_lo, maps))
+    sends = pl.pallas_call(
+        lambda *refs: pack_kernel(count, *refs),
+        out_shape=jax.ShapeDtypeStruct((across, srcs, width), jnp.float32),
+        in_specs=[SMEM, VMEM],
+        out_specs=VMEM,
+        name="pack",
+    )(maps, column)
+    arrived = exchange(sends, "x")
+    boundary = pl.pallas_call(
+        lambda *refs: pick_kernel(count, *refs),
+        out_shape=jax.ShapeDtypeStruct((srcs, width), jnp.float32),
+        in_specs=[SMEM, VMEM],
+        out_specs=VMEM,
+        name="pick",
+    )(front_map, arrived)
+    boundary, upper, right_side = lax.optimization_barrier(
+        (boundary, inverse_factor[half:], right_side)
+    )
+    inverse_hi = spread(upper, "x")
     own_share = right_side.shape[1]
     place = (
         jnp.arange(pivots, dtype=jnp.int32)[None, :]
@@ -85,54 +153,71 @@
         place,
         precision=lax.Precision.HIGHEST,
         preferred_element_type=jnp.float32,
+    ).reshape(across, piv_devs, part, pivots)
+    full = lax.all_gather(boundary.reshape(across, part, width), PIV, axis=1, tiled=True)
+    full, inverse_hi, placed = lax.optimization_barrier((full, inverse_hi, placed))
+    short = part // 2
+    rows = piv_devs * short
+    chip = cores * short
+    share_a, share_b = pl.pallas_call(
+        couple_kernel,
+        grid=(across,),
+        out_shape=(
+            jax.ShapeDtypeStruct((across, rows, pivots), jnp.float32),
+            jax.ShapeDtypeStruct((tall, across, chip, pivots), jnp.float32),
+        ),
+        in_specs=[
+            pl.BlockSpec((1, piv_devs, part, width), lambda i: (i, 0, 0, 0)),
+            pl.BlockSpec((width, pivots), lambda i: (0, 0)),
+            pl.BlockSpec((1, piv_devs, part, pivots), lambda i: (i, 0, 0, 0)),
+        ],
+        out_specs=(
+            pl.BlockSpec((1, rows, pivots), lambda i: (i, 0, 0)),
+            pl.BlockSpec((tall, 1, chip, pivots), lambda i: (0, i, 0, 0)),
+        ),
+        scratch_shapes=[
+            pltpu.VMEM((width, pivots), jnp.bfloat16),
+            pltpu.VMEM((width, pivots), jnp.bfloat16),
+        ],
+        compiler_params=pltpu.CompilerParams(vmem_limit_bytes=48 * 1024 * 1024),
+        name="couple",
+    )(full.reshape(across, piv_devs, part, width), lower_panel, placed)
+    nearer_b = lax.psum_scatter(share_b, "z", scatter_dimension=0, tiled=True)
+    nearer_a = exchange(share_a, "x").sum(axis=0)
+    nearer_a = exchange(nearer_a.reshape(deep, chip, pivots), "z")
+    nearer_a, nearer_b = lax.optimization_barrier((nearer_a, nearer_b))
+    nearer_b = exchange(nearer_b.reshape(across, chip, pivots), "x")
+    copies = pl.pallas_call(
+        join_kernel,
+        out_shape=jax.ShapeDtypeStruct((deep, 2, chip, pivots), jnp.float32),
+        in_specs=[VMEM, VMEM],
+        out_specs=VMEM,
+        name="join",
+    )(nearer_a, nearer_b)
+    reduced = exchange(copies, "z").reshape(quarter, pivots)
+    core = lax.axis_index("c")
+    kept, other = pl.pallas_call(
+        solve_kernel,
+        grid=(across,),
+        out_shape=(jax.ShapeDtypeStruct((across, tall, 2, short, span), jnp.float32),) * 2,
+        in_specs=[
+            SMEM,
+            pl.BlockSpec((quarter, pivots), lambda i: (0, 0)),
+            pl.BlockSpec((1, half, span), lambda i: (i, 0, 0)),
+            pl.BlockSpec((1, half, span), lambda i: (i, 0, 0)),
+        ],
+        out_specs=(pl.BlockSpec((1, tall, 2, short, span), lambda i: (i, 0, 0, 0, 0)),) * 2,
+        scratch_shapes=[
+            pltpu.VMEM((quarter, pivots), jnp.bfloat16),
+            pltpu.VMEM((quarter, pivots), jnp.bfloat16),
+        ],
+        name="solve",
+    )(
+        core.reshape(1),
+        reduced,
+        inverse_lo.reshape(across, half, span),
+        inverse_hi.reshape(across, half, span),
     )
-    column, inverse_lo, maps, placed = lax.optimization_barrier((column, inverse_lo, maps, placed))
-    sends = pl.pallas_call(
-        lambda *refs: pack_kernel(count, *refs),
-        out_shape=jax.ShapeDtypeStruct((across, srcs, width), jnp.float32),
-        in_specs=[SMEM, VMEM],
-        out_specs=VMEM,
-        name="pack",
-    )(maps, column)
-    arrived = exchange(sends, "x")
-    boundary = pl.pallas_call(
-        lambda *refs: pick_kernel(count, *refs),
-        out_shape=jax.ShapeDtypeStruct((srcs, width), jnp.float32),
-        in_specs=[SMEM, VMEM],
-        out_specs=VMEM,
-        name="pick",
-    )(front_map, arrived)
-    boundary, upper = lax.optimization_barrier((boundary, inverse_factor[half:]))
-    inverse_hi = spread(upper, "x")
-    full = lax.all_gather(boundary.reshape(across, part, width), PIV, axis=1, tiled=True)
-    full, inverse_hi = lax.optimization_barrier((full, inverse_hi))
-    share = placed - jnp.dot(
-        full.reshape(total, width),
-        lower_panel,
-        precision=lax.Precision.HIGH,
-        preferred_element_type=jnp.float32,
-    )
-    reduced = exchange(share.reshape(across, quarter, pivots), "x").sum(axis=0)
-    reduced = exchange(reduced.reshape(deep, quarter // deep, pivots), "z").sum(axis=0)
-    reduced = spread(reduced, "z").reshape(quarter, pivots)
-    inverse = jnp.concatenate(
-        [inverse_lo.reshape(across, half, span), inverse_hi.reshape(across, half, span)], axis=1
-    )
-    partial = jnp.stack(
-        [
-            jnp.dot(
-                reduced,
-                inverse[group],
-                precision=lax.Precision.HIGH,
-                preferred_element_type=jnp.float32,
-            )
-            for group in range(across)
-        ]
-    )
-    partial = partial.reshape(across, tall, cores, part, span)
-    core = lax.axis_index("c")
-    kept = lax.dynamic_index_in_dim(partial, core, 2, keepdims=False)
-    other = lax.dynamic_index_in_dim(partial, 1 - core, 2, keepdims=False)
     kept = kept + lax.ppermute(other, "c", [(0, 1), (1, 0)])
     pieces = exchange(kept.reshape(across * tall, part, span), ("x", "y"))
     return pl.pallas_call(

time: 293 us -> 270 us (0.922)
  Pallas kernels: 6.74 us -> 24.8 us
  local copies, waits for them, and re-layouts: 23.6 us -> 6.6 us
  matrix products: 20.3 us -> 3.47 us
  blocking collectives: 109 us -> 96.1 us
  waiting for transfers between devices: 83.1 us -> 91.3 us
  other arithmetic: 7.27 us -> 2.77 us
    pallas_call x0 -> x3, Pallas kernels: none -> 18.1 us  [the longest x1 9.6 us: body(): pl.pallas_call(couple_kernel, grid=(across,), out_shape=(jax.ShapeDtypeSt...]
    dot_general x5 -> x0, matrix products: 17.1 us -> none  [the longest x4 9.22 us: body(): jnp.dot(reduced, inverse[group], precision=lax.Precision.HIGH, preferred_...]
    all_to_all x4 -> x5, blocking collectives: 109 us -> 96.1 us  [exchange(): return lax.all_to_all(value, axes, split_axis=0, concat_axis=0, tiled=True)]
    all_to_all x4, waiting for transfers between devices: 49.7 us -> 57.7 us  [exchange(): return lax.all_to_all(value, axes, split_axis=0, concat_axis=0, tiled=True)]
    reduce_sum x2 -> x1, other arithmetic: 4.27 us -> 0.11 us  [body(): nearer_a = exchange(share_a, 'x').sum(axis=0)]
    all_gather x1, waiting for transfers between devices: 7.25 us -> 11.3 us  [body(): column = lax.all_gather(ancestor_sol, 'z', axis=0, tiled=False)]
    all_gather x1, waiting for transfers between devices: 23.2 us -> 19.5 us  [body(): lax.all_gather(boundary.reshape(across, part, width), PIV, axis=1, tiled=...]
    broadcast_in_dim x4 -> x3, local copies, waits for them, and re-layouts: 6.34 us -> 2.91 us  [spread(): return exchange(jnp.broadcast_to(value[None], (count, *value.shape)), axis)]
  transfers between devices with their start and end apart: 7 -> 8, of which waited for: 7 -> 7; matrix products, arithmetic and copies ran while one was open for 8% -> 3% of each run, Pallas kernels for 0% -> 0%
where the time goes in v2:
time: 270 us; the launch traced here: 265 us
  blocking collectives  96.1 us (36%)
  waiting for transfers between devices  91.3 us (34%)
  starting transfers between devices  27.1 us (10%)
  Pallas kernels  24.8 us (9%)
  between operations  13.2 us (5%)
  local copies, waits for them, and re-layouts  6.6 us (2%)
  matrix products  3.47 us (1%)
  other arithmetic  2.77 us (1%)
    all_to_all x5, blocking collectives, exchange(): return lax.all_to_all(value, axes, split_axis=0, concat_axis=0, tiled=True)  96.1 us
    all_to_all x4, waiting for transfers between devices, exchange(): return lax.all_to_all(value, axes, split_axis=0, concat_axis=0, tiled=True)  57.7 us
    all_gather x1, waiting for transfers between devices, body(): lax.all_gather(boundary.reshape(across, part, width), PIV, axis=1, tiled=...  19.5 us
    all_to_all x4, starting transfers between devices, exchange(): return lax.all_to_all(value, axes, split_axis=0, concat_axis=0, tiled=True)  19.1 us
    all_gather x1, waiting for transfers between devices, body(): column = lax.all_gather(ancestor_sol, 'z', axis=0, tiled=False)  11.3 us
    pallas_call x1, Pallas kernels, body(): pl.pallas_call(couple_kernel, grid=(across,), out_shape=(jax.ShapeDtypeSt...  9.6 us
    ppermute x1, starting transfers between devices, body(): kept = kept + lax.ppermute(other, 'c', [(0, 1), (1, 0)])  7.95 us
    pallas_call x1, Pallas kernels, body(): pl.pallas_call(solve_kernel, grid=(across,), out_shape=(jax.ShapeDtypeStr...  6.54 us
  transfers between devices with their start and end apart: 8, of which 7 were waited for; matrix products, arithmetic and copies ran while one was open for 3% of the time, Pallas kernels for 0%

profile of v2, /device:TPU:1, one launch (start us, length us, event | category | flops | bytes accessed | tf_op | source)
XLA Modules:
  0.0 265.4 jit_solution(2717023037188025995)
XLA Ops:
  8.5 4.8 %all-to-all-start.1 = ((s32[4,1,8]{2,1,0:T(1,128)}), s32[4,1,8]{2,1,0:T(1,128)S(1)}, u32[]{:S(2)}, u32[]{:S(2)}) async-start(s32[4,1,8]{2,1,0:T(1,128)} %broadcast_in_dim.7), calls=%async_computation.1 | async-start | bytes 4096 | tf_op jit(solution)/shard_map/all_to_all | solution.py:17
  14.6 2.7 %all-to-all-done.1 = s32[4,1,8]{2,1,0:T(1,128)S(1)} async-done(((s32[4,1,8]{2,1,0:T(1,128)}), s32[4,1,8]{2,1,0:T(1,128)S(1)}, u32[]{:S(2)}, u32[]{:S(2)}) %all-to-all-start.1) | async-done | bytes 160 | tf_op jit(solution)/shard_map/all_to_all | solution.py:17
  17.5 25.8 %all_to_all.49.inverse_lo = f32[4,384,384]{2,1,0:T(8,128)} all-to-all(f32[4,384,384]{2,1,0:T(8,128)S(1)} %broadcast_in_dim.6), channel_id=1, replica_groups=mesh['z'=8,'x'=4,'y'=8,'c'=2] {'x'}, dimensions={0} | all-to-all | bytes 4718592 | tf_op jit(solution)/shard_map/all_to_all | solution.py:17
  43.4 11.3 %all-gather.6.cloned.1.call-done = f32[512,1024]{1,0:T(8,128)} async-done(((f32[64,1024]{1,0:T(8,128)}), f32[512,1024]{1,0:T(8,128)}) %all-gather.6.cloned.1.call-update) | async-done | bytes 2097168 | tf_op jit(solution)/shard_map/all_gather | solution.py:122
  54.7 2.7 %pack.1 = f32[4,64,1024]{2,1,0:T(8,128)} custom-call(s32[4,8]{1,0:T(4,128)} %bitcast.26, f32[8,64,1024]{2,1,0:T(8,128)} %bitcast.22), custom_call_target="tpu_custom_call" | custom-call | tf_op jit(solution)/shard_map/pack/pallas_call | solution.py:126
  57.4 14.1 %all_to_all.50.refs_1_ = f32[4,64,1024]{2,1,0:T(8,128)} all-to-all(f32[4,64,1024]{2,1,0:T(8,128)} %pack.1), channel_id=1, replica_groups=mesh['z'=8,'x'=4,'y'=8,'c'=2] {'x'}, dimensions={0} | all-to-all | bytes 2097152 | tf_op jit(solution)/shard_map/all_to_all | solution.py:17
  75.1 3.8 %all-to-all-start.3 = ((f32[4,384,384]{2,1,0:T(8,128)}), f32[4,384,384]{2,1,0:T(8,128)S(1)}, u32[]{:S(2)}, u32[]{:S(2)}) async-start(f32[4,384,384]{2,1,0:T(8,128)} %broadcast_in_dim.8), calls=%async_computation.3 | async-start | bytes 4718592 | tf_op jit(solution)/shard_map/all_to_all | solution.py:17
  79.5 3.5 %fusion.placed = f32[4,16,16,768]{3,2,1,0:T(8,128)} fusion(f32[4,16,16,24]{2,0,1,3:T(4,128)S(1)} %bitcast.20, s32[24]{0:T(128)S(1)} %iota_add_fusion), kind=kOutput, calls=%fused_computation | convolution fusion | flops 226510848 | bytes 3244128 | tf_op jit(solution)/shard_map/dot_general | solution.py:151
  83.0 18.6 %all-to-all-done.3.inverse_hi = f32[4,384,384]{2,1,0:T(8,128)S(1)} async-done(((f32[4,384,384]{2,1,0:T(8,128)}), f32[4,384,384]{2,1,0:T(8,128)S(1)}, u32[]{:S(2)}, u32[]{:S(2)}) %all-to-all-start.3) | async-done | bytes 2359328 | tf_op jit(solution)/shard_map/all_to_all | solution.py:17
  101.5 19.5 %all-gather.4.cloned.1.call-done = f32[4,256,1024]{2,1,0:T(8,128)} async-done(((f32[4,16,1024]{2,1,0:T(8,128)}), f32[4,256,1024]{2,1,0:T(8,128)}) %all-gather.4.cloned.1.call-update) | async-done | bytes 4194320 | tf_op jit(solution)/shard_map/all_gather | solution.py:157
  121.0 9.6 %couple.1 = (f32[4,128,768]{2,1,0:T(8,128)S(1)}, f32[8,4,16,768]{3,2,1,0:T(8,128)}) custom-call(f32[4,16,16,1024]{3,2,1,0:T(8,128)} %bitcast.18, f32[1024,768]{1,0:T(8,128)} %panel.1, f32[4,16,16,768]{3,2,1,0:T(8,128)} %fusion.placed), custom_call_target="tpu_custom_call" | custom-call | tf_op jit(solution)/shard_map/couple/pallas_call | solution.py:162
  130.7 24.0 %all_to_all.51 = f32[4,128,768]{2,1,0:T(8,128)S(1)} all-to-all(f32[4,128,768]{2,1,0:T(8,128)S(1)} %get-tuple-element.27), channel_id=1, replica_groups=mesh['z'=8,'x'=4,'y'=8,'c'=2] {'x'}, dimensions={0} | all-to-all | bytes 3145728 | tf_op jit(solution)/shard_map/all_to_all | solution.py:17
  154.8 22.9 %all_to_all.52.pieces_a = f32[8,16,768]{2,1,0:T(8,128)} all-to-all(f32[8,16,768]{2,1,0:T(8,128)S(1)} %bitcast.23), channel_id=1, replica_groups=mesh['z'=8,'x'=4,'y'=8,'c'=2] {'z'}, dimensions={0} | all-to-all | bytes 786432 | tf_op jit(solution)/shard_map/all_to_all | solution.py:17
  177.7 9.2 %all_to_all.53.pieces_b = f32[4,16,768]{2,1,0:T(8,128)} all-to-all(f32[4,16,768]{2,1,0:T(8,128)} %bitcast.25), channel_id=1, replica_groups=mesh['z'=8,'x'=4,'y'=8,'c'=2] {'x'}, dimensions={0} | all-to-all | bytes 393216 | tf_op jit(solution)/shard_map/all_to_all | solution.py:17
  186.9 2.0 join.1
  188.9 3.5 %all-to-all-start.7 = ((f32[8,2,16,768]{3,2,1,0:T(8,128)}), f32[8,2,16,768]{3,2,1,0:T(8,128)S(1)}, u32[]{:S(2)}, u32[]{:S(2)}) async-start(f32[8,2,16,768]{3,2,1,0:T(8,128)} %join.1), calls=%async_computation.8 | async-start | bytes 1572864 | tf_op jit(solution)/shard_map/all_to_all | solution.py:17
  192.5 18.1 %all-to-all-done.7 = f32[8,2,16,768]{3,2,1,0:T(8,128)S(1)} async-done(((f32[8,2,16,768]{3,2,1,0:T(8,128)}), f32[8,2,16,768]{3,2,1,0:T(8,128)S(1)}, u32[]{:S(2)}, u32[]{:S(2)}) %all-to-all-start.7) | async-done | bytes 786464 | tf_op jit(solution)/shard_map/all_to_all | solution.py:17
  211.5 6.5 %solve.1 = (f32[4,8,2,8,384]{4,3,2,1,0:T(8,128)}, f32[4,8,2,8,384]{4,3,2,1,0:T(8,128)}) custom-call(s32[1]{0:T(128)} %bitcast.core, f32[256,768]{1,0:T(8,128)} %bitcast.21, f32[4,384,384]{2,1,0:T(8,128)} %all_to_all.49.inverse_lo, f32[4,384,384]{2,1,0:T(8,128)} %copy-done), custom_call_target="tpu_custom_call" | custom-call | tf_op jit(solution)/shard_map/solve/pallas_call | solution.py:199
  218.0 8.0 %collective-permute-start = (f32[4,8,2,8,384]{4,3,2,1,0:T(8,128)}, f32[4,8,2,8,384]{4,3,2,1,0:T(8,128)S(1)}, u32[]{:S(2)}, u32[]{:S(2)}) collective-permute-start(f32[4,8,2,8,384]{4,3,2,1,0:T(8,128)} %get-tuple-element.34), channel_id=1, source_target_pairs={{0,1},{1,0},{2,3},{3,2},{4,5},{5,4},{6,7},{7,6},{8,9},{9,8},{10,11... | collective-permute-start | bytes 2359304 | tf_op jit(solution)/shard_map/ppermute | solution.py:221
  226.0 2.1 collective-permute-done
  228.1 2.1 add.22
  230.3 6.9 %all-to-all-start.8 = ((f32[32,16,384]{2,1,0:T(8,128)}), f32[32,16,384]{2,1,0:T(8,128)S(1)}, u32[]{:S(2)}, u32[]{:S(2)}) async-start(f32[32,16,384]{2,1,0:T(8,128)} %bitcast.11), calls=%async_computation.9 | async-start | bytes 1572864 | tf_op jit(solution)/shard_map/all_to_all | solution.py:17
  237.7 18.3 %all-to-all-done.8 = f32[32,16,384]{2,1,0:T(8,128)S(1)} async-done(((f32[32,16,384]{2,1,0:T(8,128)}), f32[32,16,384]{2,1,0:T(8,128)S(1)}, u32[]{:S(2)}, u32[]{:S(2)}) %all-to-all-start.8) | async-done | bytes 786464 | tf_op jit(solution)/shard_map/all_to_all | solution.py:17
  256.9 2.0 children.1
  (28 shorter events, 10.0 us)
Async XLA Ops:
  6.5 48.2 %all-gather.6.cloned.1.call-start = ((), (), s32[]{:S(2)}) async-start(), calls=%async_computation.12 | async-start | bytes 2359296 | tf_op jit(solution)/shard_map/all_gather | solution.py:122
  8.5 8.9 %all-to-all-start.1 = ((s32[4,1,8]{2,1,0:T(1,128)}), s32[4,1,8]{2,1,0:T(1,128)S(1)}, u32[]{:S(2)}, u32[]{:S(2)}) async-start(s32[4,1,8]{2,1,0:T(1,128)} %broadcast_in_dim.7), calls=%async_computation.1 | async-start | bytes 4096 | tf_op jit(solution)/shard_map/all_to_all | solution.py:17
  13.3 107.7 %all-gather.4.cloned.1.call-start = ((), (), s32[]{:S(2)}) async-start(), calls=%async_computation.10 | async-start | bytes 4456448 | tf_op jit(solution)/shard_map/all_gather | solution.py:157
  17.4 26.0 %copy-start.4 = (s32[4,1,8]{2,1,0:T(1,128)}, s32[4,1,8]{2,1,0:T(1,128)S(1)}, u32[]{:S(2)}) copy-start(s32[4,1,8]{2,1,0:T(1,128)S(1)} %all-to-all-done.1) | copy-start | bytes 388
  75.1 3.8 %copy-start.3 = (f32[1024,24]{0,1:T(8,128)S(1)}, f32[1024,24]{0,1:T(8,128)}, u32[]{:S(2)}) copy-start(f32[1024,24]{0,1:T(8,128)} %param.11) | copy-start | bytes 294916
  75.1 26.4 %all-to-all-start.3 = ((f32[4,384,384]{2,1,0:T(8,128)}), f32[4,384,384]{2,1,0:T(8,128)S(1)}, u32[]{:S(2)}, u32[]{:S(2)}) async-start(f32[4,384,384]{2,1,0:T(8,128)} %broadcast_in_dim.8), calls=%async_computation.3 | async-start | bytes 4718592 | tf_op jit(solution)/shard_map/all_to_all | solution.py:17
  78.9 98.9 %reduce-scatter.2.cloned.1.call-start = ((), (), s32[]{:S(2)}) async-start(), calls=%async_computation.11 | async-start | bytes 1769472 | tf_op jit(solution)/shard_map/reduce_scatter | solution.py:185
  101.5 19.5 %copy-start = (f32[4,384,384]{2,1,0:T(8,128)}, f32[4,384,384]{2,1,0:T(8,128)S(1)}, u32[]{:S(2)}) copy-start(f32[4,384,384]{2,1,0:T(8,128)S(1)} %all-to-all-done.3.inverse_hi) | copy-start | bytes 7077892
  188.9 21.7 %all-to-all-start.7 = ((f32[8,2,16,768]{3,2,1,0:T(8,128)}), f32[8,2,16,768]{3,2,1,0:T(8,128)S(1)}, u32[]{:S(2)}, u32[]{:S(2)}) async-start(f32[8,2,16,768]{3,2,1,0:T(8,128)} %join.1), calls=%async_computation.8 | async-start | bytes 1572864 | tf_op jit(solution)/shard_map/all_to_all | solution.py:17
  210.6 0.9 copy-start.2
  218.0 19.2 %copy-start.5 = (s32[4]{0:T(128)S(1)}, s32[4]{0:T(128)}, u32[]{:S(2)}) copy-start(s32[4]{0:T(128)} %param.12) | copy-start | bytes 52
  218.0 10.1 %collective-permute-start = (f32[4,8,2,8,384]{4,3,2,1,0:T(8,128)}, f32[4,8,2,8,384]{4,3,2,1,0:T(8,128)S(1)}, u32[]{:S(2)}, u32[]{:S(2)}) collective-permute-start(f32[4,8,2,8,384]{4,3,2,1,0:T(8,128)} %get-tuple-element.34), channel_id=1, source_target_pairs={{0,1},{1,0},{2,3},{3,2},{4,5},{5,4},{6,7},{7,6},{8,9},{9,8},{10,11... | collective-permute-start | bytes 2359304 | tf_op jit(solution)/shard_map/ppermute | solution.py:221
  230.3 25.8 %all-to-all-start.8 = ((f32[32,16,384]{2,1,0:T(8,128)}), f32[32,16,384]{2,1,0:T(8,128)S(1)}, u32[]{:S(2)}, u32[]{:S(2)}) async-start(f32[32,16,384]{2,1,0:T(8,128)} %bitcast.11), calls=%async_computation.9 | async-start | bytes 1572864 | tf_op jit(solution)/shard_map/all_to_all | solution.py:17
  256.0 0.9 copy-start.1
Sparse Core Ops, SparseCore 0:
  9.4 45.2 all-gather.5
  73.7 47.3 all-gather.3
  130.8 40.9 reduce-scatter.1

commit v3 on v2

--- a/solution.py
+++ b/solution.py
@@ -11,6 +11,10 @@
 PIV = ("y", "c")
 VMEM = pl.BlockSpec(memory_space=pltpu.VMEM)
 SMEM = pl.BlockSpec(memory_space=pltpu.SMEM)
+
+
+def grant(size):
+    return pltpu.CompilerParams(vmem_limit_bytes=size << 20)
 
 
 def exchange(value, axes):
@@ -50,39 +54,41 @@
     return sum(jnp.dot(left[i], right[j], preferred_element_type=jnp.float32) for i, j in terms)
 
 
-def couple_kernel(full, panel, placed, share_a, share_b, high, low):
-    @pl.when(pl.program_id(0) == 0)
-    def _():
-        high[...], low[...] = split(panel[...])
-
-    _, devs, part, width = full.shape
-    short = part // 2
-    pivots = panel.shape[1]
-    left = split(full[0].reshape(devs * part, width))
-    result = placed[0].reshape(devs * part, pivots) - product(left, (high[...], low[...]))
-    result = result.reshape(devs, 2, short, pivots)
-    share_a[0] = result[:, 0].reshape(share_a.shape[1:])
-    share_b[:, 0] = result[:, 1].reshape(share_b.shape[0], *share_b.shape[2:])
+def halve_kernel(value, high, low):
+    high[...], low[...] = split(value[...])
+
+
+def halve_inverse_kernel(inverse_lo, inverse_hi, high, low):
+    half = inverse_lo.shape[1]
+    high[:, :half], low[:, :half] = split(inverse_lo[...])
+    high[:, half:], low[:, half:] = split(inverse_hi[...])
+
+
+def couple_kernel(full, high, low, placed, share_a, share_b):
+    left = split(full[0])
+    result = placed[0] - product(left, (high[...], low[...]))
+    cut = share_a.shape[2]
+    share_a[0] = result[:, :cut]
+    share_b[:, 0] = result[:, cut:].reshape(share_b.shape[0], *share_b.shape[2:])
 
 
 def join_kernel(pieces_a, pieces_b, copies):
-    joined = (jnp.sum(pieces_a[...], axis=0), jnp.sum(pieces_b[...], axis=0))
+    first, second = jnp.sum(pieces_a[...], axis=0), jnp.sum(pieces_b[...], axis=0)
+    cut = first.shape[1]
     for level in range(copies.shape[0]):
-        for side in range(2):
-            copies[level, side] = joined[side]
-
-
-def solve_kernel(core, reduced, inverse_lo, inverse_hi, kept, other, high, low):
+        copies[level, :, :cut] = first
+        copies[level, :, cut:] = second
+
+
+def solve_kernel(core, reduced, inverse_high, inverse_low, kept, other, high, low):
     @pl.when(pl.program_id(0) == 0)
     def _():
         high[...], low[...] = split(reduced[...])
 
-    _, tall, halves, short, span = kept.shape
-    half = inverse_lo.shape[1]
-    result = product((high[:, :half], low[:, :half]), split(inverse_lo[0]))
-    result = result + product((high[:, half:], low[:, half:]), split(inverse_hi[0]))
-    result = result.reshape(tall, halves, 2, short, span)
-    first, second = result[:, :, 0], result[:, :, 1]
+    _, tall, part, span = kept.shape
+    result = product((high[...], low[...]), (inverse_high[0], inverse_low[0]))
+    result = result.reshape(tall, 2, part, span)
+    first, second = result[:, 0], result[:, 1]
     mine = core[0] == 0
     kept[0] = jnp.where(mine, first, second)
     other[0] = jnp.where(mine, second, first)
@@ -118,16 +124,30 @@
     quarter = total // across
     me = lax.axis_index(ROWS)
 
+    core = lax.axis_index("c").reshape(1)
+    first = child_start - me * span
     maps = spread(front_map, "x").reshape(across, count)
     column = lax.all_gather(ancestor_sol, "z", axis=0, tiled=False)
     half = pivots // 2
     inverse_lo = spread(inverse_factor[:half], "x")
-    column, inverse_lo, maps = lax.optimization_barrier((column, inverse_lo, maps))
+    panel_high, panel_low = pl.pallas_call(
+        halve_kernel,
+        grid=(4,),
+        out_shape=(jax.ShapeDtypeStruct((width, pivots), jnp.bfloat16),) * 2,
+        in_specs=[pl.BlockSpec((width // 4, pivots), lambda i: (i, 0))],
+        out_specs=(pl.BlockSpec((width // 4, pivots), lambda i: (i, 0)),) * 2,
+        compiler_params=grant(60),
+        name="halve",
+    )(lower_panel)
+    column, inverse_lo, maps, panel_high, panel_low, core, first = lax.optimization_barrier(
+        (column, inverse_lo, maps, panel_high, panel_low, core, first)
+    )
     sends = pl.pallas_call(
         lambda *refs: pack_kernel(count, *refs),
         out_shape=jax.ShapeDtypeStruct((across, srcs, width), jnp.float32),
         in_specs=[SMEM, VMEM],
         out_specs=VMEM,
+        compiler_params=grant(12),
         name="pack",
     )(maps, column)
     arrived = exchange(sends, "x")
@@ -136,6 +156,7 @@
         out_shape=jax.ShapeDtypeStruct((srcs, width), jnp.float32),
         in_specs=[SMEM, VMEM],
         out_specs=VMEM,
+        compiler_params=grant(8),
         name="pick",
     )(front_map, arrived)
     boundary, upper, right_side = lax.optimization_barrier(
@@ -153,71 +174,75 @@
         place,
         precision=lax.Precision.HIGHEST,
         preferred_element_type=jnp.float32,
-    ).reshape(across, piv_devs, part, pivots)
+    ).reshape(across, quarter, pivots)
+    inverse_high, inverse_low = pl.pallas_call(
+        halve_inverse_kernel,
+        grid=(across,),
+        out_shape=(jax.ShapeDtypeStruct((across, pivots, span), jnp.bfloat16),) * 2,
+        in_specs=[pl.BlockSpec((1, half, span), lambda i: (i, 0, 0))] * 2,
+        out_specs=(pl.BlockSpec((1, pivots, span), lambda i: (i, 0, 0)),) * 2,
+        compiler_params=grant(60),
+        name="halve_inverse",
+    )(inverse_lo.reshape(across, half, span), inverse_hi.reshape(across, half, span))
     full = lax.all_gather(boundary.reshape(across, part, width), PIV, axis=1, tiled=True)
-    full, inverse_hi, placed = lax.optimization_barrier((full, inverse_hi, placed))
-    short = part // 2
-    rows = piv_devs * short
-    chip = cores * short
+    full, inverse_high, inverse_low, placed = lax.optimization_barrier(
+        (full, inverse_high, inverse_low, placed)
+    )
+    cut = pivots // 3 * 2
+    rest = pivots - cut
+    few = quarter // deep
     share_a, share_b = pl.pallas_call(
         couple_kernel,
         grid=(across,),
         out_shape=(
-            jax.ShapeDtypeStruct((across, rows, pivots), jnp.float32),
-            jax.ShapeDtypeStruct((tall, across, chip, pivots), jnp.float32),
+            jax.ShapeDtypeStruct((across, quarter, cut), jnp.float32),
+            jax.ShapeDtypeStruct((deep, across, few, rest), jnp.float32),
         ),
         in_specs=[
-            pl.BlockSpec((1, piv_devs, part, width), lambda i: (i, 0, 0, 0)),
+            pl.BlockSpec((1, quarter, width), lambda i: (i, 0, 0)),
             pl.BlockSpec((width, pivots), lambda i: (0, 0)),
-            pl.BlockSpec((1, piv_devs, part, pivots), lambda i: (i, 0, 0, 0)),
+            pl.BlockSpec((width, pivots), lambda i: (0, 0)),
+            pl.BlockSpec((1, quarter, pivots), lambda i: (i, 0, 0)),
         ],
         out_specs=(
-            pl.BlockSpec((1, rows, pivots), lambda i: (i, 0, 0)),
-            pl.BlockSpec((tall, 1, chip, pivots), lambda i: (0, i, 0, 0)),
+            pl.BlockSpec((1, quarter, cut), lambda i: (i, 0, 0)),
+            pl.BlockSpec((deep, 1, few, rest), lambda i: (0, i, 0, 0)),
         ),
-        scratch_shapes=[
-            pltpu.VMEM((width, pivots), jnp.bfloat16),
-            pltpu.VMEM((width, pivots), jnp.bfloat16),
-        ],
-        compiler_params=pltpu.CompilerParams(vmem_limit_bytes=48 * 1024 * 1024),
+        compiler_params=grant(60),
         name="couple",
-    )(full.reshape(across, piv_devs, part, width), lower_panel, placed)
+    )(full, panel_high, panel_low, placed)
     nearer_b = lax.psum_scatter(share_b, "z", scatter_dimension=0, tiled=True)
     nearer_a = exchange(share_a, "x").sum(axis=0)
-    nearer_a = exchange(nearer_a.reshape(deep, chip, pivots), "z")
+    nearer_a = exchange(nearer_a.reshape(deep, few, cut), "z")
     nearer_a, nearer_b = lax.optimization_barrier((nearer_a, nearer_b))
-    nearer_b = exchange(nearer_b.reshape(across, chip, pivots), "x")
+    nearer_b = exchange(nearer_b.reshape(across, few, rest), "x")
     copies = pl.pallas_call(
         join_kernel,
-        out_shape=jax.ShapeDtypeStruct((deep, 2, chip, pivots), jnp.float32),
+        out_shape=jax.ShapeDtypeStruct((deep, few, pivots), jnp.float32),
         in_specs=[VMEM, VMEM],
         out_specs=VMEM,
+        compiler_params=grant(8),
         name="join",
     )(nearer_a, nearer_b)
     reduced = exchange(copies, "z").reshape(quarter, pivots)
-    core = lax.axis_index("c")
     kept, other = pl.pallas_call(
         solve_kernel,
         grid=(across,),
-        out_shape=(jax.ShapeDtypeStruct((across, tall, 2, short, span), jnp.float32),) * 2,
+        out_shape=(jax.ShapeDtypeStruct((across, tall, part, span), jnp.float32),) * 2,
         in_specs=[
             SMEM,
             pl.BlockSpec((quarter, pivots), lambda i: (0, 0)),
-            pl.BlockSpec((1, half, span), lambda i: (i, 0, 0)),
-            pl.BlockSpec((1, half, span), lambda i: (i, 0, 0)),
+            pl.BlockSpec((1, pivots, span), lambda i: (i, 0, 0)),
+            pl.BlockSpec((1, pivots, span), lambda i: (i, 0, 0)),
         ],
-        out_specs=(pl.BlockSpec((1, tall, 2, short, span), lambda i: (i, 0, 0, 0, 0)),) * 2,
+        out_specs=(pl.BlockSpec((1, tall, part, span), lambda i: (i, 0, 0, 0)),) * 2,
         scratch_shapes=[
             pltpu.VMEM((quarter, pivots), jnp.bfloat16),
             pltpu.VMEM((quarter, pivots), jnp.bfloat16),
         ],
+        compiler_params=grant(60),
         name="solve",
-    )(
-        core.reshape(1),
-        reduced,
-        inverse_lo.reshape(across, half, span),
-        inverse_hi.reshape(across, half, span),
-    )
+    )(core, reduced, inverse_high, inverse_low)
     kept = kept + lax.ppermute(other, "c", [(0, 1), (1, 0)])
     pieces = exchange(kept.reshape(across * tall, part, span), ("x", "y"))
     return pl.pallas_call(
@@ -226,8 +251,9 @@
         in_specs=[SMEM, SMEM, VMEM],
         out_specs=VMEM,
         scratch_shapes=[pltpu.VMEM((srcs, span + BLK), jnp.float32)],
+        compiler_params=grant(8),
         name="children",
-    )(child_start - me * span, child_len, pieces.reshape(across, tall, part, span))
+    )(first, child_len, pieces.reshape(across, tall, part, span))
 
 
 def solution(mesh):

time: 270 us -> 270 us (level)
  blocking collectives: 96.1 us -> 69.4 us
  waiting for transfers between devices: 91.3 us -> 107 us
  local copies, waits for them, and re-layouts: 6.6 us -> 11.8 us
  Pallas kernels: 24.8 us -> 28.5 us
    all_to_all x5 -> x4, blocking collectives: 96.1 us -> 69.4 us  [exchange(): return lax.all_to_all(value, axes, split_axis=0, concat_axis=0, tiled=True)]
    all_to_all x4 -> x5, waiting for transfers between devices: 57.7 us -> 70.1 us  [exchange(): return lax.all_to_all(value, axes, split_axis=0, concat_axis=0, tiled=True)]
    reduce_scatter x1, waiting for transfers between devices: 0.01 us -> 10.7 us  [body(): nearer_b = lax.psum_scatter(share_b, 'z', scatter_dimension=0, tiled=True)]
    pallas_call x1 -> x3, Pallas kernels: 1.99 us -> 9.47 us  [the longest x1 5.17 us: body(): pl.pallas_call(halve_inverse_kernel, grid=(across,), out_shape=(jax.Shape...]
    all_gather x1, waiting for transfers between devices: 19.5 us -> 13.6 us  [body(): lax.all_gather(boundary.reshape(across, part, width), PIV, axis=1, tiled=...]
    all_to_all x4 -> x5, starting transfers between devices: 19.1 us -> 23.3 us  [exchange(): return lax.all_to_all(value, axes, split_axis=0, concat_axis=0, tiled=True)]
  transfers between devices with their start and end apart: 8 -> 9, of which waited for: 7 -> 9; matrix products, arithmetic and copies ran while one was open for 3% -> 5% of each run, Pallas kernels for 0% -> 4%
where the time goes in v3:
time: 270 us; the launch traced here: 265 us
  waiting for transfers between devices  107 us (40%)
  blocking collectives  69.4 us (26%)
  starting transfers between devices  29.1 us (11%)
  Pallas kernels  28.5 us (11%)
  between operations  13.2 us (5%)
  local copies, waits for them, and re-layouts  11.8 us (4%)
  matrix products  3.12 us (1%)
    all_to_all x5, waiting for transfers between devices, exchange(): return lax.all_to_all(value, axes, split_axis=0, concat_axis=0, tiled=True)  70.1 us
    all_to_all x4, blocking collectives, exchange(): return lax.all_to_all(value, axes, split_axis=0, concat_axis=0, tiled=True)  69.4 us
    all_to_all x5, starting transfers between devices, exchange(): return lax.all_to_all(value, axes, split_axis=0, concat_axis=0, tiled=True)  23.3 us
    all_gather x1, waiting for transfers between devices, body(): lax.all_gather(boundary.reshape(across, part, width), PIV, axis=1, tiled=...  13.6 us
    reduce_scatter x1, waiting for transfers between devices, body(): nearer_b = lax.psum_scatter(share_b, 'z', scatter_dimension=0, tiled=True)  10.7 us
    all_gather x1, waiting for transfers between devices, body(): column = lax.all_gather(ancestor_sol, 'z', axis=0, tiled=False)  9.54 us
    pallas_call x1, Pallas kernels, body(): pl.pallas_call(couple_kernel, grid=(across,), out_shape=(jax.ShapeDtypeSt...  9.46 us
    pallas_call x1, Pallas kernels, body(): pl.pallas_call(solve_kernel, grid=(across,), out_shape=(jax.ShapeDtypeStr...  6.23 us
  transfers between devices with their start and end apart: 9, of which 9 were waited for; matrix products, arithmetic and copies ran while one was open for 5% of the time, Pallas kernels for 4%

profile of v3, /device:TPU:1, one launch (start us, length us, event | category | flops | bytes accessed | tf_op | source)
XLA Modules:
  0.0 265.0 jit_solution(14266529582283853534)
XLA Ops:
  8.5 4.8 %all-to-all-start.1 = ((s32[4,1,8]{2,1,0:T(1,128)}), s32[4,1,8]{2,1,0:T(1,128)S(1)}, u32[]{:S(2)}, u32[]{:S(2)}) async-start(s32[4,1,8]{2,1,0:T(1,128)} %broadcast_in_dim.7), calls=%async_computation.1 | async-start | bytes 4096 | tf_op jit(solution)/shard_map/all_to_all | solution.py:21
  14.6 2.7 %all-to-all-done.1 = s32[4,1,8]{2,1,0:T(1,128)S(1)} async-done(((s32[4,1,8]{2,1,0:T(1,128)}), s32[4,1,8]{2,1,0:T(1,128)S(1)}, u32[]{:S(2)}, u32[]{:S(2)}) %all-to-all-start.1) | async-done | bytes 160 | tf_op jit(solution)/shard_map/all_to_all | solution.py:21
  19.0 3.6 %all-to-all-start = ((f32[4,384,384]{2,1,0:T(8,128)}), f32[4,384,384]{2,1,0:T(8,128)S(1)}, u32[]{:S(2)}, u32[]{:S(2)}) async-start(f32[4,384,384]{2,1,0:T(8,128)} %broadcast_in_dim.6), calls=%async_computation | async-start | bytes 4718592 | tf_op jit(solution)/shard_map/all_to_all | solution.py:21
  22.7 4.2 %halve.1 = (bf16[1024,768]{1,0:T(8,128)(2,1)}, bf16[1024,768]{1,0:T(8,128)(2,1)}) custom-call(f32[1024,768]{1,0:T(8,128)} %value.1), custom_call_target="tpu_custom_call" | custom-call | tf_op jit(solution)/shard_map/halve/pallas_call | solution.py:133
  26.9 18.2 %all-to-all-done.inverse_lo = f32[4,384,384]{2,1,0:T(8,128)S(1)} async-done(((f32[4,384,384]{2,1,0:T(8,128)}), f32[4,384,384]{2,1,0:T(8,128)S(1)}, u32[]{:S(2)}, u32[]{:S(2)}) %all-to-all-start) | async-done | bytes 2359328 | tf_op jit(solution)/shard_map/all_to_all | solution.py:21
  45.2 9.5 %all-gather.6.cloned.1.call-done = f32[512,1024]{1,0:T(8,128)} async-done(((f32[64,1024]{1,0:T(8,128)}), f32[512,1024]{1,0:T(8,128)}) %all-gather.6.cloned.1.call-update) | async-done | bytes 2097168 | tf_op jit(solution)/shard_map/all_gather | solution.py:130
  57.0 13.5 %all_to_all.49.refs_1_ = f32[4,64,1024]{2,1,0:T(8,128)S(1)} all-to-all(f32[4,64,1024]{2,1,0:T(8,128)S(1)} %pack.1), channel_id=1, replica_groups=mesh['z'=8,'x'=4,'y'=8,'c'=2] {'x'}, dimensions={0} | all-to-all | bytes 2097152 | tf_op jit(solution)/shard_map/all_to_all | solution.py:21
  73.5 3.8 %all-to-all-start.3 = ((f32[4,384,384]{2,1,0:T(8,128)}), f32[4,384,384]{2,1,0:T(8,128)S(1)}, u32[]{:S(2)}, u32[]{:S(2)}) async-start(f32[4,384,384]{2,1,0:T(8,128)} %broadcast_in_dim.8), calls=%async_computation.3 | async-start | bytes 4718592 | tf_op jit(solution)/shard_map/all_to_all | solution.py:21
  80.3 3.1 %fusion.1.placed = f32[4,256,768]{2,1,0:T(8,128)} fusion(f32[4,256,24]{1,2,0:T(8,128)S(1)} %dot_general.5, s32[24]{0:T(128)S(1)} %iota_add_fusion), kind=kOutput, calls=%fused_computation.2 | convolution fusion | flops 226510848 | bytes 3244128 | tf_op jit(solution)/shard_map/dot_general | solution.py:172
  83.4 16.3 %all-to-all-done.3.inverse_hi = f32[4,384,384]{2,1,0:T(8,128)S(1)} async-done(((f32[4,384,384]{2,1,0:T(8,128)}), f32[4,384,384]{2,1,0:T(8,128)S(1)}, u32[]{:S(2)}, u32[]{:S(2)}) %all-to-all-start.3) | async-done | bytes 2359328 | tf_op jit(solution)/shard_map/all_to_all | solution.py:21
  101.1 5.2 %halve_inverse.1 = (bf16[4,768,384]{2,1,0:T(8,128)(2,1)}, bf16[4,768,384]{2,1,0:T(8,128)(2,1)}) custom-call(f32[4,384,384]{2,1,0:T(8,128)} %copy-done.3, f32[4,384,384]{2,1,0:T(8,128)} %copy-done.4), custom_call_target="tpu_custom_call" | custom-call | tf_op jit(solution)/shard_map/halve_inverse/pallas_call | solution.py:178
  106.3 13.6 %all-gather.4.cloned.1.call-done.full = f32[4,256,1024]{2,1,0:T(8,128)} async-done(((f32[4,16,1024]{2,1,0:T(8,128)}), f32[4,256,1024]{2,1,0:T(8,128)}) %all-gather.4.cloned.1.call-update) | async-done | bytes 4194320 | tf_op jit(solution)/shard_map/all_gather | solution.py:187
  119.9 9.5 %couple.1 = (f32[4,256,512]{2,1,0:T(8,128)}, f32[8,4,32,256]{3,2,1,0:T(8,128)}) custom-call(f32[4,256,1024]{2,1,0:T(8,128)} %all-gather.4.cloned.1.call-done.full, bf16[1024,768]{1,0:T(8,128)(2,1)} %get-tuple-element.42.high, bf16[1024,768]{1,0:T(8,128)(2,1)} %get-tuple-element.43.low, f32[4,256,768]{2,1,0:T(8,128)} %fusion.1.placed), custom_call_target="tpu_custom_call" | custom-call | tf_op jit(solution)/shard_map/couple/pallas_call | solution.py:194
  129.3 4.0 %all-to-all-start.4 = ((f32[4,256,512]{2,1,0:T(8,128)}), f32[4,256,512]{2,1,0:T(8,128)S(1)}, u32[]{:S(2)}, u32[]{:S(2)}) async-start(f32[4,256,512]{2,1,0:T(8,128)} %get-tuple-element.45), calls=%async_computation.4 | async-start | bytes 4194304 | tf_op jit(solution)/shard_map/all_to_all | solution.py:21
  134.0 25.2 %all-to-all-done.4 = f32[4,256,512]{2,1,0:T(8,128)S(1)} async-done(((f32[4,256,512]{2,1,0:T(8,128)}), f32[4,256,512]{2,1,0:T(8,128)S(1)}, u32[]{:S(2)}, u32[]{:S(2)}) %all-to-all-start.4) | async-done | bytes 2097184 | tf_op jit(solution)/shard_map/all_to_all | solution.py:21
  160.3 7.1 %all-to-all-start.5 = ((f32[8,32,512]{2,1,0:T(8,128)}), f32[8,32,512]{2,1,0:T(8,128)S(1)}, u32[]{:S(2)}, u32[]{:S(2)}) async-start(f32[8,32,512]{2,1,0:T(8,128)} %bitcast.6), calls=%async_computation.5 | async-start | bytes 1048576 | tf_op jit(solution)/shard_map/all_to_all | solution.py:21
  167.3 10.7 %reduce-scatter.2.cloned.1.call-done = f32[1,4,32,256]{3,2,1,0:T(8,128)} async-done(((f32[8,4,32,256]{3,2,1,0:T(8,128)}), f32[1,4,32,256]{3,2,1,0:T(8,128)}) %reduce-scatter.2.cloned.1.call-update) | async-done | bytes 131088 | tf_op jit(solution)/shard_map/reduce_scatter | solution.py:214
  178.1 7.6 %all-to-all-done.5.pieces_a = f32[8,32,512]{2,1,0:T(8,128)S(1)} async-done(((f32[8,32,512]{2,1,0:T(8,128)}), f32[8,32,512]{2,1,0:T(8,128)S(1)}, u32[]{:S(2)}, u32[]{:S(2)}) %all-to-all-start.5) | async-done | bytes 524320 | tf_op jit(solution)/shard_map/all_to_all | solution.py:21
  185.7 8.1 %all_to_all.50.pieces_b = f32[4,32,256]{2,1,0:T(8,128)S(1)} all-to-all(f32[4,32,256]{2,1,0:T(8,128)} %bitcast.26), channel_id=1, replica_groups=mesh['z'=8,'x'=4,'y'=8,'c'=2] {'x'}, dimensions={0} | all-to-all | bytes 262144 | tf_op jit(solution)/shard_map/all_to_all | solution.py:21
  193.9 23.4 %all_to_all.51 = f32[8,32,768]{2,1,0:T(8,128)} all-to-all(f32[8,32,768]{2,1,0:T(8,128)S(1)} %join.1), channel_id=1, replica_groups=mesh['z'=8,'x'=4,'y'=8,'c'=2] {'z'}, dimensions={0} | all-to-all | bytes 1572864 | tf_op jit(solution)/shard_map/all_to_all | solution.py:21
  217.2 6.2 %solve.1 = (f32[4,8,16,384]{3,2,1,0:T(8,128)}, f32[4,8,16,384]{3,2,1,0:T(8,128)}) custom-call(s32[1]{0:T(128)} %bitcast.2.core, f32[256,768]{1,0:T(8,128)} %bitcast.25, bf16[4,768,384]{2,1,0:T(8,128)(2,1)} %get-tuple-element.49.inverse_high, bf16[4,768,384]{2,1,0:T(8,128)(2,1)} %get-tuple-element.50.inverse_low), custom_call_target="tpu_custom_call" | custom-call | tf_op jit(solution)/shard_map/solve/pallas_call | solution.py:228
  223.5 5.8 %collective-permute-start = (f32[4,8,16,384]{3,2,1,0:T(8,128)}, f32[4,8,16,384]{3,2,1,0:T(8,128)S(1)}, u32[]{:S(2)}, u32[]{:S(2)}) collective-permute-start(f32[4,8,16,384]{3,2,1,0:T(8,128)} %get-tuple-element.52), channel_id=1, source_target_pairs={{0,1},{1,0},{2,3},{3,2},{4,5},{5,4},{6,7},{7,6},{8,9},{9,8},{10,11... | collective-permute-start | bytes 2359304 | tf_op jit(solution)/shard_map/ppermute | solution.py:246
  229.3 2.1 collective-permute-done
  232.6 24.4 %all_to_all.52 = f32[32,16,384]{2,1,0:T(8,128)S(1)} all-to-all(f32[32,16,384]{2,1,0:T(8,128)S(1)} %bitcast.24), channel_id=1, replica_groups=mesh['z'=8,'x'=4,'y'=8,'c'=2] {'x','y'}, dimensions={0} | all-to-all | bytes 1572864 | tf_op jit(solution)/shard_map/all_to_all | solution.py:21
  (35 shorter events, 19.0 us)
Async XLA Ops:
  6.5 48.2 %all-gather.6.cloned.1.call-start = ((), (), s32[]{:S(2)}) async-start(), calls=%async_computation.12 | async-start | bytes 2359296 | tf_op jit(solution)/shard_map/all_gather | solution.py:130
  8.5 8.9 %all-to-all-start.1 = ((s32[4,1,8]{2,1,0:T(1,128)}), s32[4,1,8]{2,1,0:T(1,128)S(1)}, u32[]{:S(2)}, u32[]{:S(2)}) async-start(s32[4,1,8]{2,1,0:T(1,128)} %broadcast_in_dim.7), calls=%async_computation.1 | async-start | bytes 4096 | tf_op jit(solution)/shard_map/all_to_all | solution.py:21
  19.0 26.2 %all-to-all-start = ((f32[4,384,384]{2,1,0:T(8,128)}), f32[4,384,384]{2,1,0:T(8,128)S(1)}, u32[]{:S(2)}, u32[]{:S(2)}) async-start(f32[4,384,384]{2,1,0:T(8,128)} %broadcast_in_dim.6), calls=%async_computation | async-start | bytes 4718592 | tf_op jit(solution)/shard_map/all_to_all | solution.py:21
  22.6 4.3 %copy-start.6 = (s32[4]{0:T(128)S(1)}, s32[4]{0:T(128)}, u32[]{:S(2)}) copy-start(s32[4]{0:T(128)} %param.12) | copy-start | bytes 52
  22.6 97.3 %all-gather.4.cloned.1.call-start = ((), (), s32[]{:S(2)}) async-start(), calls=%async_computation.10 | async-start | bytes 4456448 | tf_op jit(solution)/shard_map/all_gather | solution.py:187
  45.2 25.4 %copy-start.3 = (f32[4,384,384]{2,1,0:T(8,128)}, f32[4,384,384]{2,1,0:T(8,128)S(1)}, u32[]{:S(2)}) copy-start(f32[4,384,384]{2,1,0:T(8,128)S(1)} %all-to-all-done.inverse_lo) | copy-start | bytes 7077892
  54.7 1.6 copy-start
  56.3 14.2 %copy-start.1 = (s32[8]{0:T(128)S(1)}, s32[8]{0:T(128)}, u32[]{:S(2)}) copy-start(s32[8]{0:T(128)} %refs_0_.1) | copy-start | bytes 100
  73.5 3.8 %copy-start.5 = (f32[1024,24]{0,1:T(8,128)S(1)}, f32[1024,24]{0,1:T(8,128)}, u32[]{:S(2)}) copy-start(f32[1024,24]{0,1:T(8,128)} %param.11) | copy-start | bytes 294916
  73.5 26.2 %all-to-all-start.3 = ((f32[4,384,384]{2,1,0:T(8,128)}), f32[4,384,384]{2,1,0:T(8,128)S(1)}, u32[]{:S(2)}, u32[]{:S(2)}) async-start(f32[4,384,384]{2,1,0:T(8,128)} %broadcast_in_dim.8), calls=%async_computation.3 | async-start | bytes 4718592 | tf_op jit(solution)/shard_map/all_to_all | solution.py:21
  99.7 1.4 copy-start.4
  129.3 29.9 %all-to-all-start.4 = ((f32[4,256,512]{2,1,0:T(8,128)}), f32[4,256,512]{2,1,0:T(8,128)S(1)}, u32[]{:S(2)}, u32[]{:S(2)}) async-start(f32[4,256,512]{2,1,0:T(8,128)} %get-tuple-element.45), calls=%async_computation.4 | async-start | bytes 4194304 | tf_op jit(solution)/shard_map/all_to_all | solution.py:21
  133.3 44.8 %reduce-scatter.2.cloned.1.call-start = ((), (), s32[]{:S(2)}) async-start(), calls=%async_computation.11 | async-start | bytes 1179648 | tf_op jit(solution)/shard_map/reduce_scatter | solution.py:214
  160.3 25.4 %all-to-all-start.5 = ((f32[8,32,512]{2,1,0:T(8,128)}), f32[8,32,512]{2,1,0:T(8,128)S(1)}, u32[]{:S(2)}, u32[]{:S(2)}) async-start(f32[8,32,512]{2,1,0:T(8,128)} %bitcast.6), calls=%async_computation.5 | async-start | bytes 1048576 | tf_op jit(solution)/shard_map/all_to_all | solution.py:21
  223.5 33.6 %copy-start.2 = (s32[4]{0:T(128)S(1)}, s32[4]{0:T(128)}, u32[]{:S(2)}) copy-start(s32[4]{0:T(128)} %length.1) | copy-start | bytes 52
  223.5 7.9 %collective-permute-start = (f32[4,8,16,384]{3,2,1,0:T(8,128)}, f32[4,8,16,384]{3,2,1,0:T(8,128)S(1)}, u32[]{:S(2)}, u32[]{:S(2)}) collective-permute-start(f32[4,8,16,384]{3,2,1,0:T(8,128)} %get-tuple-element.52), channel_id=1, source_target_pairs={{0,1},{1,0},{2,3},{3,2},{4,5},{5,4},{6,7},{7,6},{8,9},{9,8},{10,11... | collective-permute-start | bytes 2359304 | tf_op jit(solution)/shard_map/ppermute | solution.py:246
Sparse Core Ops, SparseCore 0:
  9.4 45.2 all-gather.5
  72.0 47.8 all-gather.3
  136.9 41.0 reduce-scatter.1

commit v4 on v3

--- a/solution.py
+++ b/solution.py
@@ -64,12 +64,15 @@
     high[:, half:], low[:, half:] = split(inverse_hi[...])
 
 
-def couple_kernel(full, high, low, placed, share_a, share_b):
-    left = split(full[0])
-    result = placed[0] - product(left, (high[...], low[...]))
-    cut = share_a.shape[2]
-    share_a[0] = result[:, :cut]
-    share_b[:, 0] = result[:, cut:].reshape(share_b.shape[0], *share_b.shape[2:])
+def couple_kernel(position, full, high, low, placed, *shares):
+    across = len(shares)
+    step = pl.program_id(0)
+    result = placed[0] - product(split(full[0]), (high[...], low[...]))
+    for slot in range(across):
+
+        @pl.when(step == (slot + across - 1) % across)
+        def _():
+            shares[slot][...] = result
 
 
 def join_kernel(pieces_a, pieces_b, copies):
@@ -188,34 +191,54 @@
     full, inverse_high, inverse_low, placed = lax.optimization_barrier(
         (full, inverse_high, inverse_low, placed)
     )
-    cut = pivots // 3 * 2
-    rest = pivots - cut
     few = quarter // deep
-    share_a, share_b = pl.pallas_call(
-        couple_kernel,
-        grid=(across,),
-        out_shape=(
-            jax.ShapeDtypeStruct((across, quarter, cut), jnp.float32),
-            jax.ShapeDtypeStruct((deep, across, few, rest), jnp.float32),
-        ),
-        in_specs=[
-            pl.BlockSpec((1, quarter, width), lambda i: (i, 0, 0)),
-            pl.BlockSpec((width, pivots), lambda i: (0, 0)),
-            pl.BlockSpec((width, pivots), lambda i: (0, 0)),
-            pl.BlockSpec((1, quarter, pivots), lambda i: (i, 0, 0)),
-        ],
-        out_specs=(
-            pl.BlockSpec((1, quarter, cut), lambda i: (i, 0, 0)),
-            pl.BlockSpec((deep, 1, few, rest), lambda i: (0, i, 0, 0)),
-        ),
-        compiler_params=grant(60),
-        name="couple",
-    )(full, panel_high, panel_low, placed)
-    nearer_b = lax.psum_scatter(share_b, "z", scatter_dimension=0, tiled=True)
-    nearer_a = exchange(share_a, "x").sum(axis=0)
-    nearer_a = exchange(nearer_a.reshape(deep, few, cut), "z")
-    nearer_a, nearer_b = lax.optimization_barrier((nearer_a, nearer_b))
-    nearer_b = exchange(nearer_b.reshape(across, few, rest), "x")
+    position = lax.axis_index("x").reshape(1)
+
+    def coupled(side):
+        block = pl.BlockSpec((quarter, half), lambda i, at: (0, 0))
+        return pl.pallas_call(
+            couple_kernel,
+            grid_spec=pltpu.PrefetchScalarGridSpec(
+                num_scalar_prefetch=1,
+                grid=(across,),
+                in_specs=[
+                    pl.BlockSpec(
+                        (1, quarter, width), lambda i, at: (lax.rem(at[0] + 1 + i, across), 0, 0)
+                    ),
+                    pl.BlockSpec((width, half), lambda i, at: (0, side)),
+                    pl.BlockSpec((width, half), lambda i, at: (0, side)),
+                    pl.BlockSpec(
+                        (1, quarter, half), lambda i, at: (lax.rem(at[0] + 1 + i, across), 0, side)
+                    ),
+                ],
+                out_specs=(block,) * across,
+            ),
+            out_shape=(jax.ShapeDtypeStruct((quarter, half), jnp.float32),) * across,
+            compiler_params=grant(60),
+            cost_estimate=pl.CostEstimate(
+                flops=6 * total * width * half,
+                bytes_accessed=4 * (total * width + width * half + 2 * total * half),
+                transcendentals=0,
+            ),
+            name="couple",
+        )(position, full, panel_high, panel_low, placed)
+
+    def across_sent(shares):
+        return [
+            lax.ppermute(shares[k], "x", [(i, (i + k) % across) for i in range(across)])
+            for k in range(1, across)
+        ]
+
+    def nearer(shares, arrived):
+        summed = shares[0] + sum(arrived[1:], arrived[0])
+        return exchange(summed.reshape(deep, few, half), "z")
+
+    shares_a = coupled(0)
+    arrived_a = across_sent(shares_a)
+    shares_b = coupled(1)
+    arrived_b = across_sent(shares_b)
+    nearer_a = nearer(shares_a, arrived_a)
+    nearer_b = nearer(shares_b, arrived_b)
     copies = pl.pallas_call(
         join_kernel,
         out_shape=jax.ShapeDtypeStruct((deep, few, pivots), jnp.float32),

time: 270 us -> 286 us (1.059)
  starting transfers between devices: 29.1 us -> 45.4 us
  waiting for transfers between devices: 107 us -> 92.9 us
  blocking collectives: 69.4 us -> 75.5 us
  Pallas kernels: 28.5 us -> 34 us
    all_to_all x5 -> x4, waiting for transfers between devices: 70.1 us -> 37.3 us  [exchange(): return lax.all_to_all(value, axes, split_axis=0, concat_axis=0, tiled=True)]
    ppermute x0 -> x6, waiting for transfers between devices: none -> 29.6 us  [across_sent(): lax.ppermute(shares[k], 'x', [(i, (i + k) % across) for i in range(across)])]
    ppermute x0 -> x6, starting transfers between devices: none -> 18.5 us  [across_sent(): lax.ppermute(shares[k], 'x', [(i, (i + k) % across) for i in range(across)])]
    reduce_scatter x1 -> x0, waiting for transfers between devices: 10.7 us -> none  [body(): nearer_b = lax.psum_scatter(share_b, 'z', scatter_dimension=0, tiled=True)]
    all_to_all x4, blocking collectives: 69.4 us -> 75.5 us  [exchange(): return lax.all_to_all(value, axes, split_axis=0, concat_axis=0, tiled=True)]
    pallas_call x1 -> x2, Pallas kernels: 9.46 us -> 15 us  [coupled(): pl.pallas_call(couple_kernel, grid_spec=pltpu.PrefetchScalarGridSpec(num_...]
    all_to_all x5 -> x4, starting transfers between devices: 23.3 us -> 19.3 us  [exchange(): return lax.all_to_all(value, axes, split_axis=0, concat_axis=0, tiled=True)]
    add x0 -> x2, other arithmetic: none -> 2.99 us  [nearer(): summed = shares[0] + sum(arrived[1:], arrived[0])]
  transfers between devices with their start and end apart: 9 -> 13, of which waited for: 9 -> 11; matrix products, arithmetic and copies ran while one was open for 5% -> 5% of each run, Pallas kernels for 4% -> 6%
where the time goes in v4:
time: 286 us; the launch traced here: 281 us
  waiting for transfers between devices  92.9 us (32%)
  blocking collectives  75.5 us (26%)
  starting transfers between devices  45.4 us (16%)
  Pallas kernels  34 us (12%)
  between operations  13.6 us (5%)
  local copies, waits for them, and re-layouts  11.7 us (4%)
  other arithmetic  4.21 us (1%)
  matrix products  3.13 us (1%)
    all_to_all x4, blocking collectives, exchange(): return lax.all_to_all(value, axes, split_axis=0, concat_axis=0, tiled=True)  75.5 us
    all_to_all x4, waiting for transfers between devices, exchange(): return lax.all_to_all(value, axes, split_axis=0, concat_axis=0, tiled=True)  37.3 us
    ppermute x6, waiting for transfers between devices, across_sent(): lax.ppermute(shares[k], 'x', [(i, (i + k) % across) for i in range(across)])  29.6 us
    all_to_all x4, starting transfers between devices, exchange(): return lax.all_to_all(value, axes, split_axis=0, concat_axis=0, tiled=True)  19.3 us
    ppermute x6, starting transfers between devices, across_sent(): lax.ppermute(shares[k], 'x', [(i, (i + k) % across) for i in range(across)])  18.5 us
    pallas_call x2, Pallas kernels, coupled(): pl.pallas_call(couple_kernel, grid_spec=pltpu.PrefetchScalarGridSpec(num_...  15 us
    all_gather x1, waiting for transfers between devices, body(): lax.all_gather(boundary.reshape(across, part, width), PIV, axis=1, tiled=...  13.6 us
    all_gather x1, waiting for transfers between devices, body(): column = lax.all_gather(ancestor_sol, 'z', axis=0, tiled=False)  9.58 us
  transfers between devices with their start and end apart: 13, of which 11 were waited for; matrix products, arithmetic and copies ran while one was open for 5% of the time, Pallas kernels for 6%

profile of v4, /device:TPU:1, one launch (start us, length us, event | category | flops | bytes accessed | tf_op | source)
XLA Modules:
  0.0 280.5 jit_solution(16785442366967979539)
XLA Ops:
  8.5 4.8 %all-to-all-start.1 = ((s32[4,1,8]{2,1,0:T(1,128)}), s32[4,1,8]{2,1,0:T(1,128)S(1)}, u32[]{:S(2)}, u32[]{:S(2)}) async-start(s32[4,1,8]{2,1,0:T(1,128)} %broadcast_in_dim.7), calls=%async_computation.1 | async-start | bytes 4096 | tf_op jit(solution)/shard_map/all_to_all | solution.py:21
  18.9 3.6 %all-to-all-start = ((f32[4,384,384]{2,1,0:T(8,128)}), f32[4,384,384]{2,1,0:T(8,128)S(1)}, u32[]{:S(2)}, u32[]{:S(2)}) async-start(f32[4,384,384]{2,1,0:T(8,128)} %broadcast_in_dim.6), calls=%async_computation | async-start | bytes 4718592 | tf_op jit(solution)/shard_map/all_to_all | solution.py:21
  22.7 4.2 %halve.1 = (bf16[1024,768]{1,0:T(8,128)(2,1)}, bf16[1024,768]{1,0:T(8,128)(2,1)}) custom-call(f32[1024,768]{1,0:T(8,128)} %value.1), custom_call_target="tpu_custom_call" | custom-call | tf_op jit(solution)/shard_map/halve/pallas_call | solution.py:136
  26.9 18.3 %all-to-all-done.inverse_lo = f32[4,384,384]{2,1,0:T(8,128)S(1)} async-done(((f32[4,384,384]{2,1,0:T(8,128)}), f32[4,384,384]{2,1,0:T(8,128)S(1)}, u32[]{:S(2)}, u32[]{:S(2)}) %all-to-all-start) | async-done | bytes 2359328 | tf_op jit(solution)/shard_map/all_to_all | solution.py:21
  45.1 9.6 %all-gather.6.cloned.1.call-done = f32[512,1024]{1,0:T(8,128)} async-done(((f32[64,1024]{1,0:T(8,128)}), f32[512,1024]{1,0:T(8,128)}) %all-gather.6.cloned.1.call-update) | async-done | bytes 2097168 | tf_op jit(solution)/shard_map/all_gather | solution.py:133
  57.0 13.5 %all_to_all.44.refs_1_ = f32[4,64,1024]{2,1,0:T(8,128)S(1)} all-to-all(f32[4,64,1024]{2,1,0:T(8,128)S(1)} %pack.1), channel_id=1, replica_groups=mesh['z'=8,'x'=4,'y'=8,'c'=2] {'x'}, dimensions={0} | all-to-all | bytes 2097152 | tf_op jit(solution)/shard_map/all_to_all | solution.py:21
  73.5 3.8 %all-to-all-start.3 = ((f32[4,384,384]{2,1,0:T(8,128)}), f32[4,384,384]{2,1,0:T(8,128)S(1)}, u32[]{:S(2)}, u32[]{:S(2)}) async-start(f32[4,384,384]{2,1,0:T(8,128)} %broadcast_in_dim.8), calls=%async_computation.3 | async-start | bytes 4718592 | tf_op jit(solution)/shard_map/all_to_all | solution.py:21
  83.4 16.3 %all-to-all-done.3.inverse_hi = f32[4,384,384]{2,1,0:T(8,128)S(1)} async-done(((f32[4,384,384]{2,1,0:T(8,128)}), f32[4,384,384]{2,1,0:T(8,128)S(1)}, u32[]{:S(2)}, u32[]{:S(2)}) %all-to-all-start.3) | async-done | bytes 2359328 | tf_op jit(solution)/shard_map/all_to_all | solution.py:21
  101.1 5.2 %halve_inverse.1 = (bf16[4,768,384]{2,1,0:T(8,128)(2,1)}, bf16[4,768,384]{2,1,0:T(8,128)(2,1)}) custom-call(f32[4,384,384]{2,1,0:T(8,128)} %copy-done.3, f32[4,384,384]{2,1,0:T(8,128)} %copy-done.4), custom_call_target="tpu_custom_call" | custom-call | tf_op jit(solution)/shard_map/halve_inverse/pallas_call | solution.py:181
  106.3 13.6 %all-gather.4.cloned.1.call-done.full = f32[4,256,1024]{2,1,0:T(8,128)} async-done(((f32[4,16,1024]{2,1,0:T(8,128)}), f32[4,256,1024]{2,1,0:T(8,128)}) %all-gather.4.cloned.1.call-update) | async-done | bytes 4194320 | tf_op jit(solution)/shard_map/all_gather | solution.py:190
  119.8 7.5 %couple.2 = (f32[256,384]{1,0:T(8,128)}, f32[256,384]{1,0:T(8,128)}, f32[256,384]{1,0:T(8,128)}, f32[256,384]{1,0:T(8,128)}) custom-call(s32[1]{0:T(128)} %bitcast.3.position, f32[4,256,1024]{2,1,0:T(8,128)} %all-gather.4.cloned.1.call-done.full, bf16[1024,768]{1,0:T(8,128)(2,1)} %get-tuple-element.46.high, bf16[1024,768]{1,0:T(8,128)(2,1)} %get-tuple-element.47.low, ...), custom_call_target="tpu_custom_call" | custom-call | flops 2415919104 | bytes 8912896 | tf_op jit(solution)/shard_map/couple/pallas_call | solution.py:199
  127.3 4.3 %collective-permute-start.2 = (f32[256,384]{1,0:T(8,128)}, f32[256,384]{1,0:T(8,128)S(1)}, u32[]{:S(2)}, u32[]{:S(2)}) collective-permute-start(f32[256,384]{1,0:T(8,128)} %get-tuple-element.52), channel_id=1, source_target_pairs={{0,48},{16,0},{32,16},{48,32},{1,49},{17,1},{33,17},{49,33},{2,50}... | collective-permute-start | bytes 1179656 | tf_op jit(solution)/shard_map/ppermute | solution.py:228
  133.6 3.6 %collective-permute-start.1 = (f32[256,384]{1,0:T(8,128)}, f32[256,384]{1,0:T(8,128)S(1)}, u32[]{:S(2)}, u32[]{:S(2)}) collective-permute-start(f32[256,384]{1,0:T(8,128)} %get-tuple-element.51), channel_id=1, source_target_pairs={{0,32},{16,48},{32,0},{48,16},{1,33},{17,49},{33,1},{49,17},{2,34}... | collective-permute-start | bytes 1179656 | tf_op jit(solution)/shard_map/ppermute | solution.py:228
  137.2 11.2 %collective-permute-done.2 = f32[256,384]{1,0:T(8,128)S(1)} collective-permute-done((f32[256,384]{1,0:T(8,128)}, f32[256,384]{1,0:T(8,128)S(1)}, u32[]{:S(2)}, u32[]{:S(2)}) %collective-permute-start.2) | collective-permute-done | bytes 393248 | tf_op jit(solution)/shard_map/ppermute | solution.py:228
  148.4 4.2 %collective-permute-done.1 = f32[256,384]{1,0:T(8,128)S(1)} collective-permute-done((f32[256,384]{1,0:T(8,128)}, f32[256,384]{1,0:T(8,128)S(1)}, u32[]{:S(2)}, u32[]{:S(2)}) %collective-permute-start.1) | collective-permute-done | bytes 393248 | tf_op jit(solution)/shard_map/ppermute | solution.py:228
  154.5 7.1 %all-to-all-start.4 = ((f32[8,32,384]{2,1,0:T(8,128)}), f32[8,32,384]{2,1,0:T(8,128)S(1)}, u32[]{:S(2)}, u32[]{:S(2)}) async-start(f32[8,32,384]{2,1,0:T(8,128)} %bitcast.7), calls=%async_computation.4 | async-start | bytes 786432 | tf_op jit(solution)/shard_map/all_to_all | solution.py:21
  161.6 7.5 %couple.3 = (f32[256,384]{1,0:T(8,128)}, f32[256,384]{1,0:T(8,128)}, f32[256,384]{1,0:T(8,128)}, f32[256,384]{1,0:T(8,128)}) custom-call(s32[1]{0:T(128)} %bitcast.3.position, f32[4,256,1024]{2,1,0:T(8,128)} %all-gather.4.cloned.1.call-done.full, bf16[1024,768]{1,0:T(8,128)(2,1)} %get-tuple-element.46.high, bf16[1024,768]{1,0:T(8,128)(2,1)} %get-tuple-element.47.low, ...), custom_call_target="tpu_custom_call" | custom-call | flops 2415919104 | bytes 8912896 | tf_op jit(solution)/shard_map/couple/pallas_call | solution.py:199
  171.0 3.4 %collective-permute-start.3 = (f32[256,384]{1,0:T(8,128)}, f32[256,384]{1,0:T(8,128)S(1)}, u32[]{:S(2)}, u32[]{:S(2)}) collective-permute-start(f32[256,384]{1,0:T(8,128)} %get-tuple-element.54), channel_id=1, source_target_pairs={{0,16},{16,32},{32,48},{48,0},{1,17},{17,33},{33,49},{49,1},{2,18}... | collective-permute-start | bytes 1179656 | tf_op jit(solution)/shard_map/ppermute | solution.py:228
  182.4 9.5 %collective-permute-done.4 = f32[256,384]{1,0:T(8,128)S(1)} collective-permute-done((f32[256,384]{1,0:T(8,128)}, f32[256,384]{1,0:T(8,128)S(1)}, u32[]{:S(2)}, u32[]{:S(2)}) %collective-permute-start.4) | collective-permute-done | bytes 393248 | tf_op jit(solution)/shard_map/ppermute | solution.py:228
  193.1 17.7 %all_to_all.45.pieces_b = f32[8,32,384]{2,1,0:T(8,128)S(1)} all-to-all(f32[8,32,384]{2,1,0:T(8,128)S(1)} %bitcast.27), channel_id=1, replica_groups=mesh['z'=8,'x'=4,'y'=8,'c'=2] {'z'}, dimensions={0} | all-to-all | bytes 786432 | tf_op jit(solution)/shard_map/all_to_all | solution.py:21
  210.8 21.6 %all_to_all.46 = f32[8,32,768]{2,1,0:T(8,128)} all-to-all(f32[8,32,768]{2,1,0:T(8,128)S(1)} %join.1), channel_id=1, replica_groups=mesh['z'=8,'x'=4,'y'=8,'c'=2] {'z'}, dimensions={0} | all-to-all | bytes 1572864 | tf_op jit(solution)/shard_map/all_to_all | solution.py:21
  232.4 6.2 %solve.1 = (f32[4,8,16,384]{3,2,1,0:T(8,128)}, f32[4,8,16,384]{3,2,1,0:T(8,128)}) custom-call(s32[1]{0:T(128)} %bitcast.2.core, f32[256,768]{1,0:T(8,128)} %bitcast.26, bf16[4,768,384]{2,1,0:T(8,128)(2,1)} %get-tuple-element.57.inverse_high, bf16[4,768,384]{2,1,0:T(8,128)(2,1)} %get-tuple-element.58.inverse_low), custom_call_target="tpu_custom_call" | custom-call | tf_op jit(solution)/shard_map/solve/pallas_call | solution.py:251
  238.6 7.6 %collective-permute-start.6 = (f32[4,8,16,384]{3,2,1,0:T(8,128)}, f32[4,8,16,384]{3,2,1,0:T(8,128)S(1)}, u32[]{:S(2)}, u32[]{:S(2)}) collective-permute-start(f32[4,8,16,384]{3,2,1,0:T(8,128)} %get-tuple-element.60), channel_id=1, source_target_pairs={{0,1},{1,0},{2,3},{3,2},{4,5},{5,4},{6,7},{7,6},{8,9},{9,8},{10,11... | collective-permute-start | bytes 2359304 | tf_op jit(solution)/shard_map/ppermute | solution.py:269
  249.5 22.8 %all_to_all.47 = f32[32,16,384]{2,1,0:T(8,128)S(1)} all-to-all(f32[32,16,384]{2,1,0:T(8,128)S(1)} %bitcast.25), channel_id=1, replica_groups=mesh['z'=8,'x'=4,'y'=8,'c'=2] {'x','y'}, dimensions={0} | all-to-all | bytes 1572864 | tf_op jit(solution)/shard_map/all_to_all | solution.py:21
  (44 shorter events, 40.0 us)
Async XLA Ops:
  6.5 48.2 %all-gather.6.cloned.1.call-start = ((), (), s32[]{:S(2)}) async-start(), calls=%async_computation.9 | async-start | bytes 2359296 | tf_op jit(solution)/shard_map/all_gather | solution.py:133
  8.5 8.9 %all-to-all-start.1 = ((s32[4,1,8]{2,1,0:T(1,128)}), s32[4,1,8]{2,1,0:T(1,128)S(1)}, u32[]{:S(2)}, u32[]{:S(2)}) async-start(s32[4,1,8]{2,1,0:T(1,128)} %broadcast_in_dim.7), calls=%async_computation.1 | async-start | bytes 4096 | tf_op jit(solution)/shard_map/all_to_all | solution.py:21
  18.9 26.2 %all-to-all-start = ((f32[4,384,384]{2,1,0:T(8,128)}), f32[4,384,384]{2,1,0:T(8,128)S(1)}, u32[]{:S(2)}, u32[]{:S(2)}) async-start(f32[4,384,384]{2,1,0:T(8,128)} %broadcast_in_dim.6), calls=%async_computation | async-start | bytes 4718592 | tf_op jit(solution)/shard_map/all_to_all | solution.py:21
  22.6 4.3 %copy-start.6 = (s32[4]{0:T(128)S(1)}, s32[4]{0:T(128)}, u32[]{:S(2)}) copy-start(s32[4]{0:T(128)} %param.12) | copy-start | bytes 52
  22.6 97.2 %all-gather.4.cloned.1.call-start = ((), (), s32[]{:S(2)}) async-start(), calls=%async_computation.8 | async-start | bytes 4456448 | tf_op jit(solution)/shard_map/all_gather | solution.py:190
  45.1 25.4 %copy-start.3 = (f32[4,384,384]{2,1,0:T(8,128)}, f32[4,384,384]{2,1,0:T(8,128)S(1)}, u32[]{:S(2)}) copy-start(f32[4,384,384]{2,1,0:T(8,128)S(1)} %all-to-all-done.inverse_lo) | copy-start | bytes 7077892
  54.7 1.6 copy-start
  56.3 14.2 %copy-start.1 = (s32[8]{0:T(128)S(1)}, s32[8]{0:T(128)}, u32[]{:S(2)}) copy-start(s32[8]{0:T(128)} %refs_0_.1) | copy-start | bytes 100
  73.5 3.8 %copy-start.5 = (f32[1024,24]{0,1:T(8,128)S(1)}, f32[1024,24]{0,1:T(8,128)}, u32[]{:S(2)}) copy-start(f32[1024,24]{0,1:T(8,128)} %param.11) | copy-start | bytes 294916
  73.5 26.2 %all-to-all-start.3 = ((f32[4,384,384]{2,1,0:T(8,128)}), f32[4,384,384]{2,1,0:T(8,128)S(1)}, u32[]{:S(2)}, u32[]{:S(2)}) async-start(f32[4,384,384]{2,1,0:T(8,128)} %broadcast_in_dim.8), calls=%async_computation.3 | async-start | bytes 4718592 | tf_op jit(solution)/shard_map/all_to_all | solution.py:21
  99.7 1.4 copy-start.4
  127.3 21.1 %collective-permute-start.2 = (f32[256,384]{1,0:T(8,128)}, f32[256,384]{1,0:T(8,128)S(1)}, u32[]{:S(2)}, u32[]{:S(2)}) collective-permute-start(f32[256,384]{1,0:T(8,128)} %get-tuple-element.52), channel_id=1, source_target_pairs={{0,48},{16,0},{32,16},{48,32},{1,49},{17,1},{33,17},{49,33},{2,50}... | collective-permute-start | bytes 1179656 | tf_op jit(solution)/shard_map/ppermute | solution.py:228
  131.6 16.8 %collective-permute-start = (f32[256,384]{1,0:T(8,128)}, f32[256,384]{1,0:T(8,128)S(1)}, u32[]{:S(2)}, u32[]{:S(2)}) collective-permute-start(f32[256,384]{1,0:T(8,128)} %get-tuple-element.50), channel_id=1, source_target_pairs={{0,16},{16,32},{32,48},{48,0},{1,17},{17,33},{33,49},{49,1},{2,18}... | collective-permute-start | bytes 1179656 | tf_op jit(solution)/shard_map/ppermute | solution.py:228
  133.6 19.0 %collective-permute-start.1 = (f32[256,384]{1,0:T(8,128)}, f32[256,384]{1,0:T(8,128)S(1)}, u32[]{:S(2)}, u32[]{:S(2)}) collective-permute-start(f32[256,384]{1,0:T(8,128)} %get-tuple-element.51), channel_id=1, source_target_pairs={{0,32},{16,48},{32,0},{48,16},{1,33},{17,49},{33,1},{49,17},{2,34}... | collective-permute-start | bytes 1179656 | tf_op jit(solution)/shard_map/ppermute | solution.py:228
  154.5 38.6 %all-to-all-start.4 = ((f32[8,32,384]{2,1,0:T(8,128)}), f32[8,32,384]{2,1,0:T(8,128)S(1)}, u32[]{:S(2)}, u32[]{:S(2)}) async-start(f32[8,32,384]{2,1,0:T(8,128)} %bitcast.7), calls=%async_computation.4 | async-start | bytes 786432 | tf_op jit(solution)/shard_map/all_to_all | solution.py:21
  169.1 10.2 %collective-permute-start.5 = (f32[256,384]{1,0:T(8,128)}, f32[256,384]{1,0:T(8,128)S(1)}, u32[]{:S(2)}, u32[]{:S(2)}) collective-permute-start(f32[256,384]{1,0:T(8,128)} %get-tuple-element.56), channel_id=1, source_target_pairs={{0,48},{16,0},{32,16},{48,32},{1,49},{17,1},{33,17},{49,33},{2,50}... | collective-permute-start | bytes 1179656 | tf_op jit(solution)/shard_map/ppermute | solution.py:228
  171.0 11.4 %collective-permute-start.3 = (f32[256,384]{1,0:T(8,128)}, f32[256,384]{1,0:T(8,128)S(1)}, u32[]{:S(2)}, u32[]{:S(2)}) collective-permute-start(f32[256,384]{1,0:T(8,128)} %get-tuple-element.54), channel_id=1, source_target_pairs={{0,16},{16,32},{32,48},{48,0},{1,17},{17,33},{33,49},{49,1},{2,18}... | collective-permute-start | bytes 1179656 | tf_op jit(solution)/shard_map/ppermute | solution.py:228
  174.4 17.6 %collective-permute-start.4 = (f32[256,384]{1,0:T(8,128)}, f32[256,384]{1,0:T(8,128)S(1)}, u32[]{:S(2)}, u32[]{:S(2)}) collective-permute-start(f32[256,384]{1,0:T(8,128)} %get-tuple-element.55), channel_id=1, source_target_pairs={{0,32},{16,48},{32,0},{48,16},{1,33},{17,49},{33,1},{49,17},{2,34}... | collective-permute-start | bytes 1179656 | tf_op jit(solution)/shard_map/ppermute | solution.py:228
  238.6 33.7 %copy-start.2 = (s32[4]{0:T(128)S(1)}, s32[4]{0:T(128)}, u32[]{:S(2)}) copy-start(s32[4]{0:T(128)} %length.1) | copy-start | bytes 52
  238.6 9.7 %collective-permute-start.6 = (f32[4,8,16,384]{3,2,1,0:T(8,128)}, f32[4,8,16,384]{3,2,1,0:T(8,128)S(1)}, u32[]{:S(2)}, u32[]{:S(2)}) collective-permute-start(f32[4,8,16,384]{3,2,1,0:T(8,128)} %get-tuple-element.60), channel_id=1, source_target_pairs={{0,1},{1,0},{2,3},{3,2},{4,5},{5,4},{6,7},{7,6},{8,9},{9,8},{10,11... | collective-permute-start | bytes 2359304 | tf_op jit(solution)/shard_map/ppermute | solution.py:269
Sparse Core Ops, SparseCore 0:
  9.4 45.2 all-gather.5
  72.0 47.8 all-gather.3

commit v5 on v4

--- a/solution.py
+++ b/solution.py
@@ -64,15 +64,21 @@
     high[:, half:], low[:, half:] = split(inverse_hi[...])
 
 
-def couple_kernel(position, full, high, low, placed, *shares):
-    across = len(shares)
+def couple_kernel(where, full, high, low, placed, *rest):
+    shares, total = rest[:-1], rest[-1]
+    across = len(shares) // 2
     step = pl.program_id(0)
-    result = placed[0] - product(split(full[0]), (high[...], low[...]))
+    wide = placed.shape[2]
+    total[...] = -product(split(full[0]), (high[...], low[...]))
+    window = pl.ds(pl.multiple_of(where[1] * BLK, BLK), wide)
+    total[:, window] = total[:, window] + placed[0]
+    half = total.shape[1] // 2
     for slot in range(across):
 
         @pl.when(step == (slot + across - 1) % across)
         def _():
-            shares[slot][...] = result
+            shares[slot][...] = total[:, :half]
+            shares[across + slot][...] = total[:, half:]
 
 
 def join_kernel(pieces_a, pieces_b, copies):
@@ -167,9 +173,10 @@
     )
     inverse_hi = spread(upper, "x")
     own_share = right_side.shape[1]
+    tile = jnp.minimum(lax.div(me * own_share, BLK), pivots // BLK - 2)
     place = (
-        jnp.arange(pivots, dtype=jnp.int32)[None, :]
-        == me * own_share + jnp.arange(own_share, dtype=jnp.int32)[:, None]
+        jnp.arange(2 * BLK, dtype=jnp.int32)[None, :]
+        == me * own_share - tile * BLK + jnp.arange(own_share, dtype=jnp.int32)[:, None]
     ).astype(jnp.float32)
     ordered = right_side.reshape(piv_devs, across, part, own_share).swapaxes(0, 1)
     placed = jnp.dot(
@@ -177,7 +184,7 @@
         place,
         precision=lax.Precision.HIGHEST,
         preferred_element_type=jnp.float32,
-    ).reshape(across, quarter, pivots)
+    ).reshape(across, quarter, 2 * BLK)
     inverse_high, inverse_low = pl.pallas_call(
         halve_inverse_kernel,
         grid=(across,),
@@ -192,36 +199,35 @@
         (full, inverse_high, inverse_low, placed)
     )
     few = quarter // deep
-    position = lax.axis_index("x").reshape(1)
-
-    def coupled(side):
-        block = pl.BlockSpec((quarter, half), lambda i, at: (0, 0))
-        return pl.pallas_call(
-            couple_kernel,
-            grid_spec=pltpu.PrefetchScalarGridSpec(
-                num_scalar_prefetch=1,
-                grid=(across,),
-                in_specs=[
-                    pl.BlockSpec(
-                        (1, quarter, width), lambda i, at: (lax.rem(at[0] + 1 + i, across), 0, 0)
-                    ),
-                    pl.BlockSpec((width, half), lambda i, at: (0, side)),
-                    pl.BlockSpec((width, half), lambda i, at: (0, side)),
-                    pl.BlockSpec(
-                        (1, quarter, half), lambda i, at: (lax.rem(at[0] + 1 + i, across), 0, side)
-                    ),
-                ],
-                out_specs=(block,) * across,
-            ),
-            out_shape=(jax.ShapeDtypeStruct((quarter, half), jnp.float32),) * across,
-            compiler_params=grant(60),
-            cost_estimate=pl.CostEstimate(
-                flops=6 * total * width * half,
-                bytes_accessed=4 * (total * width + width * half + 2 * total * half),
-                transcendentals=0,
-            ),
-            name="couple",
-        )(position, full, panel_high, panel_low, placed)
+    where = jnp.stack([lax.axis_index("x"), tile])
+
+    def turn(i, at):
+        return (lax.rem(at[0] + 1 + i, across), 0, 0)
+
+    shares = pl.pallas_call(
+        couple_kernel,
+        grid_spec=pltpu.PrefetchScalarGridSpec(
+            num_scalar_prefetch=1,
+            grid=(across,),
+            in_specs=[
+                pl.BlockSpec((1, quarter, width), turn),
+                pl.BlockSpec((width, pivots), lambda i, at: (0, 0)),
+                pl.BlockSpec((width, pivots), lambda i, at: (0, 0)),
+                pl.BlockSpec((1, quarter, 2 * BLK), turn),
+            ],
+            out_specs=(pl.BlockSpec((quarter, half), lambda i, at: (0, 0)),) * (2 * across),
+            scratch_shapes=[pltpu.VMEM((quarter, pivots), jnp.float32)],
+        ),
+        out_shape=(jax.ShapeDtypeStruct((quarter, half), jnp.float32),) * (2 * across),
+        compiler_params=grant(48),
+        cost_estimate=pl.CostEstimate(
+            flops=6 * total * width * pivots,
+            bytes_accessed=4 * (total * width + width * pivots + total * pivots),
+            transcendentals=0,
+        ),
+        name="couple",
+    )(where, full, panel_high, panel_low, placed)
+    shares_a, shares_b = shares[:across], shares[across:]
 
     def across_sent(shares):
         return [
@@ -233,11 +239,11 @@
         summed = shares[0] + sum(arrived[1:], arrived[0])
         return exchange(summed.reshape(deep, few, half), "z")
 
-    shares_a = coupled(0)
     arrived_a = across_sent(shares_a)
-    shares_b = coupled(1)
     arrived_b = across_sent(shares_b)
     nearer_a = nearer(shares_a, arrived_a)
+    own_b, nearer_a = lax.optimization_barrier((shares_b[0], nearer_a))
+    shares_b = (own_b, *shares_b[1:])
     nearer_b = nearer(shares_b, arrived_b)
     copies = pl.pallas_call(
         join_kernel,

time: 286 us -> 284 us (level)
  blocking collectives: 75.5 us -> 82.4 us
  Pallas kernels: 34 us -> 27.9 us
  starting transfers between devices: 45.4 us -> 49.5 us
  local copies, waits for them, and re-layouts: 11.7 us -> 8.28 us
    all_to_all x4, blocking collectives: 75.5 us -> 82.4 us  [exchange(): return lax.all_to_all(value, axes, split_axis=0, concat_axis=0, tiled=True)]
    pallas_call x2 -> x1, Pallas kernels: 15 us -> 8.63 us  [body(): pl.pallas_call(couple_kernel, grid_spec=pltpu.PrefetchScalarGridSpec(num_...]
    all_to_all x4, waiting for transfers between devices: 37.3 us -> 43.5 us  [exchange(): return lax.all_to_all(value, axes, split_axis=0, concat_axis=0, tiled=True)]
    ppermute x6, waiting for transfers between devices: 29.6 us -> 25.9 us  [across_sent(): lax.ppermute(shares[k], 'x', [(i, (i + k) % across) for i in range(across)])]
    ppermute x6, starting transfers between devices: 18.5 us -> 21.7 us  [across_sent(): lax.ppermute(shares[k], 'x', [(i, (i + k) % across) for i in range(across)])]
  transfers between devices with their start and end apart: 13 -> 13, of which waited for: 11 -> 13; matrix products, arithmetic and copies ran while one was open for 5% -> 3% of each run, Pallas kernels for 6% -> 3%
where the time goes in v5:
time: 284 us; the launch traced here: 279 us
  waiting for transfers between devices  94.1 us (33%)
  blocking collectives  82.4 us (29%)
  starting transfers between devices  49.5 us (17%)
  Pallas kernels  27.9 us (10%)
  between operations  13.6 us (5%)
  local copies, waits for them, and re-layouts  8.28 us (3%)
    all_to_all x4, blocking collectives, exchange(): return lax.all_to_all(value, axes, split_axis=0, concat_axis=0, tiled=True)  82.4 us
    all_to_all x4, waiting for transfers between devices, exchange(): return lax.all_to_all(value, axes, split_axis=0, concat_axis=0, tiled=True)  43.5 us
    ppermute x6, waiting for transfers between devices, across_sent(): lax.ppermute(shares[k], 'x', [(i, (i + k) % across) for i in range(across)])  25.9 us
    ppermute x6, starting transfers between devices, across_sent(): lax.ppermute(shares[k], 'x', [(i, (i + k) % across) for i in range(across)])  21.7 us
    all_to_all x4, starting transfers between devices, exchange(): return lax.all_to_all(value, axes, split_axis=0, concat_axis=0, tiled=True)  21 us
    all_gather x1, waiting for transfers between devices, body(): lax.all_gather(boundary.reshape(across, part, width), PIV, axis=1, tiled=...  13.3 us
    all_gather x1, waiting for transfers between devices, body(): column = lax.all_gather(ancestor_sol, 'z', axis=0, tiled=False)  8.63 us
    pallas_call x1, Pallas kernels, body(): pl.pallas_call(couple_kernel, grid_spec=pltpu.PrefetchScalarGridSpec(num_...  8.63 us
  transfers between devices with their start and end apart: 13, of which 13 were waited for; matrix products, arithmetic and copies ran while one was open for 3% of the time, Pallas kernels for 3%

profile of v5, /device:TPU:1, one launch (start us, length us, event | category | flops | bytes accessed | tf_op | source)
XLA Modules:
  0.0 278.6 jit_solution(13152004093023974037)
XLA Ops:
  8.5 4.8 %all-to-all-start.1 = ((s32[4,1,8]{2,1,0:T(1,128)}), s32[4,1,8]{2,1,0:T(1,128)S(1)}, u32[]{:S(2)}, u32[]{:S(2)}) async-start(s32[4,1,8]{2,1,0:T(1,128)} %broadcast_in_dim.7), calls=%async_computation.1 | async-start | bytes 4096 | tf_op jit(solution)/shard_map/all_to_all | solution.py:21
  18.9 4.5 %all-to-all-start = ((f32[4,384,384]{2,1,0:T(8,128)}), f32[4,384,384]{2,1,0:T(8,128)}, u32[]{:S(2)}, u32[]{:S(2)}) async-start(f32[4,384,384]{2,1,0:T(8,128)} %broadcast_in_dim.6), calls=%async_computation | async-start | bytes 4718592 | tf_op jit(solution)/shard_map/all_to_all | solution.py:21
  23.5 4.2 %halve.1 = (bf16[1024,768]{1,0:T(8,128)(2,1)}, bf16[1024,768]{1,0:T(8,128)(2,1)}) custom-call(f32[1024,768]{1,0:T(8,128)} %value.1), custom_call_target="tpu_custom_call" | custom-call | tf_op jit(solution)/shard_map/halve/pallas_call | solution.py:142
  27.8 18.3 %all-to-all-done.inverse_lo = f32[4,384,384]{2,1,0:T(8,128)} async-done(((f32[4,384,384]{2,1,0:T(8,128)}), f32[4,384,384]{2,1,0:T(8,128)}, u32[]{:S(2)}, u32[]{:S(2)}) %all-to-all-start) | async-done | bytes 2359328 | tf_op jit(solution)/shard_map/all_to_all | solution.py:21
  46.1 8.6 %all-gather.6.cloned.1.call-done = f32[512,1024]{1,0:T(8,128)} async-done(((f32[64,1024]{1,0:T(8,128)}), f32[512,1024]{1,0:T(8,128)}) %all-gather.6.cloned.1.call-update) | async-done | bytes 2097168 | tf_op jit(solution)/shard_map/all_gather | solution.py:139
  57.0 13.6 %all_to_all.44.refs_1_ = f32[4,64,1024]{2,1,0:T(8,128)S(1)} all-to-all(f32[4,64,1024]{2,1,0:T(8,128)S(1)} %pack.1), channel_id=1, replica_groups=mesh['z'=8,'x'=4,'y'=8,'c'=2] {'x'}, dimensions={0} | all-to-all | bytes 2097152 | tf_op jit(solution)/shard_map/all_to_all | solution.py:21
  73.5 4.6 %all-to-all-start.3 = ((f32[4,384,384]{2,1,0:T(8,128)}), f32[4,384,384]{2,1,0:T(8,128)}, u32[]{:S(2)}, u32[]{:S(2)}) async-start(f32[4,384,384]{2,1,0:T(8,128)} %broadcast_in_dim.8), calls=%async_computation.3 | async-start | bytes 4718592 | tf_op jit(solution)/shard_map/all_to_all | solution.py:21
  79.9 21.0 %all-to-all-done.3.inverse_hi = f32[4,384,384]{2,1,0:T(8,128)} async-done(((f32[4,384,384]{2,1,0:T(8,128)}), f32[4,384,384]{2,1,0:T(8,128)}, u32[]{:S(2)}, u32[]{:S(2)}) %all-to-all-start.3) | async-done | bytes 2359328 | tf_op jit(solution)/shard_map/all_to_all | solution.py:21
  100.9 5.3 %halve_inverse.1 = (bf16[4,768,384]{2,1,0:T(8,128)(2,1)}, bf16[4,768,384]{2,1,0:T(8,128)(2,1)}) custom-call(f32[4,384,384]{2,1,0:T(8,128)} %all-to-all-done.inverse_lo, f32[4,384,384]{2,1,0:T(8,128)} %all-to-all-done.3.inverse_hi), custom_call_target="tpu_custom_call" | custom-call | tf_op jit(solution)/shard_map/halve_inverse/pallas_call | solution.py:188
  106.2 13.3 %all-gather.4.cloned.1.call-done.full = f32[4,256,1024]{2,1,0:T(8,128)} async-done(((f32[4,16,1024]{2,1,0:T(8,128)}), f32[4,256,1024]{2,1,0:T(8,128)}) %all-gather.4.cloned.1.call-update) | async-done | bytes 4194320 | tf_op jit(solution)/shard_map/all_gather | solution.py:197
  119.5 8.6 %couple.1 = (f32[256,384]{1,0:T(8,128)S(1)}, f32[256,384]{1,0:T(8,128)S(1)}, f32[256,384]{1,0:T(8,128)S(1)}, f32[256,384]{1,0:T(8,128)S(1)}, f32[256,384]{1,0:T(...) custom-call(s32[2]{0:T(128)S(1)} %pad_add_fusion.where, ...), custom_call_target="tpu_custom_call" | custom-call | flops 4831838208 | bytes 10485760 | tf_op jit(solution)/shard_map/couple/pallas_call | solution.py:207
  128.2 3.1 %collective-permute-start = (f32[256,384]{1,0:T(8,128)S(1)}, f32[256,384]{1,0:T(8,128)S(1)}, u32[]{:S(2)}, u32[]{:S(2)}) collective-permute-start(f32[256,384]{1,0:T(8,128)S(1)} %get-tuple-element.53), channel_id=1, source_target_pairs={{0,16},{16,32},{32,48},{48,0},{1,17},{17,33},{33,49},{49,1},{2,18}... | collective-permute-start | bytes 1179656 | tf_op jit(solution)/shard_map/ppermute | solution.py:234
  131.3 4.3 %collective-permute-start.1 = (f32[256,384]{1,0:T(8,128)S(1)}, f32[256,384]{1,0:T(8,128)S(1)}, u32[]{:S(2)}, u32[]{:S(2)}) collective-permute-start(f32[256,384]{1,0:T(8,128)S(1)} %get-tuple-element.54), channel_id=1, source_target_pairs={{0,32},{16,48},{32,0},{48,16},{1,33},{17,49},{33,1},{49,17},{2,34}... | collective-permute-start | bytes 1179656 | tf_op jit(solution)/shard_map/ppermute | solution.py:234
  135.6 3.1 %collective-permute-start.2 = (f32[256,384]{1,0:T(8,128)S(1)}, f32[256,384]{1,0:T(8,128)S(1)}, u32[]{:S(2)}, u32[]{:S(2)}) collective-permute-start(f32[256,384]{1,0:T(8,128)S(1)} %get-tuple-element.55), channel_id=1, source_target_pairs={{0,48},{16,0},{32,16},{48,32},{1,49},{17,1},{33,17},{49,33},{2,50}... | collective-permute-start | bytes 1179656 | tf_op jit(solution)/shard_map/ppermute | solution.py:234
  141.7 9.3 %collective-permute-done.1 = f32[256,384]{1,0:T(8,128)S(1)} collective-permute-done((f32[256,384]{1,0:T(8,128)S(1)}, f32[256,384]{1,0:T(8,128)S(1)}, u32[]{:S(2)}, u32[]{:S(2)}) %collective-permute-start.1) | collective-permute-done | bytes 393248 | tf_op jit(solution)/shard_map/ppermute | solution.py:234
  153.2 7.1 %all-to-all-start.4 = ((f32[8,32,384]{2,1,0:T(8,128)}), f32[8,32,384]{2,1,0:T(8,128)S(1)}, u32[]{:S(2)}, u32[]{:S(2)}) async-start(f32[8,32,384]{2,1,0:T(8,128)} %bitcast.8), calls=%async_computation.4 | async-start | bytes 786432 | tf_op jit(solution)/shard_map/all_to_all | solution.py:21
  160.3 4.9 %collective-permute-start.3 = (f32[256,384]{1,0:T(8,128)}, f32[256,384]{1,0:T(8,128)S(1)}, u32[]{:S(2)}, u32[]{:S(2)}) collective-permute-start(f32[256,384]{1,0:T(8,128)} %copy-done.5), channel_id=1, source_target_pairs={{0,16},{16,32},{32,48},{48,0},{1,17},{17,33},{33,49},{49,1},{2,18}... | collective-permute-start | bytes 1179656 | tf_op jit(solution)/shard_map/ppermute | solution.py:234
  165.2 3.3 %collective-permute-start.4 = (f32[256,384]{1,0:T(8,128)}, f32[256,384]{1,0:T(8,128)S(1)}, u32[]{:S(2)}, u32[]{:S(2)}) collective-permute-start(f32[256,384]{1,0:T(8,128)} %copy-done.4), channel_id=1, source_target_pairs={{0,32},{16,48},{32,0},{48,16},{1,33},{17,49},{33,1},{49,17},{2,34}... | collective-permute-start | bytes 1179656 | tf_op jit(solution)/shard_map/ppermute | solution.py:234
  173.8 9.9 %collective-permute-done.4 = f32[256,384]{1,0:T(8,128)S(1)} collective-permute-done((f32[256,384]{1,0:T(8,128)}, f32[256,384]{1,0:T(8,128)S(1)}, u32[]{:S(2)}, u32[]{:S(2)}) %collective-permute-start.4) | collective-permute-done | bytes 393248 | tf_op jit(solution)/shard_map/ppermute | solution.py:234
  185.2 18.9 %all_to_all.45.pieces_b = f32[8,32,384]{2,1,0:T(8,128)S(1)} all-to-all(f32[8,32,384]{2,1,0:T(8,128)S(1)} %bitcast.28), channel_id=1, replica_groups=mesh['z'=8,'x'=4,'y'=8,'c'=2] {'z'}, dimensions={0} | all-to-all | bytes 786432 | tf_op jit(solution)/shard_map/all_to_all | solution.py:21
  204.2 22.6 %all_to_all.46 = f32[8,32,768]{2,1,0:T(8,128)} all-to-all(f32[8,32,768]{2,1,0:T(8,128)S(1)} %join.1), channel_id=1, replica_groups=mesh['z'=8,'x'=4,'y'=8,'c'=2] {'z'}, dimensions={0} | all-to-all | bytes 1572864 | tf_op jit(solution)/shard_map/all_to_all | solution.py:21
  226.8 6.2 %solve.1 = (f32[4,8,16,384]{3,2,1,0:T(8,128)}, f32[4,8,16,384]{3,2,1,0:T(8,128)}) custom-call(s32[1]{0:T(128)} %bitcast.2.core, f32[256,768]{1,0:T(8,128)} %bitcast.27, bf16[4,768,384]{2,1,0:T(8,128)(2,1)} %get-tuple-element.61.inverse_high, bf16[4,768,384]{2,1,0:T(8,128)(2,1)} %get-tuple-element.62.inverse_low), custom_call_target="tpu_custom_call" | custom-call | tf_op jit(solution)/shard_map/solve/pallas_call | solution.py:257
  233.0 6.7 %collective-permute-start.6 = (f32[4,8,16,384]{3,2,1,0:T(8,128)}, f32[4,8,16,384]{3,2,1,0:T(8,128)S(1)}, u32[]{:S(2)}, u32[]{:S(2)}) collective-permute-start(f32[4,8,16,384]{3,2,1,0:T(8,128)} %get-tuple-element.64), channel_id=1, source_target_pairs={{0,1},{1,0},{2,3},{3,2},{4,5},{5,4},{6,7},{7,6},{8,9},{9,8},{10,11... | collective-permute-start | bytes 2359304 | tf_op jit(solution)/shard_map/ppermute | solution.py:275
  243.0 27.3 %all_to_all.47 = f32[32,16,384]{2,1,0:T(8,128)S(1)} all-to-all(f32[32,16,384]{2,1,0:T(8,128)S(1)} %bitcast.26), channel_id=1, replica_groups=mesh['z'=8,'x'=4,'y'=8,'c'=2] {'x','y'}, dimensions={0} | all-to-all | bytes 1572864 | tf_op jit(solution)/shard_map/all_to_all | solution.py:21
  (46 shorter events, 31.1 us)
Async XLA Ops:
  6.5 48.2 %all-gather.6.cloned.1.call-start = ((), (), s32[]{:S(2)}) async-start(), calls=%async_computation.9 | async-start | bytes 2359296 | tf_op jit(solution)/shard_map/all_gather | solution.py:139
  8.5 8.9 %all-to-all-start.1 = ((s32[4,1,8]{2,1,0:T(1,128)}), s32[4,1,8]{2,1,0:T(1,128)S(1)}, u32[]{:S(2)}, u32[]{:S(2)}) async-start(s32[4,1,8]{2,1,0:T(1,128)} %broadcast_in_dim.7), calls=%async_computation.1 | async-start | bytes 4096 | tf_op jit(solution)/shard_map/all_to_all | solution.py:21
  18.9 27.1 %all-to-all-start = ((f32[4,384,384]{2,1,0:T(8,128)}), f32[4,384,384]{2,1,0:T(8,128)}, u32[]{:S(2)}, u32[]{:S(2)}) async-start(f32[4,384,384]{2,1,0:T(8,128)} %broadcast_in_dim.6), calls=%async_computation | async-start | bytes 4718592 | tf_op jit(solution)/shard_map/all_to_all | solution.py:21
  23.4 4.3 %copy-start.7 = (s32[4]{0:T(128)S(1)}, s32[4]{0:T(128)}, u32[]{:S(2)}) copy-start(s32[4]{0:T(128)} %param.12) | copy-start | bytes 52
  23.4 96.0 %all-gather.4.cloned.1.call-start = ((), (), s32[]{:S(2)}) async-start(), calls=%async_computation.8 | async-start | bytes 4456448 | tf_op jit(solution)/shard_map/all_gather | solution.py:197
  54.7 1.6 copy-start
  56.3 14.3 %copy-start.1 = (s32[8]{0:T(128)S(1)}, s32[8]{0:T(128)}, u32[]{:S(2)}) copy-start(s32[8]{0:T(128)} %refs_0_.1) | copy-start | bytes 100
  73.5 4.7 %copy-start.6 = (f32[1024,24]{0,1:T(8,128)S(1)}, f32[1024,24]{0,1:T(8,128)}, u32[]{:S(2)}) copy-start(f32[1024,24]{0,1:T(8,128)} %param.11) | copy-start | bytes 294916
  73.5 27.4 %all-to-all-start.3 = ((f32[4,384,384]{2,1,0:T(8,128)}), f32[4,384,384]{2,1,0:T(8,128)}, u32[]{:S(2)}, u32[]{:S(2)}) async-start(f32[4,384,384]{2,1,0:T(8,128)} %broadcast_in_dim.8), calls=%async_computation.3 | async-start | bytes 4718592 | tf_op jit(solution)/shard_map/all_to_all | solution.py:21
  79.9 39.6 %copy-start.3 = (bf16[1024,768]{1,0:T(8,128)(2,1)S(1)}, bf16[1024,768]{1,0:T(8,128)(2,1)}, u32[]{:S(2)}) copy-start(bf16[1024,768]{1,0:T(8,128)(2,1)} %get-tuple-element.48.high) | copy-start | bytes 4718596
  128.1 25.0 %copy-start.4 = (f32[256,384]{1,0:T(8,128)}, f32[256,384]{1,0:T(8,128)S(1)}, u32[]{:S(2)}) copy-start(f32[256,384]{1,0:T(8,128)S(1)} %get-tuple-element.59) | copy-start | bytes 1179652
  128.1 25.0 %copy-start.5 = (f32[256,384]{1,0:T(8,128)}, f32[256,384]{1,0:T(8,128)S(1)}, u32[]{:S(2)}) copy-start(f32[256,384]{1,0:T(8,128)S(1)} %get-tuple-element.58) | copy-start | bytes 1179652
  128.2 13.5 %collective-permute-start = (f32[256,384]{1,0:T(8,128)S(1)}, f32[256,384]{1,0:T(8,128)S(1)}, u32[]{:S(2)}, u32[]{:S(2)}) collective-permute-start(f32[256,384]{1,0:T(8,128)S(1)} %get-tuple-element.53), channel_id=1, source_target_pairs={{0,16},{16,32},{32,48},{48,0},{1,17},{17,33},{33,49},{49,1},{2,18}... | collective-permute-start | bytes 1179656 | tf_op jit(solution)/shard_map/ppermute | solution.py:234
  131.3 19.7 %collective-permute-start.1 = (f32[256,384]{1,0:T(8,128)S(1)}, f32[256,384]{1,0:T(8,128)S(1)}, u32[]{:S(2)}, u32[]{:S(2)}) collective-permute-start(f32[256,384]{1,0:T(8,128)S(1)} %get-tuple-element.54), channel_id=1, source_target_pairs={{0,32},{16,48},{32,0},{48,16},{1,33},{17,49},{33,1},{49,17},{2,34}... | collective-permute-start | bytes 1179656 | tf_op jit(solution)/shard_map/ppermute | solution.py:234
  135.6 16.8 %collective-permute-start.2 = (f32[256,384]{1,0:T(8,128)S(1)}, f32[256,384]{1,0:T(8,128)S(1)}, u32[]{:S(2)}, u32[]{:S(2)}) collective-permute-start(f32[256,384]{1,0:T(8,128)S(1)} %get-tuple-element.55), channel_id=1, source_target_pairs={{0,48},{16,0},{32,16},{48,32},{1,49},{17,1},{33,17},{49,33},{2,50}... | collective-permute-start | bytes 1179656 | tf_op jit(solution)/shard_map/ppermute | solution.py:234
  153.2 19.7 %all-to-all-start.4 = ((f32[8,32,384]{2,1,0:T(8,128)}), f32[8,32,384]{2,1,0:T(8,128)S(1)}, u32[]{:S(2)}, u32[]{:S(2)}) async-start(f32[8,32,384]{2,1,0:T(8,128)} %bitcast.8), calls=%async_computation.4 | async-start | bytes 786432 | tf_op jit(solution)/shard_map/all_to_all | solution.py:21
  160.3 13.5 %collective-permute-start.3 = (f32[256,384]{1,0:T(8,128)}, f32[256,384]{1,0:T(8,128)S(1)}, u32[]{:S(2)}, u32[]{:S(2)}) collective-permute-start(f32[256,384]{1,0:T(8,128)} %copy-done.5), channel_id=1, source_target_pairs={{0,16},{16,32},{32,48},{48,0},{1,17},{17,33},{33,49},{49,1},{2,18}... | collective-permute-start | bytes 1179656 | tf_op jit(solution)/shard_map/ppermute | solution.py:234
  165.2 18.5 %collective-permute-start.4 = (f32[256,384]{1,0:T(8,128)}, f32[256,384]{1,0:T(8,128)S(1)}, u32[]{:S(2)}, u32[]{:S(2)}) collective-permute-start(f32[256,384]{1,0:T(8,128)} %copy-done.4), channel_id=1, source_target_pairs={{0,32},{16,48},{32,0},{48,16},{1,33},{17,49},{33,1},{49,17},{2,34}... | collective-permute-start | bytes 1179656 | tf_op jit(solution)/shard_map/ppermute | solution.py:234
  168.5 16.6 %collective-permute-start.5 = (f32[256,384]{1,0:T(8,128)S(1)}, f32[256,384]{1,0:T(8,128)S(1)}, u32[]{:S(2)}, u32[]{:S(2)}) collective-permute-start(f32[256,384]{1,0:T(8,128)S(1)} %get-tuple-element.60), channel_id=1, source_target_pairs={{0,48},{16,0},{32,16},{48,32},{1,49},{17,1},{33,17},{49,33},{2,50}... | collective-permute-start | bytes 1179656 | tf_op jit(solution)/shard_map/ppermute | solution.py:234
  233.0 37.4 %copy-start.2 = (s32[4]{0:T(128)S(1)}, s32[4]{0:T(128)}, u32[]{:S(2)}) copy-start(s32[4]{0:T(128)} %length.1) | copy-start | bytes 52
  233.0 8.8 %collective-permute-start.6 = (f32[4,8,16,384]{3,2,1,0:T(8,128)}, f32[4,8,16,384]{3,2,1,0:T(8,128)S(1)}, u32[]{:S(2)}, u32[]{:S(2)}) collective-permute-start(f32[4,8,16,384]{3,2,1,0:T(8,128)} %get-tuple-element.64), channel_id=1, source_target_pairs={{0,1},{1,0},{2,3},{3,2},{4,5},{5,4},{6,7},{7,6},{8,9},{9,8},{10,11... | collective-permute-start | bytes 2359304 | tf_op jit(solution)/shard_map/ppermute | solution.py:275
Sparse Core Ops, SparseCore 0:
  9.4 45.2 all-gather.5
  72.1 47.3 all-gather.3

commit v6 on v5

--- a/solution.py
+++ b/solution.py
@@ -26,12 +26,18 @@
     return exchange(jnp.broadcast_to(value[None], (count, *value.shape)), axis)
 
 
-def pack_kernel(count, maps, column, sends):
-    across = maps.shape[0]
+def pack_kernel(count, maps, where, *rest):
+    pieces, sends, column = rest[:-2], rest[-2], rest[-1]
+    across, deep = maps.shape[0], column.shape[0]
+    for level, piece in enumerate(pieces[:-2]):
+        column[level if level < deep // 2 else level + 1] = piece[...]
+    upper, lower = pieces[-2:]
+    column[deep // 2, : upper.shape[0]] = upper[...]
+    column[deep // 2, upper.shape[0] :] = lower[...]
     for dest in range(across):
         for slot in range(count):
             block = maps[dest, slot]
-            level = lax.div(block, count * across)
+            level = lax.rem(lax.div(block, count * across) - where[0] + deep, deep)
             offset = pl.multiple_of(lax.rem(block, count) * BLK, BLK)
             sends[dest, :, slot * BLK : (slot + 1) * BLK] = column[level, :, pl.ds(offset, BLK)]
 
@@ -54,25 +60,40 @@
     return sum(jnp.dot(left[i], right[j], preferred_element_type=jnp.float32) for i, j in terms)
 
 
-def halve_kernel(value, high, low):
-    high[...], low[...] = split(value[...])
-
-
-def halve_inverse_kernel(inverse_lo, inverse_hi, high, low):
-    half = inverse_lo.shape[1]
-    high[:, :half], low[:, :half] = split(inverse_lo[...])
-    high[:, half:], low[:, half:] = split(inverse_hi[...])
-
-
-def couple_kernel(where, full, high, low, placed, *rest):
-    shares, total = rest[:-1], rest[-1]
-    across = len(shares) // 2
+def couple_kernel(slots, where, *rest):
+    pieces, (panel, placed) = rest[:9], rest[9:11]
+    shares, (rows, high, low, total) = rest[11 : 11 + slots], rest[11 + slots :]
     step = pl.program_id(0)
+
+    @pl.when(step == 0)
+    def _():
+        high[...], low[...] = split(panel[...])
+
+    part = pieces[0].shape[2]
+    tall = rows.shape[0] // (2 * part)
+    level, core = where[2], where[3]
+    way = 1 - 2 * core
+
+    def put(piece, entry, distance, owner):
+        at = lax.rem(level + distance + tall, tall)
+        rows[pl.ds(pl.multiple_of((at * 2 + owner) * part, part), part)] = piece[entry, 0]
+
+    own, near, far = pieces[0], pieces[1:4], pieces[4:7]
+    put(own, 0, 0, core)
+    put(own, 1, 0, 1 - core)
+    for k in range(3):
+        put(near[k], 0, -(k + 1) * way, core)
+        put(near[k], 1, -(k + 1) * way, 1 - core)
+        put(far[k], 0, (k + 1) * way, 1 - core)
+        put(far[k], 1, (k + 1) * way, core)
+    put(pieces[7], 0, tall // 2, core)
+    put(pieces[8], 0, tall // 2, 1 - core)
     wide = placed.shape[2]
-    total[...] = -product(split(full[0]), (high[...], low[...]))
+    total[...] = -product(split(rows[...]), (high[...], low[...]))
     window = pl.ds(pl.multiple_of(where[1] * BLK, BLK), wide)
     total[:, window] = total[:, window] + placed[0]
     half = total.shape[1] // 2
+    across = slots // 2
     for slot in range(across):
 
         @pl.when(step == (slot + across - 1) % across)
@@ -89,13 +110,15 @@
         copies[level, :, cut:] = second
 
 
-def solve_kernel(core, reduced, inverse_high, inverse_low, kept, other, high, low):
+def solve_kernel(core, reduced, inverse_lo, inverse_hi, kept, other, high, low):
     @pl.when(pl.program_id(0) == 0)
     def _():
         high[...], low[...] = split(reduced[...])
 
     _, tall, part, span = kept.shape
-    result = product((high[...], low[...]), (inverse_high[0], inverse_low[0]))
+    cut = inverse_lo.shape[1]
+    result = product((high[:, :cut], low[:, :cut]), split(inverse_lo[0]))
+    result = result + product((high[:, cut:], low[:, cut:]), split(inverse_hi[0]))
     result = result.reshape(tall, 2, part, span)
     first, second = result[:, 0], result[:, 1]
     mine = core[0] == 0
@@ -133,32 +156,34 @@
     quarter = total // across
     me = lax.axis_index(ROWS)
 
-    core = lax.axis_index("c").reshape(1)
+    half = pivots // 2
+    cut = pivots // 96 * 40
+    core = lax.axis_index("c")
     first = child_start - me * span
+
+    def ring(value, axis, hops):
+        length = lax.axis_size(axis)
+        return lax.ppermute(value, axis, [(i, (i + hops) % length) for i in range(length)])
+
     maps = spread(front_map, "x").reshape(across, count)
-    column = lax.all_gather(ancestor_sol, "z", axis=0, tiled=False)
-    half = pivots // 2
-    inverse_lo = spread(inverse_factor[:half], "x")
-    panel_high, panel_low = pl.pallas_call(
-        halve_kernel,
-        grid=(4,),
-        out_shape=(jax.ShapeDtypeStruct((width, pivots), jnp.bfloat16),) * 2,
-        in_specs=[pl.BlockSpec((width // 4, pivots), lambda i: (i, 0))],
-        out_specs=(pl.BlockSpec((width // 4, pivots), lambda i: (i, 0)),) * 2,
-        compiler_params=grant(60),
-        name="halve",
-    )(lower_panel)
-    column, inverse_lo, maps, panel_high, panel_low, core, first = lax.optimization_barrier(
-        (column, inverse_lo, maps, panel_high, panel_low, core, first)
-    )
+    down_2, up_2 = ring(ancestor_sol, "z", 2), ring(ancestor_sol, "z", -2)
+    down_1, up_1 = ring(ancestor_sol, "z", 1), ring(ancestor_sol, "z", -1)
+    inverse_lo = spread(inverse_factor[:cut], "x")
+    mid = srcs // 2
+    upper, lower = ring(down_2[:mid], "z", 2), ring(up_2[mid:], "z", -2)
+    down_3, up_3 = ring(down_2, "z", 1), ring(up_2, "z", -1)
+    column = (ancestor_sol, up_1, up_2, up_3, down_3, down_2, down_1, upper, lower)
+    column, maps, first = lax.optimization_barrier((column, maps, first))
     sends = pl.pallas_call(
         lambda *refs: pack_kernel(count, *refs),
         out_shape=jax.ShapeDtypeStruct((across, srcs, width), jnp.float32),
-        in_specs=[SMEM, VMEM],
+        in_specs=[SMEM, SMEM] + [VMEM] * len(column),
         out_specs=VMEM,
+        scratch_shapes=[pltpu.VMEM((deep, srcs, width), jnp.float32)],
         compiler_params=grant(12),
         name="pack",
-    )(maps, column)
+    )(maps, lax.axis_index("z").reshape(1), *column)
+    sends, inverse_lo = lax.optimization_barrier((sends, inverse_lo))
     arrived = exchange(sends, "x")
     boundary = pl.pallas_call(
         lambda *refs: pick_kernel(count, *refs),
@@ -168,10 +193,26 @@
         compiler_params=grant(8),
         name="pick",
     )(front_map, arrived)
-    boundary, upper, right_side = lax.optimization_barrier(
-        (boundary, inverse_factor[half:], right_side)
+    boundary, rest, right_side = lax.optimization_barrier(
+        (boundary, inverse_factor[cut:], right_side)
     )
-    inverse_hi = spread(upper, "x")
+
+    def swap(value):
+        return lax.ppermute(value, "c", [(0, 1), (1, 0)])
+
+    def apart(value, hops):
+        pairs = [
+            (2 * y + c, 2 * ((y + (hops, -hops)[c]) % tall) + c)
+            for y in range(tall)
+            for c in range(cores)
+        ]
+        return lax.ppermute(value, PIV, pairs)
+
+    chip = jnp.stack([boundary, swap(boundary)])
+    near_2, near_1 = apart(chip, 2), apart(chip, 1)
+    inverse_hi = spread(rest, "x")
+    near_4, near_3 = apart(near_2[0], 2), apart(near_2, 1)
+    far_2, far_1, far_4, far_3 = swap(near_2), swap(near_1), swap(near_4), swap(near_3)
     own_share = right_side.shape[1]
     tile = jnp.minimum(lax.div(me * own_share, BLK), pivots // BLK - 2)
     place = (
@@ -185,38 +226,37 @@
         precision=lax.Precision.HIGHEST,
         preferred_element_type=jnp.float32,
     ).reshape(across, quarter, 2 * BLK)
-    inverse_high, inverse_low = pl.pallas_call(
-        halve_inverse_kernel,
-        grid=(across,),
-        out_shape=(jax.ShapeDtypeStruct((across, pivots, span), jnp.bfloat16),) * 2,
-        in_specs=[pl.BlockSpec((1, half, span), lambda i: (i, 0, 0))] * 2,
-        out_specs=(pl.BlockSpec((1, pivots, span), lambda i: (i, 0, 0)),) * 2,
-        compiler_params=grant(60),
-        name="halve_inverse",
-    )(inverse_lo.reshape(across, half, span), inverse_hi.reshape(across, half, span))
-    full = lax.all_gather(boundary.reshape(across, part, width), PIV, axis=1, tiled=True)
-    full, inverse_high, inverse_low, placed = lax.optimization_barrier(
-        (full, inverse_high, inverse_low, placed)
-    )
+    pieces = (chip, near_1, near_2, near_3, far_1, far_2, far_3, near_4, far_4)
+    pieces, inverse_hi, placed = lax.optimization_barrier((pieces, inverse_hi, placed))
+    pieces = [piece.reshape(-1, across, part, width) for piece in pieces]
     few = quarter // deep
-    where = jnp.stack([lax.axis_index("x"), tile])
+    where = jnp.stack([lax.axis_index("x"), tile, lax.axis_index("y"), core])
 
     def turn(i, at):
         return (lax.rem(at[0] + 1 + i, across), 0, 0)
 
     shares = pl.pallas_call(
-        couple_kernel,
+        lambda *refs: couple_kernel(2 * across, *refs),
         grid_spec=pltpu.PrefetchScalarGridSpec(
             num_scalar_prefetch=1,
             grid=(across,),
             in_specs=[
-                pl.BlockSpec((1, quarter, width), turn),
-                pl.BlockSpec((width, pivots), lambda i, at: (0, 0)),
+                pl.BlockSpec(
+                    (piece.shape[0], 1, part, width), lambda i, at: (0, turn(i, at)[0], 0, 0)
+                )
+                for piece in pieces
+            ]
+            + [
                 pl.BlockSpec((width, pivots), lambda i, at: (0, 0)),
                 pl.BlockSpec((1, quarter, 2 * BLK), turn),
             ],
             out_specs=(pl.BlockSpec((quarter, half), lambda i, at: (0, 0)),) * (2 * across),
-            scratch_shapes=[pltpu.VMEM((quarter, pivots), jnp.float32)],
+            scratch_shapes=[
+                pltpu.VMEM((quarter, width), jnp.float32),
+                pltpu.VMEM((width, pivots), jnp.bfloat16),
+                pltpu.VMEM((width, pivots), jnp.bfloat16),
+                pltpu.VMEM((quarter, pivots), jnp.float32),
+            ],
         ),
         out_shape=(jax.ShapeDtypeStruct((quarter, half), jnp.float32),) * (2 * across),
         compiler_params=grant(48),
@@ -226,7 +266,7 @@
             transcendentals=0,
         ),
         name="couple",
-    )(where, full, panel_high, panel_low, placed)
+    )(where, *pieces, lower_panel, placed)
     shares_a, shares_b = shares[:across], shares[across:]
 
     def across_sent(shares):
@@ -261,8 +301,8 @@
         in_specs=[
             SMEM,
             pl.BlockSpec((quarter, pivots), lambda i: (0, 0)),
-            pl.BlockSpec((1, pivots, span), lambda i: (i, 0, 0)),
-            pl.BlockSpec((1, pivots, span), lambda i: (i, 0, 0)),
+            pl.BlockSpec((1, cut, span), lambda i: (i, 0, 0)),
+            pl.BlockSpec((1, pivots - cut, span), lambda i: (i, 0, 0)),
         ],
         out_specs=(pl.BlockSpec((1, tall, part, span), lambda i: (i, 0, 0, 0)),) * 2,
         scratch_shapes=[
@@ -271,9 +311,14 @@
         ],
         compiler_params=grant(60),
         name="solve",
-    )(core, reduced, inverse_high, inverse_low)
-    kept = kept + lax.ppermute(other, "c", [(0, 1), (1, 0)])
-    pieces = exchange(kept.reshape(across * tall, part, span), ("x", "y"))
+    )(
+        core.reshape(1),
+        reduced,
+        inverse_lo.reshape(across, cut, span),
+        inverse_hi.reshape(across, pivots - cut, span),
+    )
+    kept = kept + swap(other)
+    arrived = exchange(kept.reshape(across * tall, part, span), ("x", "y"))
     return pl.pallas_call(
         child_kernel,
         out_shape=jax.ShapeDtypeStruct((srcs, child_len.shape[0] * BLK), jnp.float32),
@@ -282,7 +327,7 @@
         scratch_shapes=[pltpu.VMEM((srcs, span + BLK), jnp.float32)],
         compiler_params=grant(8),
         name="children",
-    )(first, child_len, pieces.reshape(across, tall, part, span))
+    )(first, child_len, arrived.reshape(across, tall, part, span))
 
 
 def solution(mesh):

time: 284 us -> 294 us (1.035)
  starting transfers between devices: 49.5 us -> 122 us
  waiting for transfers between devices: 94.1 us -> 59.6 us
  between operations: 13.6 us -> 0.44 us
  blocking collectives: 82.4 us -> 71.8 us
  Pallas kernels: 27.9 us -> 20.7 us
    ppermute x1 -> x18, starting transfers between devices: 6.72 us -> 77.9 us  [the longest x8 35.5 us: ring(): lax.ppermute(value, axis, [(i, (i + hops) % length) for i in range(length)])]
    all_to_all x4 -> x5, waiting for transfers between devices: 43.5 us -> 15.4 us  [exchange(): return lax.all_to_all(value, axes, split_axis=0, concat_axis=0, tiled=True)]
    all_gather x2 -> x0, waiting for transfers between devices: 21.9 us -> none  [the longest x1 13.3 us: body(): lax.all_gather(boundary.reshape(across, part, width), PIV, axis=1, tiled=...]
    ppermute x1 -> x18, waiting for transfers between devices: 2.1 us -> 19.6 us  [the longest x4 11.1 us: apart(): return lax.ppermute(value, PIV, pairs)]
    all_to_all x4 -> x3, blocking collectives: 82.4 us -> 71.8 us  [exchange(): return lax.all_to_all(value, axes, split_axis=0, concat_axis=0, tiled=True)]
    pallas_call x3 -> x1, Pallas kernels: 18.2 us -> 10.1 us  [body(): pl.pallas_call(lambda *refs: couple_kernel(2 * across, *refs), grid_spec=...]
    all_to_all x4 -> x5, starting transfers between devices: 21 us -> 22.4 us  [exchange(): return lax.all_to_all(value, axes, split_axis=0, concat_axis=0, tiled=True)]
  transfers between devices with their start and end apart: 13 -> 29, of which waited for: 13 -> 14; matrix products, arithmetic and copies ran while one was open for 3% -> 2% of each run, Pallas kernels for 3% -> 1%
where the time goes in v6:
time: 294 us; the launch traced here: 289 us
  starting transfers between devices  122 us (41%)
  blocking collectives  71.8 us (24%)
  waiting for transfers between devices  59.6 us (20%)
  Pallas kernels  20.7 us (7%)
  local copies, waits for them, and re-layouts  10.2 us (3%)
    all_to_all x3, blocking collectives, exchange(): return lax.all_to_all(value, axes, split_axis=0, concat_axis=0, tiled=True)  71.8 us
    ppermute x8, starting transfers between devices, ring(): lax.ppermute(value, axis, [(i, (i + hops) % length) for i in range(length)])  35.5 us
    ppermute x6, starting transfers between devices, swap(): return lax.ppermute(value, 'c', [(0, 1), (1, 0)])  25.3 us
    ppermute x6, waiting for transfers between devices, across_sent(): lax.ppermute(shares[k], 'x', [(i, (i + k) % across) for i in range(across)])  24.5 us
    all_to_all x5, starting transfers between devices, exchange(): return lax.all_to_all(value, axes, split_axis=0, concat_axis=0, tiled=True)  22.4 us
    ppermute x6, starting transfers between devices, across_sent(): lax.ppermute(shares[k], 'x', [(i, (i + k) % across) for i in range(across)])  21.9 us
    ppermute x4, starting transfers between devices, apart(): return lax.ppermute(value, PIV, pairs)  17.2 us
    all_to_all x5, waiting for transfers between devices, exchange(): return lax.all_to_all(value, axes, split_axis=0, concat_axis=0, tiled=True)  15.4 us
  transfers between devices with their start and end apart: 29, of which 14 were waited for; matrix products, arithmetic and copies ran while one was open for 2% of the time, Pallas kernels for 1%

profile of v6, /device:TPU:1, one launch (start us, length us, event | category | flops | bytes accessed | tf_op | source)
XLA Modules:
  0.0 288.8 jit_solution(4886583111866855333)
XLA Ops:
  1.2 4.8 %all-to-all-start = ((s32[4,1,8]{2,1,0:T(1,128)}), s32[4,1,8]{2,1,0:T(1,128)S(1)}, u32[]{:S(2)}, u32[]{:S(2)}) async-start(s32[4,1,8]{2,1,0:T(1,128)} %broadcast_in_dim.6), calls=%async_computation | async-start | bytes 4096 | tf_op jit(solution)/shard_map/all_to_all | solution.py:21
  11.6 4.6 %all-to-all-start.1 = ((f32[4,320,384]{2,1,0:T(8,128)}), f32[4,320,384]{2,1,0:T(8,128)}, u32[]{:S(2)}, u32[]{:S(2)}) async-start(f32[4,320,384]{2,1,0:T(8,128)} %broadcast_in_dim.7), calls=%async_computation.1 | async-start | bytes 3932160 | tf_op jit(solution)/shard_map/all_to_all | solution.py:21
  16.1 5.8 %collective-permute-start.3 = (f32[64,1024]{1,0:T(8,128)S(1)}, f32[64,1024]{1,0:T(8,128)S(1)}, u32[]{:S(2)}, u32[]{:S(2)}) collective-permute-start(f32[64,1024]{1,0:T(8,128)S(1)} %copy-done), channel_id=1, source_target_pairs={{0,128},{64,192},{128,256},{192,320},{256,384},{320,448},{384,0},{... | collective-permute-start | bytes 786440 | tf_op jit(solution)/shard_map/ppermute | solution.py:166
  22.0 6.8 %collective-permute-start.1 = (f32[64,1024]{1,0:T(8,128)S(1)}, f32[64,1024]{1,0:T(8,128)S(1)}, u32[]{:S(2)}, u32[]{:S(2)}) collective-permute-start(f32[64,1024]{1,0:T(8,128)S(1)} %copy-done), channel_id=1, source_target_pairs={{0,384},{64,448},{128,0},{192,64},{256,128},{320,192},{384,256},{4... | collective-permute-start | bytes 786440 | tf_op jit(solution)/shard_map/ppermute | solution.py:166
  35.0 7.4 %collective-permute-start.4 = (f32[64,1024]{1,0:T(8,128)S(1)}, f32[64,1024]{1,0:T(8,128)S(1)}, u32[]{:S(2)}, u32[]{:S(2)}) collective-permute-start(f32[64,1024]{1,0:T(8,128)S(1)} %collective-permute-done.3.refs_7_), channel_id=1, source_target_pairs={{0,64},{64,128},{128,192},{192,256},{256,320},{320,384},{384,448},... | collective-permute-start | bytes 786440 | tf_op jit(solution)/shard_map/ppermute | solution.py:166
  47.5 4.3 %collective-permute-start.7 = (f32[32,1024]{1,0:T(8,128)S(1)}, f32[32,1024]{1,0:T(8,128)S(1)}, u32[]{:S(2)}, u32[]{:S(2)}) collective-permute-start(f32[32,1024]{1,0:T(8,128)S(1)} %slice.21), channel_id=1, source_target_pairs={{0,384},{64,448},{128,0},{192,64},{256,128},{320,192},{384,256},{4... | collective-permute-start | bytes 393224 | tf_op jit(solution)/shard_map/ppermute | solution.py:166
  52.7 4.3 %collective-permute-done.7.refs_10_ = f32[32,1024]{1,0:T(8,128)S(1)} collective-permute-done((f32[32,1024]{1,0:T(8,128)S(1)}, f32[32,1024]{1,0:T(8,128)S(1)}, u32[]{:S(2)}, u32[]{:S(2)}) %collective-permute-start.7) | collective-permute-done | bytes 131104 | tf_op jit(solution)/shard_map/ppermute | solution.py:166
  58.9 4.3 %all-to-all-start.2 = ((f32[4,64,1024]{2,1,0:T(8,128)}), f32[4,64,1024]{2,1,0:T(8,128)S(1)}, u32[]{:S(2)}, u32[]{:S(2)}) async-start(f32[4,64,1024]{2,1,0:T(8,128)} %pack.1), calls=%async_computation.2 | async-start | bytes 2097152 | tf_op jit(solution)/shard_map/all_to_all | solution.py:21
  63.3 9.8 %all-to-all-done.2.refs_1_ = f32[4,64,1024]{2,1,0:T(8,128)S(1)} async-done(((f32[4,64,1024]{2,1,0:T(8,128)}), f32[4,64,1024]{2,1,0:T(8,128)S(1)}, u32[]{:S(2)}, u32[]{:S(2)}) %all-to-all-start.2) | async-done | bytes 1048608 | tf_op jit(solution)/shard_map/all_to_all | solution.py:21
  75.4 4.7 %all-to-all-start.3 = ((f32[4,448,384]{2,1,0:T(8,128)}), f32[4,448,384]{2,1,0:T(8,128)}, u32[]{:S(2)}, u32[]{:S(2)}) async-start(f32[4,448,384]{2,1,0:T(8,128)} %broadcast_in_dim.8), calls=%async_computation.3 | async-start | bytes 5505024 | tf_op jit(solution)/shard_map/all_to_all | solution.py:21
  80.1 8.2 %collective-permute-start.8 = (f32[64,1024]{1,0:T(8,128)S(1)}, f32[64,1024]{1,0:T(8,128)S(1)}, u32[]{:S(2)}, u32[]{:S(2)}) collective-permute-start(f32[64,1024]{1,0:T(8,128)S(1)} %pick.1), channel_id=1, source_target_pairs={{0,1},{1,0},{2,3},{3,2},{4,5},{5,4},{6,7},{7,6},{8,9},{9,8},{10,11... | collective-permute-start | bytes 786440 | tf_op jit(solution)/shard_map/ppermute | solution.py:201
  89.5 6.0 %collective-permute-start.10 = (f32[2,64,1024]{2,1,0:T(8,128)S(1)}, f32[2,64,1024]{2,1,0:T(8,128)S(1)}, u32[]{:S(2)}, u32[]{:S(2)}) collective-permute-start(f32[2,64,1024]{2,1,0:T(8,128)S(1)} %pad_maximum_fusion), channel_id=1, source_target_pairs={{0,4},{1,13},{2,6},{3,15},{4,8},{5,1},{6,10},{7,3},{8,12},{9,5},{1... | collective-permute-start | bytes 1572872 | tf_op jit(solution)/shard_map/ppermute | solution.py:209
  98.4 8.7 %collective-permute-done.10 = f32[2,64,1024]{2,1,0:T(8,128)S(1)} collective-permute-done((f32[2,64,1024]{2,1,0:T(8,128)S(1)}, f32[2,64,1024]{2,1,0:T(8,128)S(1)}, u32[]{:S(2)}, u32[]{:S(2)}) %collective-permute-start.10) | collective-permute-done | bytes 524320 | tf_op jit(solution)/shard_map/ppermute | solution.py:209
  107.2 4.5 %collective-permute-start.11 = (f32[2,64,1024]{2,1,0:T(8,128)S(1)}, f32[2,64,1024]{2,1,0:T(8,128)S(1)}, u32[]{:S(2)}, u32[]{:S(2)}) collective-permute-start(f32[2,64,1024]{2,1,0:T(8,128)S(1)} %collective-permute-done.10), channel_id=1, source_target_pairs={{0,2},{1,15},{2,4},{3,1},{4,6},{5,3},{6,8},{7,5},{8,10},{9,7},{10,... | collective-permute-start | bytes 1572872 | tf_op jit(solution)/shard_map/ppermute | solution.py:209
  134.7 10.1 %couple.1 = (f32[256,384]{1,0:T(8,128)S(1)}, f32[256,384]{1,0:T(8,128)S(1)}, f32[256,384]{1,0:T(8,128)S(1)}, f32[256,384]{1,0:T(8,128)S(1)}, f32[256,384]{1,0:T(...) custom-call(s32[4]{0:T(128)S(1)} %pad_add_fusion.refs_0_, ...), custom_call_target="tpu_custom_call" | custom-call | flops 4831838208 | bytes 10485760 | tf_op jit(solution)/shard_map/couple/pallas_call | solution.py:238
  148.4 4.3 %collective-permute-start.18 = (f32[256,384]{1,0:T(8,128)S(1)}, f32[256,384]{1,0:T(8,128)S(1)}, u32[]{:S(2)}, u32[]{:S(2)}) collective-permute-start(f32[256,384]{1,0:T(8,128)S(1)} %get-tuple-element.72), channel_id=1, source_target_pairs={{0,32},{16,48},{32,0},{48,16},{1,33},{17,49},{33,1},{49,17},{2,34}... | collective-permute-start | bytes 1179656 | tf_op jit(solution)/shard_map/ppermute | solution.py:274
  159.1 9.4 %collective-permute-done.18 = f32[256,384]{1,0:T(8,128)S(1)} collective-permute-done((f32[256,384]{1,0:T(8,128)S(1)}, f32[256,384]{1,0:T(8,128)S(1)}, u32[]{:S(2)}, u32[]{:S(2)}) %collective-permute-start.18) | collective-permute-done | bytes 393248 | tf_op jit(solution)/shard_map/ppermute | solution.py:274
  174.6 4.6 %collective-permute-start.20 = (f32[256,384]{1,0:T(8,128)}, f32[256,384]{1,0:T(8,128)S(1)}, u32[]{:S(2)}, u32[]{:S(2)}) collective-permute-start(f32[256,384]{1,0:T(8,128)} %copy-done.3), channel_id=1, source_target_pairs={{0,16},{16,32},{32,48},{48,0},{1,17},{17,33},{33,49},{49,1},{2,18}... | collective-permute-start | bytes 1179656 | tf_op jit(solution)/shard_map/ppermute | solution.py:274
  188.1 9.3 %collective-permute-done.21 = f32[256,384]{1,0:T(8,128)S(1)} collective-permute-done((f32[256,384]{1,0:T(8,128)S(1)}, f32[256,384]{1,0:T(8,128)S(1)}, u32[]{:S(2)}, u32[]{:S(2)}) %collective-permute-start.21) | collective-permute-done | bytes 393248 | tf_op jit(solution)/shard_map/ppermute | solution.py:274
  198.8 18.9 %all_to_all.44.pieces_b = f32[8,32,384]{2,1,0:T(8,128)S(1)} all-to-all(f32[8,32,384]{2,1,0:T(8,128)S(1)} %bitcast.47), channel_id=1, replica_groups=mesh['z'=8,'x'=4,'y'=8,'c'=2] {'z'}, dimensions={0} | all-to-all | bytes 786432 | tf_op jit(solution)/shard_map/all_to_all | solution.py:21
  217.8 22.6 %all_to_all.45 = f32[8,32,768]{2,1,0:T(8,128)} all-to-all(f32[8,32,768]{2,1,0:T(8,128)S(1)} %join.1), channel_id=1, replica_groups=mesh['z'=8,'x'=4,'y'=8,'c'=2] {'z'}, dimensions={0} | all-to-all | bytes 1572864 | tf_op jit(solution)/shard_map/all_to_all | solution.py:21
  240.3 6.7 %solve.1 = (f32[4,8,16,384]{3,2,1,0:T(8,128)}, f32[4,8,16,384]{3,2,1,0:T(8,128)}) custom-call(s32[1]{0:T(128)} %bitcast.1.core, f32[256,768]{1,0:T(8,128)} %bitcast.46, f32[4,320,384]{2,1,0:T(8,128)} %all-to-all-done.1.inverse_lo, f32[4,448,384]{2,1,0:T(8,128)} %all-to-all-done.3.inverse_hi), custom_call_target="tpu_custom_call" | custom-call | tf_op jit(solution)/shard_map/solve/pallas_call | solution.py:297
  247.1 6.7 %collective-permute-start.23 = (f32[4,8,16,384]{3,2,1,0:T(8,128)}, f32[4,8,16,384]{3,2,1,0:T(8,128)S(1)}, u32[]{:S(2)}, u32[]{:S(2)}) collective-permute-start(f32[4,8,16,384]{3,2,1,0:T(8,128)} %get-tuple-element.82), channel_id=1, source_target_pairs={{0,1},{1,0},{2,3},{3,2},{4,5},{5,4},{6,7},{7,6},{8,9},{9,8},{10,11... | collective-permute-start | bytes 2359304 | tf_op jit(solution)/shard_map/ppermute | solution.py:201
  257.1 30.3 %all_to_all.46 = f32[32,16,384]{2,1,0:T(8,128)S(1)} all-to-all(f32[32,16,384]{2,1,0:T(8,128)S(1)} %bitcast.45), channel_id=1, replica_groups=mesh['z'=8,'x'=4,'y'=8,'c'=2] {'x','y'}, dimensions={0} | all-to-all | bytes 1572864 | tf_op jit(solution)/shard_map/all_to_all | solution.py:21
  (79 shorter events, 81.2 us)
Async XLA Ops:
  11.6 47.4 %all-to-all-start.1 = ((f32[4,320,384]{2,1,0:T(8,128)}), f32[4,320,384]{2,1,0:T(8,128)}, u32[]{:S(2)}, u32[]{:S(2)}) async-start(f32[4,320,384]{2,1,0:T(8,128)} %broadcast_in_dim.7), calls=%async_computation.1 | async-start | bytes 3932160 | tf_op jit(solution)/shard_map/all_to_all | solution.py:21
  16.1 18.8 %collective-permute-start.3 = (f32[64,1024]{1,0:T(8,128)S(1)}, f32[64,1024]{1,0:T(8,128)S(1)}, u32[]{:S(2)}, u32[]{:S(2)}) collective-permute-start(f32[64,1024]{1,0:T(8,128)S(1)} %copy-done), channel_id=1, source_target_pairs={{0,128},{64,192},{128,256},{192,320},{256,384},{320,448},{384,0},{... | collective-permute-start | bytes 786440 | tf_op jit(solution)/shard_map/ppermute | solution.py:166
  22.0 20.4 %collective-permute-start.1 = (f32[64,1024]{1,0:T(8,128)S(1)}, f32[64,1024]{1,0:T(8,128)S(1)}, u32[]{:S(2)}, u32[]{:S(2)}) collective-permute-start(f32[64,1024]{1,0:T(8,128)S(1)} %copy-done), channel_id=1, source_target_pairs={{0,384},{64,448},{128,0},{192,64},{256,128},{320,192},{384,256},{4... | collective-permute-start | bytes 786440 | tf_op jit(solution)/shard_map/ppermute | solution.py:166
  28.7 18.7 %collective-permute-start = (f32[64,1024]{1,0:T(8,128)S(1)}, f32[64,1024]{1,0:T(8,128)S(1)}, u32[]{:S(2)}, u32[]{:S(2)}) collective-permute-start(f32[64,1024]{1,0:T(8,128)S(1)} %copy-done), channel_id=1, source_target_pairs={{0,448},{64,0},{128,64},{192,128},{256,192},{320,256},{384,320},{4... | collective-permute-start | bytes 786440 | tf_op jit(solution)/shard_map/ppermute | solution.py:166
  33.0 18.8 %collective-permute-start.5 = (f32[64,1024]{1,0:T(8,128)S(1)}, f32[64,1024]{1,0:T(8,128)S(1)}, u32[]{:S(2)}, u32[]{:S(2)}) collective-permute-start(f32[64,1024]{1,0:T(8,128)S(1)} %copy-done), channel_id=1, source_target_pairs={{0,64},{64,128},{128,192},{192,256},{256,320},{320,384},{384,448},... | collective-permute-start | bytes 786440 | tf_op jit(solution)/shard_map/ppermute | solution.py:166
  35.0 22.1 %collective-permute-start.4 = (f32[64,1024]{1,0:T(8,128)S(1)}, f32[64,1024]{1,0:T(8,128)S(1)}, u32[]{:S(2)}, u32[]{:S(2)}) collective-permute-start(f32[64,1024]{1,0:T(8,128)S(1)} %collective-permute-done.3.refs_7_), channel_id=1, source_target_pairs={{0,64},{64,128},{128,192},{192,256},{256,320},{320,384},{384,448},... | collective-permute-start | bytes 786440 | tf_op jit(solution)/shard_map/ppermute | solution.py:166
  42.4 14.7 %collective-permute-start.2 = (f32[64,1024]{1,0:T(8,128)S(1)}, f32[64,1024]{1,0:T(8,128)S(1)}, u32[]{:S(2)}, u32[]{:S(2)}) collective-permute-start(f32[64,1024]{1,0:T(8,128)S(1)} %collective-permute-done.1.refs_4_), channel_id=1, source_target_pairs={{0,448},{64,0},{128,64},{192,128},{256,192},{320,256},{384,320},{4... | collective-permute-start | bytes 786440 | tf_op jit(solution)/shard_map/ppermute | solution.py:166
  47.5 9.6 %collective-permute-start.7 = (f32[32,1024]{1,0:T(8,128)S(1)}, f32[32,1024]{1,0:T(8,128)S(1)}, u32[]{:S(2)}, u32[]{:S(2)}) collective-permute-start(f32[32,1024]{1,0:T(8,128)S(1)} %slice.21), channel_id=1, source_target_pairs={{0,384},{64,448},{128,0},{192,64},{256,128},{320,192},{384,256},{4... | collective-permute-start | bytes 393224 | tf_op jit(solution)/shard_map/ppermute | solution.py:166
  58.9 14.1 %all-to-all-start.2 = ((f32[4,64,1024]{2,1,0:T(8,128)}), f32[4,64,1024]{2,1,0:T(8,128)S(1)}, u32[]{:S(2)}, u32[]{:S(2)}) async-start(f32[4,64,1024]{2,1,0:T(8,128)} %pack.1), calls=%async_computation.2 | async-start | bytes 2097152 | tf_op jit(solution)/shard_map/all_to_all | solution.py:21
  75.4 58.4 %all-to-all-start.3 = ((f32[4,448,384]{2,1,0:T(8,128)}), f32[4,448,384]{2,1,0:T(8,128)}, u32[]{:S(2)}, u32[]{:S(2)}) async-start(f32[4,448,384]{2,1,0:T(8,128)} %broadcast_in_dim.8), calls=%async_computation.3 | async-start | bytes 5505024 | tf_op jit(solution)/shard_map/all_to_all | solution.py:21
  89.5 17.7 %collective-permute-start.10 = (f32[2,64,1024]{2,1,0:T(8,128)S(1)}, f32[2,64,1024]{2,1,0:T(8,128)S(1)}, u32[]{:S(2)}, u32[]{:S(2)}) collective-permute-start(f32[2,64,1024]{2,1,0:T(8,128)S(1)} %pad_maximum_fusion), channel_id=1, source_target_pairs={{0,4},{1,13},{2,6},{3,15},{4,8},{5,1},{6,10},{7,3},{8,12},{9,5},{1... | collective-permute-start | bytes 1572872 | tf_op jit(solution)/shard_map/ppermute | solution.py:209
  95.4 22.0 %collective-permute-start.9 = (f32[2,64,1024]{2,1,0:T(8,128)S(1)}, f32[2,64,1024]{2,1,0:T(8,128)S(1)}, u32[]{:S(2)}, u32[]{:S(2)}) collective-permute-start(f32[2,64,1024]{2,1,0:T(8,128)S(1)} %pad_maximum_fusion), channel_id=1, source_target_pairs={{0,2},{1,15},{2,4},{3,1},{4,6},{5,3},{6,8},{7,5},{8,10},{9,7},{10,... | collective-permute-start | bytes 1572872 | tf_op jit(solution)/shard_map/ppermute | solution.py:209
  107.2 12.6 %collective-permute-start.11 = (f32[2,64,1024]{2,1,0:T(8,128)S(1)}, f32[2,64,1024]{2,1,0:T(8,128)S(1)}, u32[]{:S(2)}, u32[]{:S(2)}) collective-permute-start(f32[2,64,1024]{2,1,0:T(8,128)S(1)} %collective-permute-done.10), channel_id=1, source_target_pairs={{0,2},{1,15},{2,4},{3,1},{4,6},{5,3},{6,8},{7,5},{8,10},{9,7},{10,... | collective-permute-start | bytes 1572872 | tf_op jit(solution)/shard_map/ppermute | solution.py:209
  111.6 12.8 %collective-permute-start.15 = (f32[64,1024]{1,0:T(8,128)S(1)}, f32[64,1024]{1,0:T(8,128)S(1)}, u32[]{:S(2)}, u32[]{:S(2)}) collective-permute-start(f32[64,1024]{1,0:T(8,128)S(1)} %slice_bitcast_fusion), channel_id=1, source_target_pairs={{0,4},{1,13},{2,6},{3,15},{4,8},{5,1},{6,10},{7,3},{8,12},{9,5},{1... | collective-permute-start | bytes 786440 | tf_op jit(solution)/shard_map/ppermute | solution.py:209
  115.4 18.3 %collective-permute-start.13 = (f32[2,64,1024]{2,1,0:T(8,128)S(1)}, f32[2,64,1024]{2,1,0:T(8,128)}, u32[]{:S(2)}, u32[]{:S(2)}) collective-permute-start(f32[2,64,1024]{2,1,0:T(8,128)S(1)} %collective-permute-done.10), channel_id=1, source_target_pairs={{0,1},{1,0},{2,3},{3,2},{4,5},{5,4},{6,7},{7,6},{8,9},{9,8},{10,11... | collective-permute-start | bytes 1572872 | tf_op jit(solution)/shard_map/ppermute | solution.py:201
  117.4 16.3 %collective-permute-start.12 = (f32[2,64,1024]{2,1,0:T(8,128)S(1)}, f32[2,64,1024]{2,1,0:T(8,128)}, u32[]{:S(2)}, u32[]{:S(2)}) collective-permute-start(f32[2,64,1024]{2,1,0:T(8,128)S(1)} %collective-permute-done.9), channel_id=1, source_target_pairs={{0,1},{1,0},{2,3},{3,2},{4,5},{5,4},{6,7},{7,6},{8,9},{9,8},{10,11... | collective-permute-start | bytes 1572872 | tf_op jit(solution)/shard_map/ppermute | solution.py:201
  119.8 14.0 %collective-permute-start.14 = (f32[2,64,1024]{2,1,0:T(8,128)S(1)}, f32[2,64,1024]{2,1,0:T(8,128)}, u32[]{:S(2)}, u32[]{:S(2)}) collective-permute-start(f32[2,64,1024]{2,1,0:T(8,128)S(1)} %collective-permute-done.11), channel_id=1, source_target_pairs={{0,1},{1,0},{2,3},{3,2},{4,5},{5,4},{6,7},{7,6},{8,9},{9,8},{10,11... | collective-permute-start | bytes 1572872 | tf_op jit(solution)/shard_map/ppermute | solution.py:201
  144.8 14.3 %collective-permute-start.17 = (f32[256,384]{1,0:T(8,128)S(1)}, f32[256,384]{1,0:T(8,128)S(1)}, u32[]{:S(2)}, u32[]{:S(2)}) collective-permute-start(f32[256,384]{1,0:T(8,128)S(1)} %get-tuple-element.71), channel_id=1, source_target_pairs={{0,16},{16,32},{32,48},{48,0},{1,17},{17,33},{33,49},{49,1},{2,18}... | collective-permute-start | bytes 1179656 | tf_op jit(solution)/shard_map/ppermute | solution.py:274
  148.4 20.0 %collective-permute-start.18 = (f32[256,384]{1,0:T(8,128)S(1)}, f32[256,384]{1,0:T(8,128)S(1)}, u32[]{:S(2)}, u32[]{:S(2)}) collective-permute-start(f32[256,384]{1,0:T(8,128)S(1)} %get-tuple-element.72), channel_id=1, source_target_pairs={{0,32},{16,48},{32,0},{48,16},{1,33},{17,49},{33,1},{49,17},{2,34}... | collective-permute-start | bytes 1179656 | tf_op jit(solution)/shard_map/ppermute | solution.py:274
  152.7 17.0 %collective-permute-start.19 = (f32[256,384]{1,0:T(8,128)S(1)}, f32[256,384]{1,0:T(8,128)S(1)}, u32[]{:S(2)}, u32[]{:S(2)}) collective-permute-start(f32[256,384]{1,0:T(8,128)S(1)} %get-tuple-element.73), channel_id=1, source_target_pairs={{0,48},{16,0},{32,16},{48,32},{1,49},{17,1},{33,17},{49,33},{2,50}... | collective-permute-start | bytes 1179656 | tf_op jit(solution)/shard_map/ppermute | solution.py:274
  170.6 17.5 %all-to-all-start.4 = ((f32[8,32,384]{2,1,0:T(8,128)}), f32[8,32,384]{2,1,0:T(8,128)S(1)}, u32[]{:S(2)}, u32[]{:S(2)}) async-start(f32[8,32,384]{2,1,0:T(8,128)} %bitcast.20), calls=%async_computation.4 | async-start | bytes 786432 | tf_op jit(solution)/shard_map/all_to_all | solution.py:21
  174.6 13.6 %collective-permute-start.20 = (f32[256,384]{1,0:T(8,128)}, f32[256,384]{1,0:T(8,128)S(1)}, u32[]{:S(2)}, u32[]{:S(2)}) collective-permute-start(f32[256,384]{1,0:T(8,128)} %copy-done.3), channel_id=1, source_target_pairs={{0,16},{16,32},{32,48},{48,0},{1,17},{17,33},{33,49},{49,1},{2,18}... | collective-permute-start | bytes 1179656 | tf_op jit(solution)/shard_map/ppermute | solution.py:274
  179.2 18.3 %collective-permute-start.21 = (f32[256,384]{1,0:T(8,128)S(1)}, f32[256,384]{1,0:T(8,128)S(1)}, u32[]{:S(2)}, u32[]{:S(2)}) collective-permute-start(f32[256,384]{1,0:T(8,128)S(1)} %get-tuple-element.77), channel_id=1, source_target_pairs={{0,32},{16,48},{32,0},{48,16},{1,33},{17,49},{33,1},{49,17},{2,34}... | collective-permute-start | bytes 1179656 | tf_op jit(solution)/shard_map/ppermute | solution.py:274
  182.3 16.4 %collective-permute-start.22 = (f32[256,384]{1,0:T(8,128)S(1)}, f32[256,384]{1,0:T(8,128)S(1)}, u32[]{:S(2)}, u32[]{:S(2)}) collective-permute-start(f32[256,384]{1,0:T(8,128)S(1)} %get-tuple-element.78), channel_id=1, source_target_pairs={{0,48},{16,0},{32,16},{48,32},{1,49},{17,1},{33,17},{49,33},{2,50}... | collective-permute-start | bytes 1179656 | tf_op jit(solution)/shard_map/ppermute | solution.py:274
  (14 other events, 244.7 us)

commit v7 on v6

--- a/solution.py
+++ b/solution.py
@@ -60,15 +60,14 @@
     return sum(jnp.dot(left[i], right[j], preferred_element_type=jnp.float32) for i, j in terms)
 
 
+def halve_kernel(value, high, low):
+    high[...], low[...] = split(value[...])
+
+
 def couple_kernel(slots, where, *rest):
-    pieces, (panel, placed) = rest[:9], rest[9:11]
-    shares, (rows, high, low, total) = rest[11 : 11 + slots], rest[11 + slots :]
+    pieces, (high, low, placed) = rest[:9], rest[9:12]
+    shares, (rows, total) = rest[12 : 12 + slots], rest[12 + slots :]
     step = pl.program_id(0)
-
-    @pl.when(step == 0)
-    def _():
-        high[...], low[...] = split(panel[...])
-
     part = pieces[0].shape[2]
     tall = rows.shape[0] // (2 * part)
     level, core = where[2], where[3]
@@ -157,7 +156,7 @@
     me = lax.axis_index(ROWS)
 
     half = pivots // 2
-    cut = pivots // 96 * 40
+    cut = pivots // 96 * 44
     core = lax.axis_index("c")
     first = child_start - me * span
 
@@ -165,10 +164,12 @@
         length = lax.axis_size(axis)
         return lax.ppermute(value, axis, [(i, (i + hops) % length) for i in range(length)])
 
-    maps = spread(front_map, "x").reshape(across, count)
     down_2, up_2 = ring(ancestor_sol, "z", 2), ring(ancestor_sol, "z", -2)
     down_1, up_1 = ring(ancestor_sol, "z", 1), ring(ancestor_sol, "z", -1)
-    inverse_lo = spread(inverse_factor[:cut], "x")
+    rows = jnp.broadcast_to(front_map.astype(jnp.float32)[:, None], (count, span))
+    inverse_lo = spread(jnp.concatenate([inverse_factor[:cut], rows]), "x")
+    inverse_lo = inverse_lo.reshape(across, cut + count, span)
+    maps = inverse_lo[:, cut:, 0].astype(jnp.int32)
     mid = srcs // 2
     upper, lower = ring(down_2[:mid], "z", 2), ring(up_2[mid:], "z", -2)
     down_3, up_3 = ring(down_2, "z", 1), ring(up_2, "z", -1)
@@ -183,36 +184,23 @@
         compiler_params=grant(12),
         name="pack",
     )(maps, lax.axis_index("z").reshape(1), *column)
-    sends, inverse_lo = lax.optimization_barrier((sends, inverse_lo))
+    sends, inverse_lo, rest, right_side, lower_panel = lax.optimization_barrier(
+        (sends, inverse_lo, inverse_factor[cut:], right_side, lower_panel)
+    )
     arrived = exchange(sends, "x")
-    boundary = pl.pallas_call(
-        lambda *refs: pick_kernel(count, *refs),
-        out_shape=jax.ShapeDtypeStruct((srcs, width), jnp.float32),
-        in_specs=[SMEM, VMEM],
-        out_specs=VMEM,
-        compiler_params=grant(8),
-        name="pick",
-    )(front_map, arrived)
-    boundary, rest, right_side = lax.optimization_barrier(
-        (boundary, inverse_factor[cut:], right_side)
-    )
-
-    def swap(value):
-        return lax.ppermute(value, "c", [(0, 1), (1, 0)])
-
-    def apart(value, hops):
-        pairs = [
-            (2 * y + c, 2 * ((y + (hops, -hops)[c]) % tall) + c)
-            for y in range(tall)
-            for c in range(cores)
-        ]
-        return lax.ppermute(value, PIV, pairs)
-
-    chip = jnp.stack([boundary, swap(boundary)])
-    near_2, near_1 = apart(chip, 2), apart(chip, 1)
-    inverse_hi = spread(rest, "x")
-    near_4, near_3 = apart(near_2[0], 2), apart(near_2, 1)
-    far_2, far_1, far_4, far_3 = swap(near_2), swap(near_1), swap(near_4), swap(near_3)
+    rest = jnp.broadcast_to(rest[None], (across, *rest.shape))
+    panel_high, panel_low = pl.pallas_call(
+        halve_kernel,
+        grid=(4,),
+        out_shape=(jax.ShapeDtypeStruct((width, pivots), jnp.bfloat16),) * 2,
+        in_specs=[pl.BlockSpec((width // 4, pivots), lambda i: (i, 0))],
+        out_specs=(pl.BlockSpec((width // 4, pivots), lambda i: (i, 0)),) * 2,
+        compiler_params=grant(60),
+        cost_estimate=pl.CostEstimate(
+            flops=4 * width * pivots, bytes_accessed=8 * width * pivots, transcendentals=0
+        ),
+        name="halve",
+    )(lower_panel)
     own_share = right_side.shape[1]
     tile = jnp.minimum(lax.div(me * own_share, BLK), pivots // BLK - 2)
     place = (
@@ -226,8 +214,35 @@
         precision=lax.Precision.HIGHEST,
         preferred_element_type=jnp.float32,
     ).reshape(across, quarter, 2 * BLK)
+    boundary = pl.pallas_call(
+        lambda *refs: pick_kernel(count, *refs),
+        out_shape=jax.ShapeDtypeStruct((srcs, width), jnp.float32),
+        in_specs=[SMEM, VMEM],
+        out_specs=VMEM,
+        compiler_params=grant(8),
+        name="pick",
+    )(front_map, arrived)
+    boundary, rest, placed, panel_high, panel_low = lax.optimization_barrier(
+        (boundary, rest, placed, panel_high, panel_low)
+    )
+
+    def swap(value):
+        return lax.ppermute(value, "c", [(0, 1), (1, 0)])
+
+    def apart(value, hops):
+        pairs = [
+            (2 * y + c, 2 * ((y + (hops, -hops)[c]) % tall) + c)
+            for y in range(tall)
+            for c in range(cores)
+        ]
+        return lax.ppermute(value, PIV, pairs)
+
+    chip = jnp.stack([boundary, swap(boundary)])
+    near_2, near_1 = apart(chip, 2), apart(chip, 1)
+    inverse_hi = exchange(rest, "x")
+    near_4, near_3 = apart(near_2[0], 2), apart(near_2, 1)
+    far_2, far_1, far_4, far_3 = swap(near_2), swap(near_1), swap(near_4), swap(near_3)
     pieces = (chip, near_1, near_2, near_3, far_1, far_2, far_3, near_4, far_4)
-    pieces, inverse_hi, placed = lax.optimization_barrier((pieces, inverse_hi, placed))
     pieces = [piece.reshape(-1, across, part, width) for piece in pieces]
     few = quarter // deep
     where = jnp.stack([lax.axis_index("x"), tile, lax.axis_index("y"), core])
@@ -248,13 +263,12 @@
             ]
             + [
                 pl.BlockSpec((width, pivots), lambda i, at: (0, 0)),
+                pl.BlockSpec((width, pivots), lambda i, at: (0, 0)),
                 pl.BlockSpec((1, quarter, 2 * BLK), turn),
             ],
             out_specs=(pl.BlockSpec((quarter, half), lambda i, at: (0, 0)),) * (2 * across),
             scratch_shapes=[
                 pltpu.VMEM((quarter, width), jnp.float32),
-                pltpu.VMEM((width, pivots), jnp.bfloat16),
-                pltpu.VMEM((width, pivots), jnp.bfloat16),
                 pltpu.VMEM((quarter, pivots), jnp.float32),
             ],
         ),
@@ -266,7 +280,7 @@
             transcendentals=0,
         ),
         name="couple",
-    )(where, *pieces, lower_panel, placed)
+    )(where, *pieces, panel_high, panel_low, placed)
     shares_a, shares_b = shares[:across], shares[across:]
 
     def across_sent(shares):
@@ -281,6 +295,8 @@
 
     arrived_a = across_sent(shares_a)
     arrived_b = across_sent(shares_b)
+    own_a, inverse_hi = lax.optimization_barrier((shares_a[0], inverse_hi))
+    shares_a = (own_a, *shares_a[1:])
     nearer_a = nearer(shares_a, arrived_a)
     own_b, nearer_a = lax.optimization_barrier((shares_b[0], nearer_a))
     shares_b = (own_b, *shares_b[1:])
@@ -314,8 +330,8 @@
     )(
         core.reshape(1),
         reduced,
-        inverse_lo.reshape(across, cut, span),
-        inverse_hi.reshape(across, pivots - cut, span),
+        inverse_lo,
+        inverse_hi,
     )
     kept = kept + swap(other)
     arrived = exchange(kept.reshape(across * tall, part, span), ("x", "y"))

time: 294 us -> 280 us (0.952)
  starting transfers between devices: 122 us -> 111 us
  waiting for transfers between devices: 59.6 us -> 52.4 us
  Pallas kernels: 20.7 us -> 25.4 us
    all_to_all x5 -> x4, waiting for transfers between devices: 15.4 us -> 7.64 us  [exchange(): return lax.all_to_all(value, axes, split_axis=0, concat_axis=0, tiled=True)]
    all_to_all x5 -> x4, starting transfers between devices: 22.4 us -> 17 us  [exchange(): return lax.all_to_all(value, axes, split_axis=0, concat_axis=0, tiled=True)]
    ppermute x4, waiting for transfers between devices: 11.1 us -> 6.73 us  [apart(): return lax.ppermute(value, PIV, pairs)]
    pallas_call x0 -> x1, Pallas kernels: none -> 4.34 us  [body(): pl.pallas_call(halve_kernel, grid=(4,), out_shape=(jax.ShapeDtypeStruct((...]
    ppermute x6, waiting for transfers between devices: 24.5 us -> 28 us  [across_sent(): lax.ppermute(shares[k], 'x', [(i, (i + k) % across) for i in range(across)])]
    ppermute x6, starting transfers between devices: 21.9 us -> 18.8 us  [across_sent(): lax.ppermute(shares[k], 'x', [(i, (i + k) % across) for i in range(across)])]
  transfers between devices with their start and end apart: 29 -> 28, of which waited for: 14 -> 17; matrix products, arithmetic and copies ran while one was open for 2% -> 1% of each run, Pallas kernels for 1% -> 5%
where the time goes in v7:
time: 280 us; the launch traced here: 275 us
  starting transfers between devices  111 us (40%)
  blocking collectives  71.7 us (26%)
  waiting for transfers between devices  52.4 us (19%)
  Pallas kernels  25.4 us (9%)
  local copies, waits for them, and re-layouts  7.83 us (3%)
  other arithmetic  4.01 us (1%)
    all_to_all x3, blocking collectives, exchange(): return lax.all_to_all(value, axes, split_axis=0, concat_axis=0, tiled=True)  71.7 us
    ppermute x8, starting transfers between devices, ring(): lax.ppermute(value, axis, [(i, (i + hops) % length) for i in range(length)])  35.8 us
    ppermute x6, waiting for transfers between devices, across_sent(): lax.ppermute(shares[k], 'x', [(i, (i + k) % across) for i in range(across)])  28 us
    ppermute x6, starting transfers between devices, swap(): return lax.ppermute(value, 'c', [(0, 1), (1, 0)])  22.9 us
    ppermute x6, starting transfers between devices, across_sent(): lax.ppermute(shares[k], 'x', [(i, (i + k) % across) for i in range(across)])  18.8 us
    all_to_all x4, starting transfers between devices, exchange(): return lax.all_to_all(value, axes, split_axis=0, concat_axis=0, tiled=True)  17 us
    ppermute x4, starting transfers between devices, apart(): return lax.ppermute(value, PIV, pairs)  16.8 us
    pallas_call x1, Pallas kernels, body(): pl.pallas_call(lambda *refs: couple_kernel(2 * across, *refs), grid_spec=...  10.5 us
  transfers between devices with their start and end apart: 28, of which 17 were waited for; matrix products, arithmetic and copies ran while one was open for 1% of the time, Pallas kernels for 5%

profile of v7, /device:TPU:1, one launch (start us, length us, event | category | flops | bytes accessed | tf_op | source)
XLA Modules:
  0.0 274.7 jit_solution(10467774993693642177)
XLA Ops:
  3.5 5.0 %all-to-all-start = ((f32[4,360,384]{2,1,0:T(8,128)}), f32[4,360,384]{2,1,0:T(8,128)}, u32[]{:S(2)}, u32[]{:S(2)}) async-start(f32[4,360,384]{2,1,0:T(8,128)} %broadcast_in_dim.7), calls=%async_computation | async-start | bytes 4423680 | tf_op jit(solution)/shard_map/all_to_all | solution.py:21
  8.4 6.3 %collective-permute-start.3 = (f32[64,1024]{1,0:T(8,128)S(1)}, f32[64,1024]{1,0:T(8,128)S(1)}, u32[]{:S(2)}, u32[]{:S(2)}) collective-permute-start(f32[64,1024]{1,0:T(8,128)S(1)} %copy-done), channel_id=1, source_target_pairs={{0,128},{64,192},{128,256},{192,320},{256,384},{320,448},{384,0},{... | collective-permute-start | bytes 786440 | tf_op jit(solution)/shard_map/ppermute | solution.py:165
  14.7 6.8 %collective-permute-start.1 = (f32[64,1024]{1,0:T(8,128)S(1)}, f32[64,1024]{1,0:T(8,128)S(1)}, u32[]{:S(2)}, u32[]{:S(2)}) collective-permute-start(f32[64,1024]{1,0:T(8,128)S(1)} %copy-done), channel_id=1, source_target_pairs={{0,384},{64,448},{128,0},{192,64},{256,128},{320,192},{384,256},{4... | collective-permute-start | bytes 786440 | tf_op jit(solution)/shard_map/ppermute | solution.py:165
  21.5 4.3 %collective-permute-start = (f32[64,1024]{1,0:T(8,128)S(1)}, f32[64,1024]{1,0:T(8,128)S(1)}, u32[]{:S(2)}, u32[]{:S(2)}) collective-permute-start(f32[64,1024]{1,0:T(8,128)S(1)} %copy-done), channel_id=1, source_target_pairs={{0,448},{64,0},{128,64},{192,128},{256,192},{320,256},{384,320},{4... | collective-permute-start | bytes 786440 | tf_op jit(solution)/shard_map/ppermute | solution.py:165
  27.7 4.6 %collective-permute-start.6 = (f32[32,1024]{1,0:T(8,128)S(1)}, f32[32,1024]{1,0:T(8,128)S(1)}, u32[]{:S(2)}, u32[]{:S(2)}) collective-permute-start(f32[32,1024]{1,0:T(8,128)S(1)} %slice.24), channel_id=1, source_target_pairs={{0,128},{64,192},{128,256},{192,320},{256,384},{320,448},{384,0},{... | collective-permute-start | bytes 393224 | tf_op jit(solution)/shard_map/ppermute | solution.py:165
  32.5 5.1 %collective-permute-start.7 = (f32[32,1024]{1,0:T(8,128)S(1)}, f32[32,1024]{1,0:T(8,128)S(1)}, u32[]{:S(2)}, u32[]{:S(2)}) collective-permute-start(f32[32,1024]{1,0:T(8,128)S(1)} %slice.25), channel_id=1, source_target_pairs={{0,384},{64,448},{128,0},{192,64},{256,128},{320,192},{384,256},{4... | collective-permute-start | bytes 393224 | tf_op jit(solution)/shard_map/ppermute | solution.py:165
  37.6 5.0 %collective-permute-start.4 = (f32[64,1024]{1,0:T(8,128)S(1)}, f32[64,1024]{1,0:T(8,128)S(1)}, u32[]{:S(2)}, u32[]{:S(2)}) collective-permute-start(f32[64,1024]{1,0:T(8,128)S(1)} %collective-permute-done.3.refs_7_), channel_id=1, source_target_pairs={{0,64},{64,128},{128,192},{192,256},{256,320},{320,384},{384,448},... | collective-permute-start | bytes 786440 | tf_op jit(solution)/shard_map/ppermute | solution.py:165
  57.8 4.3 %halve.1 = (bf16[1024,768]{1,0:T(8,128)(2,1)}, bf16[1024,768]{1,0:T(8,128)(2,1)}) custom-call(f32[1024,768]{1,0:T(8,128)} %value), custom_call_target="tpu_custom_call" | custom-call | flops 3145728 | bytes 6291456 | tf_op jit(solution)/shard_map/halve/pallas_call | solution.py:192
  63.8 5.3 %all-to-all-done.1.refs_1_ = f32[4,64,1024]{2,1,0:T(8,128)S(1)} async-done(((f32[4,64,1024]{2,1,0:T(8,128)}), f32[4,64,1024]{2,1,0:T(8,128)S(1)}, u32[]{:S(2)}, u32[]{:S(2)}) %all-to-all-start.1) | async-done | bytes 1048608 | tf_op jit(solution)/shard_map/all_to_all | solution.py:21
  71.4 5.7 %collective-permute-start.8 = (f32[64,1024]{1,0:T(8,128)S(1)}, f32[64,1024]{1,0:T(8,128)S(1)}, u32[]{:S(2)}, u32[]{:S(2)}) collective-permute-start(f32[64,1024]{1,0:T(8,128)S(1)} %pick.1), channel_id=1, source_target_pairs={{0,1},{1,0},{2,3},{3,2},{4,5},{5,4},{6,7},{7,6},{8,9},{9,8},{10,11... | collective-permute-start | bytes 786440 | tf_op jit(solution)/shard_map/ppermute | solution.py:230
  78.2 5.9 %collective-permute-start.10 = (f32[2,64,1024]{2,1,0:T(8,128)S(1)}, f32[2,64,1024]{2,1,0:T(8,128)S(1)}, u32[]{:S(2)}, u32[]{:S(2)}) collective-permute-start(f32[2,64,1024]{2,1,0:T(8,128)S(1)} %pad_maximum_fusion.2), channel_id=1, source_target_pairs={{0,4},{1,13},{2,6},{3,15},{4,8},{5,1},{6,10},{7,3},{8,12},{9,5},{1... | collective-permute-start | bytes 1572872 | tf_op jit(solution)/shard_map/ppermute | solution.py:238
  84.1 4.5 %all-to-all-start.2 = ((f32[4,416,384]{2,1,0:T(8,128)}), f32[4,416,384]{2,1,0:T(8,128)}, u32[]{:S(2)}, u32[]{:S(2)}) async-start(f32[4,416,384]{2,1,0:T(8,128)} %broadcast_in_dim.8), calls=%async_computation.2 | async-start | bytes 5111808 | tf_op jit(solution)/shard_map/all_to_all | solution.py:21
  91.7 4.2 %collective-permute-done.10 = f32[2,64,1024]{2,1,0:T(8,128)S(1)} collective-permute-done((f32[2,64,1024]{2,1,0:T(8,128)S(1)}, f32[2,64,1024]{2,1,0:T(8,128)S(1)}, u32[]{:S(2)}, u32[]{:S(2)}) %collective-permute-start.10) | collective-permute-done | bytes 524320 | tf_op jit(solution)/shard_map/ppermute | solution.py:238
  95.8 4.2 %collective-permute-start.11 = (f32[2,64,1024]{2,1,0:T(8,128)S(1)}, f32[2,64,1024]{2,1,0:T(8,128)S(1)}, u32[]{:S(2)}, u32[]{:S(2)}) collective-permute-start(f32[2,64,1024]{2,1,0:T(8,128)S(1)} %collective-permute-done.10), channel_id=1, source_target_pairs={{0,2},{1,15},{2,4},{3,1},{4,6},{5,3},{6,8},{7,5},{8,10},{9,7},{10,... | collective-permute-start | bytes 1572872 | tf_op jit(solution)/shard_map/ppermute | solution.py:238
  119.7 10.5 %couple.1 = (f32[256,384]{1,0:T(8,128)S(1)}, f32[256,384]{1,0:T(8,128)}, f32[256,384]{1,0:T(8,128)}, f32[256,384]{1,0:T(8,128)}, f32[256,384]{1,0:T(8,128)S(1)},...) custom-call(s32[4]{0:T(128)S(1)} %pad_add_fusion.refs_0_, ...), custom_call_target="tpu_custom_call" | custom-call | flops 4831838208 | bytes 10485760 | tf_op jit(solution)/shard_map/couple/pallas_call | solution.py:253
  139.6 5.7 %collective-permute-done.17 = f32[256,384]{1,0:T(8,128)S(1)} collective-permute-done((f32[256,384]{1,0:T(8,128)}, f32[256,384]{1,0:T(8,128)S(1)}, u32[]{:S(2)}, u32[]{:S(2)}) %collective-permute-start.17) | collective-permute-done | bytes 393248 | tf_op jit(solution)/shard_map/ppermute | solution.py:288
  145.3 7.3 %collective-permute-done.18 = f32[256,384]{1,0:T(8,128)S(1)} collective-permute-done((f32[256,384]{1,0:T(8,128)}, f32[256,384]{1,0:T(8,128)S(1)}, u32[]{:S(2)}, u32[]{:S(2)}) %collective-permute-start.18) | collective-permute-done | bytes 393248 | tf_op jit(solution)/shard_map/ppermute | solution.py:288
  162.8 5.5 %collective-permute-start.21 = (f32[256,384]{1,0:T(8,128)S(1)}, f32[256,384]{1,0:T(8,128)S(1)}, u32[]{:S(2)}, u32[]{:S(2)}) collective-permute-start(f32[256,384]{1,0:T(8,128)S(1)} %get-tuple-element.73), channel_id=1, source_target_pairs={{0,32},{16,48},{32,0},{48,16},{1,33},{17,49},{33,1},{49,17},{2,34}... | collective-permute-start | bytes 1179656 | tf_op jit(solution)/shard_map/ppermute | solution.py:288
  173.2 9.9 %collective-permute-done.21 = f32[256,384]{1,0:T(8,128)S(1)} collective-permute-done((f32[256,384]{1,0:T(8,128)S(1)}, f32[256,384]{1,0:T(8,128)S(1)}, u32[]{:S(2)}, u32[]{:S(2)}) %collective-permute-start.21) | collective-permute-done | bytes 393248 | tf_op jit(solution)/shard_map/ppermute | solution.py:288
  184.7 18.9 %all_to_all.35.pieces_b = f32[8,32,384]{2,1,0:T(8,128)S(1)} all-to-all(f32[8,32,384]{2,1,0:T(8,128)S(1)} %bitcast.46), channel_id=1, replica_groups=mesh['z'=8,'x'=4,'y'=8,'c'=2] {'z'}, dimensions={0} | all-to-all | bytes 786432 | tf_op jit(solution)/shard_map/all_to_all | solution.py:21
  203.7 22.6 %all_to_all.36 = f32[8,32,768]{2,1,0:T(8,128)} all-to-all(f32[8,32,768]{2,1,0:T(8,128)S(1)} %join.1), channel_id=1, replica_groups=mesh['z'=8,'x'=4,'y'=8,'c'=2] {'z'}, dimensions={0} | all-to-all | bytes 1572864 | tf_op jit(solution)/shard_map/all_to_all | solution.py:21
  226.3 6.7 %solve.1 = (f32[4,8,16,384]{3,2,1,0:T(8,128)}, f32[4,8,16,384]{3,2,1,0:T(8,128)}) custom-call(s32[1]{0:T(128)} %bitcast.core, f32[256,768]{1,0:T(8,128)} %bitcast.45, f32[4,360,384]{2,1,0:T(8,128)} %all-to-all-done.inverse_lo, f32[4,416,384]{2,1,0:T(8,128)} %all-to-all-done.2.inverse_hi), custom_call_target="tpu_custom_call" | custom-call | tf_op jit(solution)/shard_map/solve/pallas_call | solution.py:313
  233.0 6.7 %collective-permute-start.23 = (f32[4,8,16,384]{3,2,1,0:T(8,128)}, f32[4,8,16,384]{3,2,1,0:T(8,128)S(1)}, u32[]{:S(2)}, u32[]{:S(2)}) collective-permute-start(f32[4,8,16,384]{3,2,1,0:T(8,128)} %get-tuple-element.78), channel_id=1, source_target_pairs={{0,1},{1,0},{2,3},{3,2},{4,5},{5,4},{6,7},{7,6},{8,9},{9,8},{10,11... | collective-permute-start | bytes 2359304 | tf_op jit(solution)/shard_map/ppermute | solution.py:230
  243.0 30.3 %all_to_all.37 = f32[32,16,384]{2,1,0:T(8,128)S(1)} all-to-all(f32[32,16,384]{2,1,0:T(8,128)S(1)} %bitcast.44), channel_id=1, replica_groups=mesh['z'=8,'x'=4,'y'=8,'c'=2] {'x','y'}, dimensions={0} | all-to-all | bytes 1572864 | tf_op jit(solution)/shard_map/all_to_all | solution.py:21
  (86 shorter events, 79.0 us)
Async XLA Ops:
  3.5 41.1 %all-to-all-start = ((f32[4,360,384]{2,1,0:T(8,128)}), f32[4,360,384]{2,1,0:T(8,128)}, u32[]{:S(2)}, u32[]{:S(2)}) async-start(f32[4,360,384]{2,1,0:T(8,128)} %broadcast_in_dim.7), calls=%async_computation | async-start | bytes 4423680 | tf_op jit(solution)/shard_map/all_to_all | solution.py:21
  8.4 19.3 %collective-permute-start.3 = (f32[64,1024]{1,0:T(8,128)S(1)}, f32[64,1024]{1,0:T(8,128)S(1)}, u32[]{:S(2)}, u32[]{:S(2)}) collective-permute-start(f32[64,1024]{1,0:T(8,128)S(1)} %copy-done), channel_id=1, source_target_pairs={{0,128},{64,192},{128,256},{192,320},{256,384},{320,448},{384,0},{... | collective-permute-start | bytes 786440 | tf_op jit(solution)/shard_map/ppermute | solution.py:165
  14.7 17.8 %collective-permute-start.1 = (f32[64,1024]{1,0:T(8,128)S(1)}, f32[64,1024]{1,0:T(8,128)S(1)}, u32[]{:S(2)}, u32[]{:S(2)}) collective-permute-start(f32[64,1024]{1,0:T(8,128)S(1)} %copy-done), channel_id=1, source_target_pairs={{0,384},{64,448},{128,0},{192,64},{256,128},{320,192},{384,256},{4... | collective-permute-start | bytes 786440 | tf_op jit(solution)/shard_map/ppermute | solution.py:165
  21.5 21.1 %collective-permute-start = (f32[64,1024]{1,0:T(8,128)S(1)}, f32[64,1024]{1,0:T(8,128)S(1)}, u32[]{:S(2)}, u32[]{:S(2)}) collective-permute-start(f32[64,1024]{1,0:T(8,128)S(1)} %copy-done), channel_id=1, source_target_pairs={{0,448},{64,0},{128,64},{192,128},{256,192},{320,256},{384,320},{4... | collective-permute-start | bytes 786440 | tf_op jit(solution)/shard_map/ppermute | solution.py:165
  25.8 19.7 %collective-permute-start.5 = (f32[64,1024]{1,0:T(8,128)S(1)}, f32[64,1024]{1,0:T(8,128)S(1)}, u32[]{:S(2)}, u32[]{:S(2)}) collective-permute-start(f32[64,1024]{1,0:T(8,128)S(1)} %copy-done), channel_id=1, source_target_pairs={{0,64},{64,128},{128,192},{192,256},{256,320},{320,384},{384,448},... | collective-permute-start | bytes 786440 | tf_op jit(solution)/shard_map/ppermute | solution.py:165
  27.7 17.7 %collective-permute-start.6 = (f32[32,1024]{1,0:T(8,128)S(1)}, f32[32,1024]{1,0:T(8,128)S(1)}, u32[]{:S(2)}, u32[]{:S(2)}) collective-permute-start(f32[32,1024]{1,0:T(8,128)S(1)} %slice.24), channel_id=1, source_target_pairs={{0,128},{64,192},{128,256},{192,320},{256,384},{320,448},{384,0},{... | collective-permute-start | bytes 393224 | tf_op jit(solution)/shard_map/ppermute | solution.py:165
  32.5 13.0 %collective-permute-start.7 = (f32[32,1024]{1,0:T(8,128)S(1)}, f32[32,1024]{1,0:T(8,128)S(1)}, u32[]{:S(2)}, u32[]{:S(2)}) collective-permute-start(f32[32,1024]{1,0:T(8,128)S(1)} %slice.25), channel_id=1, source_target_pairs={{0,384},{64,448},{128,0},{192,64},{256,128},{320,192},{384,256},{4... | collective-permute-start | bytes 393224 | tf_op jit(solution)/shard_map/ppermute | solution.py:165
  37.6 9.7 %collective-permute-start.4 = (f32[64,1024]{1,0:T(8,128)S(1)}, f32[64,1024]{1,0:T(8,128)S(1)}, u32[]{:S(2)}, u32[]{:S(2)}) collective-permute-start(f32[64,1024]{1,0:T(8,128)S(1)} %collective-permute-done.3.refs_7_), channel_id=1, source_target_pairs={{0,64},{64,128},{128,192},{192,256},{256,320},{320,384},{384,448},... | collective-permute-start | bytes 786440 | tf_op jit(solution)/shard_map/ppermute | solution.py:165
  52.9 16.2 %all-to-all-start.1 = ((f32[4,64,1024]{2,1,0:T(8,128)}), f32[4,64,1024]{2,1,0:T(8,128)S(1)}, u32[]{:S(2)}, u32[]{:S(2)}) async-start(f32[4,64,1024]{2,1,0:T(8,128)} %pack.1), calls=%async_computation.1 | async-start | bytes 2097152 | tf_op jit(solution)/shard_map/all_to_all | solution.py:21
  78.2 17.6 %collective-permute-start.10 = (f32[2,64,1024]{2,1,0:T(8,128)S(1)}, f32[2,64,1024]{2,1,0:T(8,128)S(1)}, u32[]{:S(2)}, u32[]{:S(2)}) collective-permute-start(f32[2,64,1024]{2,1,0:T(8,128)S(1)} %pad_maximum_fusion.2), channel_id=1, source_target_pairs={{0,4},{1,13},{2,6},{3,15},{4,8},{5,1},{6,10},{7,3},{8,12},{9,5},{1... | collective-permute-start | bytes 1572872 | tf_op jit(solution)/shard_map/ppermute | solution.py:238
  84.1 55.4 %all-to-all-start.2 = ((f32[4,416,384]{2,1,0:T(8,128)}), f32[4,416,384]{2,1,0:T(8,128)}, u32[]{:S(2)}, u32[]{:S(2)}) async-start(f32[4,416,384]{2,1,0:T(8,128)} %broadcast_in_dim.8), calls=%async_computation.2 | async-start | bytes 5111808 | tf_op jit(solution)/shard_map/all_to_all | solution.py:21
  88.7 17.4 %collective-permute-start.9 = (f32[2,64,1024]{2,1,0:T(8,128)S(1)}, f32[2,64,1024]{2,1,0:T(8,128)S(1)}, u32[]{:S(2)}, u32[]{:S(2)}) collective-permute-start(f32[2,64,1024]{2,1,0:T(8,128)S(1)} %pad_maximum_fusion.2), channel_id=1, source_target_pairs={{0,2},{1,15},{2,4},{3,1},{4,6},{5,3},{6,8},{7,5},{8,10},{9,7},{10,... | collective-permute-start | bytes 1572872 | tf_op jit(solution)/shard_map/ppermute | solution.py:238
  95.8 12.7 %collective-permute-start.11 = (f32[2,64,1024]{2,1,0:T(8,128)S(1)}, f32[2,64,1024]{2,1,0:T(8,128)S(1)}, u32[]{:S(2)}, u32[]{:S(2)}) collective-permute-start(f32[2,64,1024]{2,1,0:T(8,128)S(1)} %collective-permute-done.10), channel_id=1, source_target_pairs={{0,2},{1,15},{2,4},{3,1},{4,6},{5,3},{6,8},{7,5},{8,10},{9,7},{10,... | collective-permute-start | bytes 1572872 | tf_op jit(solution)/shard_map/ppermute | solution.py:238
  100.1 12.8 %collective-permute-start.15 = (f32[64,1024]{1,0:T(8,128)S(1)}, f32[64,1024]{1,0:T(8,128)S(1)}, u32[]{:S(2)}, u32[]{:S(2)}) collective-permute-start(f32[64,1024]{1,0:T(8,128)S(1)} %slice_bitcast_fusion), channel_id=1, source_target_pairs={{0,4},{1,13},{2,6},{3,15},{4,8},{5,1},{6,10},{7,3},{8,12},{9,5},{1... | collective-permute-start | bytes 786440 | tf_op jit(solution)/shard_map/ppermute | solution.py:238
  103.8 13.2 %collective-permute-start.13 = (f32[2,64,1024]{2,1,0:T(8,128)S(1)}, f32[2,64,1024]{2,1,0:T(8,128)}, u32[]{:S(2)}, u32[]{:S(2)}) collective-permute-start(f32[2,64,1024]{2,1,0:T(8,128)S(1)} %collective-permute-done.10), channel_id=1, source_target_pairs={{0,1},{1,0},{2,3},{3,2},{4,5},{5,4},{6,7},{7,6},{8,9},{9,8},{10,11... | collective-permute-start | bytes 1572872 | tf_op jit(solution)/shard_map/ppermute | solution.py:230
  106.1 10.9 %collective-permute-start.12 = (f32[2,64,1024]{2,1,0:T(8,128)S(1)}, f32[2,64,1024]{2,1,0:T(8,128)S(1)}, u32[]{:S(2)}, u32[]{:S(2)}) collective-permute-start(f32[2,64,1024]{2,1,0:T(8,128)S(1)} %collective-permute-done.9), channel_id=1, source_target_pairs={{0,1},{1,0},{2,3},{3,2},{4,5},{5,4},{6,7},{7,6},{8,9},{9,8},{10,11... | collective-permute-start | bytes 1572872 | tf_op jit(solution)/shard_map/ppermute | solution.py:230
  108.5 10.2 %collective-permute-start.14 = (f32[2,64,1024]{2,1,0:T(8,128)S(1)}, f32[2,64,1024]{2,1,0:T(8,128)}, u32[]{:S(2)}, u32[]{:S(2)}) collective-permute-start(f32[2,64,1024]{2,1,0:T(8,128)S(1)} %collective-permute-done.11), channel_id=1, source_target_pairs={{0,1},{1,0},{2,3},{3,2},{4,5},{5,4},{6,7},{7,6},{8,9},{9,8},{10,11... | collective-permute-start | bytes 1572872 | tf_op jit(solution)/shard_map/ppermute | solution.py:230
  131.0 14.3 %collective-permute-start.17 = (f32[256,384]{1,0:T(8,128)}, f32[256,384]{1,0:T(8,128)S(1)}, u32[]{:S(2)}, u32[]{:S(2)}) collective-permute-start(f32[256,384]{1,0:T(8,128)} %get-tuple-element.67), channel_id=1, source_target_pairs={{0,16},{16,32},{32,48},{48,0},{1,17},{17,33},{33,49},{49,1},{2,18}... | collective-permute-start | bytes 1179656 | tf_op jit(solution)/shard_map/ppermute | solution.py:288
  133.3 19.3 %collective-permute-start.18 = (f32[256,384]{1,0:T(8,128)}, f32[256,384]{1,0:T(8,128)S(1)}, u32[]{:S(2)}, u32[]{:S(2)}) collective-permute-start(f32[256,384]{1,0:T(8,128)} %get-tuple-element.68), channel_id=1, source_target_pairs={{0,32},{16,48},{32,0},{48,16},{1,33},{17,49},{33,1},{49,17},{2,34}... | collective-permute-start | bytes 1179656 | tf_op jit(solution)/shard_map/ppermute | solution.py:288
  137.0 18.5 %collective-permute-start.19 = (f32[256,384]{1,0:T(8,128)}, f32[256,384]{1,0:T(8,128)S(1)}, u32[]{:S(2)}, u32[]{:S(2)}) collective-permute-start(f32[256,384]{1,0:T(8,128)} %get-tuple-element.69), channel_id=1, source_target_pairs={{0,48},{16,0},{32,16},{48,32},{1,49},{17,1},{33,17},{49,33},{2,50}... | collective-permute-start | bytes 1179656 | tf_op jit(solution)/shard_map/ppermute | solution.py:288
  156.3 16.1 %all-to-all-start.3 = ((f32[8,32,384]{2,1,0:T(8,128)}), f32[8,32,384]{2,1,0:T(8,128)S(1)}, u32[]{:S(2)}, u32[]{:S(2)}) async-start(f32[8,32,384]{2,1,0:T(8,128)} %bitcast.20), calls=%async_computation.3 | async-start | bytes 786432 | tf_op jit(solution)/shard_map/all_to_all | solution.py:21
  159.9 13.3 %collective-permute-start.20 = (f32[256,384]{1,0:T(8,128)S(1)}, f32[256,384]{1,0:T(8,128)S(1)}, u32[]{:S(2)}, u32[]{:S(2)}) collective-permute-start(f32[256,384]{1,0:T(8,128)S(1)} %copy-done.4), channel_id=1, source_target_pairs={{0,16},{16,32},{32,48},{48,0},{1,17},{17,33},{33,49},{49,1},{2,18}... | collective-permute-start | bytes 1179656 | tf_op jit(solution)/shard_map/ppermute | solution.py:288
  162.8 20.4 %collective-permute-start.21 = (f32[256,384]{1,0:T(8,128)S(1)}, f32[256,384]{1,0:T(8,128)S(1)}, u32[]{:S(2)}, u32[]{:S(2)}) collective-permute-start(f32[256,384]{1,0:T(8,128)S(1)} %get-tuple-element.73), channel_id=1, source_target_pairs={{0,32},{16,48},{32,0},{48,16},{1,33},{17,49},{33,1},{49,17},{2,34}... | collective-permute-start | bytes 1179656 | tf_op jit(solution)/shard_map/ppermute | solution.py:288
  168.2 16.4 %collective-permute-start.22 = (f32[256,384]{1,0:T(8,128)S(1)}, f32[256,384]{1,0:T(8,128)S(1)}, u32[]{:S(2)}, u32[]{:S(2)}) collective-permute-start(f32[256,384]{1,0:T(8,128)S(1)} %get-tuple-element.74), channel_id=1, source_target_pairs={{0,48},{16,0},{32,16},{48,32},{1,49},{17,1},{33,17},{49,33},{2,50}... | collective-permute-start | bytes 1179656 | tf_op jit(solution)/shard_map/ppermute | solution.py:288
  (15 other events, 177.7 us)

commit v8 on v7

--- a/solution.py
+++ b/solution.py
@@ -19,11 +19,6 @@
 
 def exchange(value, axes):
     return lax.all_to_all(value, axes, split_axis=0, concat_axis=0, tiled=True)
-
-
-def spread(value, axis):
-    count = lax.axis_size(axis)
-    return exchange(jnp.broadcast_to(value[None], (count, *value.shape)), axis)
 
 
 def pack_kernel(count, maps, where, *rest):
@@ -58,6 +53,19 @@
 def product(left, right):
     terms = ((0, 0), (0, 1), (1, 0))
     return sum(jnp.dot(left[i], right[j], preferred_element_type=jnp.float32) for i, j in terms)
+
+
+def repeat_kernel(own, inverse, repeated):
+    _, rows, span = repeated.shape
+    cut = inverse.shape[0]
+    repeated[0, :cut] = inverse[...]
+    for block in range(rows - cut):
+        value = own[block].astype(jnp.float32)
+        repeated[0, cut + block : cut + block + 1] = jnp.full((1, span), value, jnp.float32)
+
+
+def copy_kernel(inverse, repeated):
+    repeated[0] = inverse[...]
 
 
 def halve_kernel(value, high, low):
@@ -156,7 +164,7 @@
     me = lax.axis_index(ROWS)
 
     half = pivots // 2
-    cut = pivots // 96 * 44
+    cut = pivots // 3
     core = lax.axis_index("c")
     first = child_start - me * span
 
@@ -166,9 +174,16 @@
 
     down_2, up_2 = ring(ancestor_sol, "z", 2), ring(ancestor_sol, "z", -2)
     down_1, up_1 = ring(ancestor_sol, "z", 1), ring(ancestor_sol, "z", -1)
-    rows = jnp.broadcast_to(front_map.astype(jnp.float32)[:, None], (count, span))
-    inverse_lo = spread(jnp.concatenate([inverse_factor[:cut], rows]), "x")
-    inverse_lo = inverse_lo.reshape(across, cut + count, span)
+    inverse_lo = pl.pallas_call(
+        repeat_kernel,
+        grid=(across,),
+        out_shape=jax.ShapeDtypeStruct((across, cut + count, span), jnp.float32),
+        in_specs=[SMEM, pl.BlockSpec((cut, span), lambda i: (0, 0))],
+        out_specs=pl.BlockSpec((1, cut + count, span), lambda i: (i, 0, 0)),
+        compiler_params=grant(60),
+        name="repeat",
+    )(front_map, inverse_factor)
+    inverse_lo = exchange(inverse_lo, "x")
     maps = inverse_lo[:, cut:, 0].astype(jnp.int32)
     mid = srcs // 2
     upper, lower = ring(down_2[:mid], "z", 2), ring(up_2[mid:], "z", -2)
@@ -184,11 +199,22 @@
         compiler_params=grant(12),
         name="pack",
     )(maps, lax.axis_index("z").reshape(1), *column)
-    sends, inverse_lo, rest, right_side, lower_panel = lax.optimization_barrier(
-        (sends, inverse_lo, inverse_factor[cut:], right_side, lower_panel)
+    sends, inverse_lo, inverse_factor, right_side, lower_panel = lax.optimization_barrier(
+        (sends, inverse_lo, inverse_factor, right_side, lower_panel)
     )
     arrived = exchange(sends, "x")
-    rest = jnp.broadcast_to(rest[None], (across, *rest.shape))
+    rest = pl.pallas_call(
+        copy_kernel,
+        grid=(pivots // cut - 1, across),
+        out_shape=jax.ShapeDtypeStruct((across, pivots - cut, span), jnp.float32),
+        in_specs=[pl.BlockSpec((cut, span), lambda j, i: (j + 1, 0))],
+        out_specs=pl.BlockSpec((1, cut, span), lambda j, i: (i, j, 0)),
+        compiler_params=grant(60),
+        cost_estimate=pl.CostEstimate(
+            flops=pivots * span, bytes_accessed=5 * 4 * pivots * span, transcendentals=0
+        ),
+        name="copies",
+    )(inverse_factor)
     panel_high, panel_low = pl.pallas_call(
         halve_kernel,
         grid=(4,),

time: 280 us -> 278 us (level)
  waiting for transfers between devices: 52.4 us -> 45 us
  Pallas kernels: 25.4 us -> 32.5 us
  local copies, waits for them, and re-layouts: 7.83 us -> 4.24 us
  starting transfers between devices: 111 us -> 114 us
    pallas_call x0 -> x2, Pallas kernels: none -> 7.6 us  [the longest x1 4.85 us: body(): pl.pallas_call(copy_kernel, grid=(pivots // cut - 1, across), out_shape=j...]
    all_to_all x4, waiting for transfers between devices: 7.64 us -> 2.26 us  [exchange(): return lax.all_to_all(value, axes, split_axis=0, concat_axis=0, tiled=True)]
    broadcast_in_dim x2 -> x0, local copies, waits for them, and re-layouts: 3.21 us -> none  [the longest x1 1.69 us: body(): rest = jnp.broadcast_to(rest[None], (across, *rest.shape))]
  transfers between devices with their start and end apart: 28 -> 28, of which waited for: 17 -> 17; matrix products, arithmetic and copies ran while one was open for 1% -> 1% of each run, Pallas kernels for 5% -> 7%
where the time goes in v8:
time: 278 us; the launch traced here: 273 us
  starting transfers between devices  114 us (41%)
  blocking collectives  71.7 us (26%)
  waiting for transfers between devices  45 us (16%)
  Pallas kernels  32.5 us (12%)
  local copies, waits for them, and re-layouts  4.24 us (2%)
  other arithmetic  3.26 us (1%)
    all_to_all x3, blocking collectives, exchange(): return lax.all_to_all(value, axes, split_axis=0, concat_axis=0, tiled=True)  71.7 us
    ppermute x8, starting transfers between devices, ring(): lax.ppermute(value, axis, [(i, (i + hops) % length) for i in range(length)])  35.7 us
    ppermute x6, waiting for transfers between devices, across_sent(): lax.ppermute(shares[k], 'x', [(i, (i + k) % across) for i in range(across)])  26.5 us
    ppermute x6, starting transfers between devices, swap(): return lax.ppermute(value, 'c', [(0, 1), (1, 0)])  22.9 us
    ppermute x6, starting transfers between devices, across_sent(): lax.ppermute(shares[k], 'x', [(i, (i + k) % across) for i in range(across)])  20.7 us
    all_to_all x4, starting transfers between devices, exchange(): return lax.all_to_all(value, axes, split_axis=0, concat_axis=0, tiled=True)  18.1 us
    ppermute x4, starting transfers between devices, apart(): return lax.ppermute(value, PIV, pairs)  16.8 us
    pallas_call x1, Pallas kernels, body(): pl.pallas_call(lambda *refs: couple_kernel(2 * across, *refs), grid_spec=...  10.5 us
  transfers between devices with their start and end apart: 28, of which 17 were waited for; matrix products, arithmetic and copies ran while one was open for 1% of the time, Pallas kernels for 7%

profile of v8, /device:TPU:1, one launch (start us, length us, event | category | flops | bytes accessed | tf_op | source)
XLA Modules:
  0.0 273.0 jit_solution(11150407987381529349)
XLA Ops:
  2.8 5.0 %all-to-all-start = ((f32[4,264,384]{2,1,0:T(8,128)}), f32[4,264,384]{2,1,0:T(8,128)}, u32[]{:S(2)}, u32[]{:S(2)}) async-start(f32[4,264,384]{2,1,0:T(8,128)} %repeat.1), calls=%async_computation | async-start | bytes 3244032 | tf_op jit(solution)/shard_map/all_to_all | solution.py:21
  7.7 6.2 %collective-permute-start.3 = (f32[64,1024]{1,0:T(8,128)S(1)}, f32[64,1024]{1,0:T(8,128)S(1)}, u32[]{:S(2)}, u32[]{:S(2)}) collective-permute-start(f32[64,1024]{1,0:T(8,128)S(1)} %copy-done), channel_id=1, source_target_pairs={{0,128},{64,192},{128,256},{192,320},{256,384},{320,448},{384,0},{... | collective-permute-start | bytes 786440 | tf_op jit(solution)/shard_map/ppermute | solution.py:173
  13.9 6.8 %collective-permute-start.1 = (f32[64,1024]{1,0:T(8,128)S(1)}, f32[64,1024]{1,0:T(8,128)S(1)}, u32[]{:S(2)}, u32[]{:S(2)}) collective-permute-start(f32[64,1024]{1,0:T(8,128)S(1)} %copy-done), channel_id=1, source_target_pairs={{0,384},{64,448},{128,0},{192,64},{256,128},{320,192},{384,256},{4... | collective-permute-start | bytes 786440 | tf_op jit(solution)/shard_map/ppermute | solution.py:173
  20.7 4.3 %collective-permute-start = (f32[64,1024]{1,0:T(8,128)S(1)}, f32[64,1024]{1,0:T(8,128)S(1)}, u32[]{:S(2)}, u32[]{:S(2)}) collective-permute-start(f32[64,1024]{1,0:T(8,128)S(1)} %copy-done), channel_id=1, source_target_pairs={{0,448},{64,0},{128,64},{192,128},{256,192},{320,256},{384,320},{4... | collective-permute-start | bytes 786440 | tf_op jit(solution)/shard_map/ppermute | solution.py:173
  26.9 4.6 %collective-permute-start.6 = (f32[32,1024]{1,0:T(8,128)S(1)}, f32[32,1024]{1,0:T(8,128)S(1)}, u32[]{:S(2)}, u32[]{:S(2)}) collective-permute-start(f32[32,1024]{1,0:T(8,128)S(1)} %slice.16), channel_id=1, source_target_pairs={{0,128},{64,192},{128,256},{192,320},{256,384},{320,448},{384,0},{... | collective-permute-start | bytes 393224 | tf_op jit(solution)/shard_map/ppermute | solution.py:173
  31.6 5.2 %collective-permute-start.7 = (f32[32,1024]{1,0:T(8,128)S(1)}, f32[32,1024]{1,0:T(8,128)S(1)}, u32[]{:S(2)}, u32[]{:S(2)}) collective-permute-start(f32[32,1024]{1,0:T(8,128)S(1)} %slice.17), channel_id=1, source_target_pairs={{0,384},{64,448},{128,0},{192,64},{256,128},{320,192},{384,256},{4... | collective-permute-start | bytes 393224 | tf_op jit(solution)/shard_map/ppermute | solution.py:173
  36.8 4.9 %collective-permute-start.4 = (f32[64,1024]{1,0:T(8,128)S(1)}, f32[64,1024]{1,0:T(8,128)S(1)}, u32[]{:S(2)}, u32[]{:S(2)}) collective-permute-start(f32[64,1024]{1,0:T(8,128)S(1)} %collective-permute-done.3.refs_7_), channel_id=1, source_target_pairs={{0,64},{64,128},{128,192},{192,256},{256,320},{320,384},{384,448},... | collective-permute-start | bytes 786440 | tf_op jit(solution)/shard_map/ppermute | solution.py:173
  56.0 4.8 %copies.1 = f32[4,512,384]{2,1,0:T(8,128)} custom-call(f32[768,384]{1,0:T(8,128)} %inverse.2), custom_call_target="tpu_custom_call" | custom-call | flops 294912 | bytes 5898240 | tf_op jit(solution)/shard_map/copies/pallas_call | solution.py:206
  61.8 4.3 %halve.1 = (bf16[1024,768]{1,0:T(8,128)(2,1)}, bf16[1024,768]{1,0:T(8,128)(2,1)}) custom-call(f32[1024,768]{1,0:T(8,128)} %value), custom_call_target="tpu_custom_call" | custom-call | flops 3145728 | bytes 6291456 | tf_op jit(solution)/shard_map/halve/pallas_call | solution.py:218
  68.9 5.7 %collective-permute-start.8 = (f32[64,1024]{1,0:T(8,128)S(1)}, f32[64,1024]{1,0:T(8,128)S(1)}, u32[]{:S(2)}, u32[]{:S(2)}) collective-permute-start(f32[64,1024]{1,0:T(8,128)S(1)} %pick.1), channel_id=1, source_target_pairs={{0,1},{1,0},{2,3},{3,2},{4,5},{5,4},{6,7},{7,6},{8,9},{9,8},{10,11... | collective-permute-start | bytes 786440 | tf_op jit(solution)/shard_map/ppermute | solution.py:256
  75.7 5.9 %collective-permute-start.10 = (f32[2,64,1024]{2,1,0:T(8,128)S(1)}, f32[2,64,1024]{2,1,0:T(8,128)S(1)}, u32[]{:S(2)}, u32[]{:S(2)}) collective-permute-start(f32[2,64,1024]{2,1,0:T(8,128)S(1)} %pad_maximum_fusion.1), channel_id=1, source_target_pairs={{0,4},{1,13},{2,6},{3,15},{4,8},{5,1},{6,10},{7,3},{8,12},{9,5},{1... | collective-permute-start | bytes 1572872 | tf_op jit(solution)/shard_map/ppermute | solution.py:264
  81.6 4.7 %all-to-all-start.2 = ((f32[4,512,384]{2,1,0:T(8,128)}), f32[4,512,384]{2,1,0:T(8,128)}, u32[]{:S(2)}, u32[]{:S(2)}) async-start(f32[4,512,384]{2,1,0:T(8,128)} %copies.1), calls=%async_computation.2 | async-start | bytes 6291456 | tf_op jit(solution)/shard_map/all_to_all | solution.py:21
  110.2 4.2 %collective-permute-start.16 = (f32[64,1024]{1,0:T(8,128)S(1)}, f32[64,1024]{1,0:T(8,128)S(1)}, u32[]{:S(2)}, u32[]{:S(2)}) collective-permute-start(f32[64,1024]{1,0:T(8,128)S(1)} %collective-permute-done.15), channel_id=1, source_target_pairs={{0,1},{1,0},{2,3},{3,2},{4,5},{5,4},{6,7},{7,6},{8,9},{9,8},{10,11... | collective-permute-start | bytes 786440 | tf_op jit(solution)/shard_map/ppermute | solution.py:256
  118.0 10.5 %couple.1 = (f32[256,384]{1,0:T(8,128)S(1)}, f32[256,384]{1,0:T(8,128)}, f32[256,384]{1,0:T(8,128)}, f32[256,384]{1,0:T(8,128)}, f32[256,384]{1,0:T(8,128)S(1)},...) custom-call(s32[4]{0:T(128)S(1)} %pad_add_fusion.refs_0_, ...), custom_call_target="tpu_custom_call" | custom-call | flops 4831838208 | bytes 10485760 | tf_op jit(solution)/shard_map/couple/pallas_call | solution.py:279
  138.8 4.4 %collective-permute-done.17 = f32[256,384]{1,0:T(8,128)S(1)} collective-permute-done((f32[256,384]{1,0:T(8,128)}, f32[256,384]{1,0:T(8,128)S(1)}, u32[]{:S(2)}, u32[]{:S(2)}) %collective-permute-start.17) | collective-permute-done | bytes 393248 | tf_op jit(solution)/shard_map/ppermute | solution.py:314
  143.2 8.0 %collective-permute-done.18 = f32[256,384]{1,0:T(8,128)S(1)} collective-permute-done((f32[256,384]{1,0:T(8,128)}, f32[256,384]{1,0:T(8,128)S(1)}, u32[]{:S(2)}, u32[]{:S(2)}) %collective-permute-start.18) | collective-permute-done | bytes 393248 | tf_op jit(solution)/shard_map/ppermute | solution.py:314
  154.6 4.3 %all-to-all-start.3 = ((f32[8,32,384]{2,1,0:T(8,128)}), f32[8,32,384]{2,1,0:T(8,128)S(1)}, u32[]{:S(2)}, u32[]{:S(2)}) async-start(f32[8,32,384]{2,1,0:T(8,128)} %bitcast.20), calls=%async_computation.3 | async-start | bytes 786432 | tf_op jit(solution)/shard_map/all_to_all | solution.py:21
  159.0 5.0 %collective-permute-start.20 = (f32[256,384]{1,0:T(8,128)S(1)}, f32[256,384]{1,0:T(8,128)S(1)}, u32[]{:S(2)}, u32[]{:S(2)}) collective-permute-start(f32[256,384]{1,0:T(8,128)S(1)} %copy-done.4), channel_id=1, source_target_pairs={{0,16},{16,32},{32,48},{48,0},{1,17},{17,33},{33,49},{49,1},{2,18}... | collective-permute-start | bytes 1179656 | tf_op jit(solution)/shard_map/ppermute | solution.py:314
  172.1 9.9 %collective-permute-done.21 = f32[256,384]{1,0:T(8,128)S(1)} collective-permute-done((f32[256,384]{1,0:T(8,128)S(1)}, f32[256,384]{1,0:T(8,128)S(1)}, u32[]{:S(2)}, u32[]{:S(2)}) %collective-permute-start.21) | collective-permute-done | bytes 393248 | tf_op jit(solution)/shard_map/ppermute | solution.py:314
  183.6 18.9 %all_to_all.35.pieces_b = f32[8,32,384]{2,1,0:T(8,128)S(1)} all-to-all(f32[8,32,384]{2,1,0:T(8,128)S(1)} %bitcast.46), channel_id=1, replica_groups=mesh['z'=8,'x'=4,'y'=8,'c'=2] {'z'}, dimensions={0} | all-to-all | bytes 786432 | tf_op jit(solution)/shard_map/all_to_all | solution.py:21
  202.6 22.6 %all_to_all.36 = f32[8,32,768]{2,1,0:T(8,128)} all-to-all(f32[8,32,768]{2,1,0:T(8,128)S(1)} %join.1), channel_id=1, replica_groups=mesh['z'=8,'x'=4,'y'=8,'c'=2] {'z'}, dimensions={0} | all-to-all | bytes 1572864 | tf_op jit(solution)/shard_map/all_to_all | solution.py:21
  225.1 6.3 %solve.1 = (f32[4,8,16,384]{3,2,1,0:T(8,128)}, f32[4,8,16,384]{3,2,1,0:T(8,128)}) custom-call(s32[1]{0:T(128)} %bitcast.core, f32[256,768]{1,0:T(8,128)} %bitcast.45, f32[4,264,384]{2,1,0:T(8,128)} %all-to-all-done.inverse_lo, f32[4,512,384]{2,1,0:T(8,128)} %all-to-all-done.2.inverse_hi), custom_call_target="tpu_custom_call" | custom-call | tf_op jit(solution)/shard_map/solve/pallas_call | solution.py:339
  231.4 6.6 %collective-permute-start.23 = (f32[4,8,16,384]{3,2,1,0:T(8,128)}, f32[4,8,16,384]{3,2,1,0:T(8,128)S(1)}, u32[]{:S(2)}, u32[]{:S(2)}) collective-permute-start(f32[4,8,16,384]{3,2,1,0:T(8,128)} %get-tuple-element.78), channel_id=1, source_target_pairs={{0,1},{1,0},{2,3},{3,2},{4,5},{5,4},{6,7},{7,6},{8,9},{9,8},{10,11... | collective-permute-start | bytes 2359304 | tf_op jit(solution)/shard_map/ppermute | solution.py:256
  241.3 30.3 %all_to_all.37 = f32[32,16,384]{2,1,0:T(8,128)S(1)} all-to-all(f32[32,16,384]{2,1,0:T(8,128)S(1)} %bitcast.44), channel_id=1, replica_groups=mesh['z'=8,'x'=4,'y'=8,'c'=2] {'x','y'}, dimensions={0} | all-to-all | bytes 1572864 | tf_op jit(solution)/shard_map/all_to_all | solution.py:21
  (80 shorter events, 79.5 us)
Async XLA Ops:
  2.8 40.9 %all-to-all-start = ((f32[4,264,384]{2,1,0:T(8,128)}), f32[4,264,384]{2,1,0:T(8,128)}, u32[]{:S(2)}, u32[]{:S(2)}) async-start(f32[4,264,384]{2,1,0:T(8,128)} %repeat.1), calls=%async_computation | async-start | bytes 3244032 | tf_op jit(solution)/shard_map/all_to_all | solution.py:21
  7.7 19.2 %collective-permute-start.3 = (f32[64,1024]{1,0:T(8,128)S(1)}, f32[64,1024]{1,0:T(8,128)S(1)}, u32[]{:S(2)}, u32[]{:S(2)}) collective-permute-start(f32[64,1024]{1,0:T(8,128)S(1)} %copy-done), channel_id=1, source_target_pairs={{0,128},{64,192},{128,256},{192,320},{256,384},{320,448},{384,0},{... | collective-permute-start | bytes 786440 | tf_op jit(solution)/shard_map/ppermute | solution.py:173
  13.9 17.7 %collective-permute-start.1 = (f32[64,1024]{1,0:T(8,128)S(1)}, f32[64,1024]{1,0:T(8,128)S(1)}, u32[]{:S(2)}, u32[]{:S(2)}) collective-permute-start(f32[64,1024]{1,0:T(8,128)S(1)} %copy-done), channel_id=1, source_target_pairs={{0,384},{64,448},{128,0},{192,64},{256,128},{320,192},{384,256},{4... | collective-permute-start | bytes 786440 | tf_op jit(solution)/shard_map/ppermute | solution.py:173
  20.7 21.0 %collective-permute-start = (f32[64,1024]{1,0:T(8,128)S(1)}, f32[64,1024]{1,0:T(8,128)S(1)}, u32[]{:S(2)}, u32[]{:S(2)}) collective-permute-start(f32[64,1024]{1,0:T(8,128)S(1)} %copy-done), channel_id=1, source_target_pairs={{0,448},{64,0},{128,64},{192,128},{256,192},{320,256},{384,320},{4... | collective-permute-start | bytes 786440 | tf_op jit(solution)/shard_map/ppermute | solution.py:173
  25.0 19.6 %collective-permute-start.5 = (f32[64,1024]{1,0:T(8,128)S(1)}, f32[64,1024]{1,0:T(8,128)S(1)}, u32[]{:S(2)}, u32[]{:S(2)}) collective-permute-start(f32[64,1024]{1,0:T(8,128)S(1)} %copy-done), channel_id=1, source_target_pairs={{0,64},{64,128},{128,192},{192,256},{256,320},{320,384},{384,448},... | collective-permute-start | bytes 786440 | tf_op jit(solution)/shard_map/ppermute | solution.py:173
  26.9 17.6 %collective-permute-start.6 = (f32[32,1024]{1,0:T(8,128)S(1)}, f32[32,1024]{1,0:T(8,128)S(1)}, u32[]{:S(2)}, u32[]{:S(2)}) collective-permute-start(f32[32,1024]{1,0:T(8,128)S(1)} %slice.16), channel_id=1, source_target_pairs={{0,128},{64,192},{128,256},{192,320},{256,384},{320,448},{384,0},{... | collective-permute-start | bytes 393224 | tf_op jit(solution)/shard_map/ppermute | solution.py:173
  31.6 13.0 %collective-permute-start.7 = (f32[32,1024]{1,0:T(8,128)S(1)}, f32[32,1024]{1,0:T(8,128)S(1)}, u32[]{:S(2)}, u32[]{:S(2)}) collective-permute-start(f32[32,1024]{1,0:T(8,128)S(1)} %slice.17), channel_id=1, source_target_pairs={{0,384},{64,448},{128,0},{192,64},{256,128},{320,192},{384,256},{4... | collective-permute-start | bytes 393224 | tf_op jit(solution)/shard_map/ppermute | solution.py:173
  36.8 9.4 %collective-permute-start.4 = (f32[64,1024]{1,0:T(8,128)S(1)}, f32[64,1024]{1,0:T(8,128)S(1)}, u32[]{:S(2)}, u32[]{:S(2)}) collective-permute-start(f32[64,1024]{1,0:T(8,128)S(1)} %collective-permute-done.3.refs_7_), channel_id=1, source_target_pairs={{0,64},{64,128},{128,192},{192,256},{256,320},{320,384},{384,448},... | collective-permute-start | bytes 786440 | tf_op jit(solution)/shard_map/ppermute | solution.py:173
  51.9 16.4 %all-to-all-start.1 = ((f32[4,64,1024]{2,1,0:T(8,128)}), f32[4,64,1024]{2,1,0:T(8,128)S(1)}, u32[]{:S(2)}, u32[]{:S(2)}) async-start(f32[4,64,1024]{2,1,0:T(8,128)} %pack.1), calls=%async_computation.1 | async-start | bytes 2097152 | tf_op jit(solution)/shard_map/all_to_all | solution.py:21
  75.7 17.7 %collective-permute-start.10 = (f32[2,64,1024]{2,1,0:T(8,128)S(1)}, f32[2,64,1024]{2,1,0:T(8,128)S(1)}, u32[]{:S(2)}, u32[]{:S(2)}) collective-permute-start(f32[2,64,1024]{2,1,0:T(8,128)S(1)} %pad_maximum_fusion.1), channel_id=1, source_target_pairs={{0,4},{1,13},{2,6},{3,15},{4,8},{5,1},{6,10},{7,3},{8,12},{9,5},{1... | collective-permute-start | bytes 1572872 | tf_op jit(solution)/shard_map/ppermute | solution.py:264
  81.6 57.2 %all-to-all-start.2 = ((f32[4,512,384]{2,1,0:T(8,128)}), f32[4,512,384]{2,1,0:T(8,128)}, u32[]{:S(2)}, u32[]{:S(2)}) async-start(f32[4,512,384]{2,1,0:T(8,128)} %copies.1), calls=%async_computation.2 | async-start | bytes 6291456 | tf_op jit(solution)/shard_map/all_to_all | solution.py:21
  86.3 17.3 %collective-permute-start.9 = (f32[2,64,1024]{2,1,0:T(8,128)S(1)}, f32[2,64,1024]{2,1,0:T(8,128)S(1)}, u32[]{:S(2)}, u32[]{:S(2)}) collective-permute-start(f32[2,64,1024]{2,1,0:T(8,128)S(1)} %pad_maximum_fusion.1), channel_id=1, source_target_pairs={{0,2},{1,15},{2,4},{3,1},{4,6},{5,3},{6,8},{7,5},{8,10},{9,7},{10,... | collective-permute-start | bytes 1572872 | tf_op jit(solution)/shard_map/ppermute | solution.py:264
  93.4 12.6 %collective-permute-start.11 = (f32[2,64,1024]{2,1,0:T(8,128)S(1)}, f32[2,64,1024]{2,1,0:T(8,128)S(1)}, u32[]{:S(2)}, u32[]{:S(2)}) collective-permute-start(f32[2,64,1024]{2,1,0:T(8,128)S(1)} %collective-permute-done.10), channel_id=1, source_target_pairs={{0,2},{1,15},{2,4},{3,1},{4,6},{5,3},{6,8},{7,5},{8,10},{9,7},{10,... | collective-permute-start | bytes 1572872 | tf_op jit(solution)/shard_map/ppermute | solution.py:264
  97.6 12.7 %collective-permute-start.15 = (f32[64,1024]{1,0:T(8,128)S(1)}, f32[64,1024]{1,0:T(8,128)S(1)}, u32[]{:S(2)}, u32[]{:S(2)}) collective-permute-start(f32[64,1024]{1,0:T(8,128)S(1)} %slice_bitcast_fusion), channel_id=1, source_target_pairs={{0,4},{1,13},{2,6},{3,15},{4,8},{5,1},{6,10},{7,3},{8,12},{9,5},{1... | collective-permute-start | bytes 786440 | tf_op jit(solution)/shard_map/ppermute | solution.py:264
  101.4 14.9 %collective-permute-start.13 = (f32[2,64,1024]{2,1,0:T(8,128)S(1)}, f32[2,64,1024]{2,1,0:T(8,128)}, u32[]{:S(2)}, u32[]{:S(2)}) collective-permute-start(f32[2,64,1024]{2,1,0:T(8,128)S(1)} %collective-permute-done.10), channel_id=1, source_target_pairs={{0,1},{1,0},{2,3},{3,2},{4,5},{5,4},{6,7},{7,6},{8,9},{9,8},{10,11... | collective-permute-start | bytes 1572872 | tf_op jit(solution)/shard_map/ppermute | solution.py:256
  103.6 12.6 %collective-permute-start.12 = (f32[2,64,1024]{2,1,0:T(8,128)S(1)}, f32[2,64,1024]{2,1,0:T(8,128)S(1)}, u32[]{:S(2)}, u32[]{:S(2)}) collective-permute-start(f32[2,64,1024]{2,1,0:T(8,128)S(1)} %collective-permute-done.9), channel_id=1, source_target_pairs={{0,1},{1,0},{2,3},{3,2},{4,5},{5,4},{6,7},{7,6},{8,9},{9,8},{10,11... | collective-permute-start | bytes 1572872 | tf_op jit(solution)/shard_map/ppermute | solution.py:256
  106.0 10.3 %collective-permute-start.14 = (f32[2,64,1024]{2,1,0:T(8,128)S(1)}, f32[2,64,1024]{2,1,0:T(8,128)}, u32[]{:S(2)}, u32[]{:S(2)}) collective-permute-start(f32[2,64,1024]{2,1,0:T(8,128)S(1)} %collective-permute-done.11), channel_id=1, source_target_pairs={{0,1},{1,0},{2,3},{3,2},{4,5},{5,4},{6,7},{7,6},{8,9},{9,8},{10,11... | collective-permute-start | bytes 1572872 | tf_op jit(solution)/shard_map/ppermute | solution.py:256
  129.3 13.9 %collective-permute-start.17 = (f32[256,384]{1,0:T(8,128)}, f32[256,384]{1,0:T(8,128)S(1)}, u32[]{:S(2)}, u32[]{:S(2)}) collective-permute-start(f32[256,384]{1,0:T(8,128)} %get-tuple-element.67), channel_id=1, source_target_pairs={{0,16},{16,32},{32,48},{48,0},{1,17},{17,33},{33,49},{49,1},{2,18}... | collective-permute-start | bytes 1179656 | tf_op jit(solution)/shard_map/ppermute | solution.py:314
  131.6 19.6 %collective-permute-start.18 = (f32[256,384]{1,0:T(8,128)}, f32[256,384]{1,0:T(8,128)S(1)}, u32[]{:S(2)}, u32[]{:S(2)}) collective-permute-start(f32[256,384]{1,0:T(8,128)} %get-tuple-element.68), channel_id=1, source_target_pairs={{0,32},{16,48},{32,0},{48,16},{1,33},{17,49},{33,1},{49,17},{2,34}... | collective-permute-start | bytes 1179656 | tf_op jit(solution)/shard_map/ppermute | solution.py:314
  135.7 18.1 %collective-permute-start.19 = (f32[256,384]{1,0:T(8,128)}, f32[256,384]{1,0:T(8,128)S(1)}, u32[]{:S(2)}, u32[]{:S(2)}) collective-permute-start(f32[256,384]{1,0:T(8,128)} %get-tuple-element.69), channel_id=1, source_target_pairs={{0,48},{16,0},{32,16},{48,32},{1,49},{17,1},{33,17},{49,33},{2,50}... | collective-permute-start | bytes 1179656 | tf_op jit(solution)/shard_map/ppermute | solution.py:314
  154.6 17.3 %all-to-all-start.3 = ((f32[8,32,384]{2,1,0:T(8,128)}), f32[8,32,384]{2,1,0:T(8,128)S(1)}, u32[]{:S(2)}, u32[]{:S(2)}) async-start(f32[8,32,384]{2,1,0:T(8,128)} %bitcast.20), calls=%async_computation.3 | async-start | bytes 786432 | tf_op jit(solution)/shard_map/all_to_all | solution.py:21
  159.0 13.1 %collective-permute-start.20 = (f32[256,384]{1,0:T(8,128)S(1)}, f32[256,384]{1,0:T(8,128)S(1)}, u32[]{:S(2)}, u32[]{:S(2)}) collective-permute-start(f32[256,384]{1,0:T(8,128)S(1)} %copy-done.4), channel_id=1, source_target_pairs={{0,16},{16,32},{32,48},{48,0},{1,17},{17,33},{33,49},{49,1},{2,18}... | collective-permute-start | bytes 1179656 | tf_op jit(solution)/shard_map/ppermute | solution.py:314
  164.0 18.1 %collective-permute-start.21 = (f32[256,384]{1,0:T(8,128)S(1)}, f32[256,384]{1,0:T(8,128)S(1)}, u32[]{:S(2)}, u32[]{:S(2)}) collective-permute-start(f32[256,384]{1,0:T(8,128)S(1)} %get-tuple-element.73), channel_id=1, source_target_pairs={{0,32},{16,48},{32,0},{48,16},{1,33},{17,49},{33,1},{49,17},{2,34}... | collective-permute-start | bytes 1179656 | tf_op jit(solution)/shard_map/ppermute | solution.py:314
  167.1 16.4 %collective-permute-start.22 = (f32[256,384]{1,0:T(8,128)S(1)}, f32[256,384]{1,0:T(8,128)S(1)}, u32[]{:S(2)}, u32[]{:S(2)}) collective-permute-start(f32[256,384]{1,0:T(8,128)S(1)} %get-tuple-element.74), channel_id=1, source_target_pairs={{0,48},{16,0},{32,16},{48,32},{1,49},{17,1},{33,17},{49,33},{2,50}... | collective-permute-start | bytes 1179656 | tf_op jit(solution)/shard_map/ppermute | solution.py:314
  (14 other events, 150.8 us)

commit v9 on v8

--- a/solution.py
+++ b/solution.py
@@ -117,15 +117,17 @@
         copies[level, :, cut:] = second
 
 
-def solve_kernel(core, reduced, inverse_lo, inverse_hi, kept, other, high, low):
+def solve_kernel(core, reduced, inverse_lo, inverse_hi, kept, other, *parts):
+    cut = inverse_lo.shape[1]
+
     @pl.when(pl.program_id(0) == 0)
     def _():
-        high[...], low[...] = split(reduced[...])
+        for at, piece in enumerate((reduced[:, :cut], reduced[:, cut:])):
+            parts[2 * at][...], parts[2 * at + 1][...] = split(piece)
 
     _, tall, part, span = kept.shape
-    cut = inverse_lo.shape[1]
-    result = product((high[:, :cut], low[:, :cut]), split(inverse_lo[0]))
-    result = result + product((high[:, cut:], low[:, cut:]), split(inverse_hi[0]))
+    result = product((parts[0][...], parts[1][...]), split(inverse_lo[0]))
+    result = result + product((parts[2][...], parts[3][...]), split(inverse_hi[0]))
     result = result.reshape(tall, 2, part, span)
     first, second = result[:, 0], result[:, 1]
     mine = core[0] == 0
@@ -164,7 +166,7 @@
     me = lax.axis_index(ROWS)
 
     half = pivots // 2
-    cut = pivots // 3
+    cut = pivots // 4
     core = lax.axis_index("c")
     first = child_start - me * span
 
@@ -299,7 +301,7 @@
             ],
         ),
         out_shape=(jax.ShapeDtypeStruct((quarter, half), jnp.float32),) * (2 * across),
-        compiler_params=grant(48),
+        compiler_params=grant(52),
         cost_estimate=pl.CostEstimate(
             flops=6 * total * width * pivots,
             bytes_accessed=4 * (total * width + width * pivots + total * pivots),
@@ -348,8 +350,8 @@
         ],
         out_specs=(pl.BlockSpec((1, tall, part, span), lambda i: (i, 0, 0, 0)),) * 2,
         scratch_shapes=[
-            pltpu.VMEM((quarter, pivots), jnp.bfloat16),
-            pltpu.VMEM((quarter, pivots), jnp.bfloat16),
+            pltpu.VMEM((quarter, size), jnp.bfloat16)
+            for size in (cut, cut, pivots - cut, pivots - cut)
         ],
         compiler_params=grant(60),
         name="solve",

time: 278 us -> 282 us (1.014)
    ppermute x4, waiting for transfers between devices: 6.43 us -> 11.5 us  [apart(): return lax.ppermute(value, PIV, pairs)]
  transfers between devices with their start and end apart: 28 -> 28, of which waited for: 17 -> 15; matrix products, arithmetic and copies ran while one was open for 1% -> 2% of each run, Pallas kernels for 7% -> 8%
where the time goes in v9:
time: 282 us; the launch traced here: 277 us
  starting transfers between devices  115 us (41%)
  blocking collectives  71.7 us (25%)
  waiting for transfers between devices  47 us (17%)
  Pallas kernels  35.1 us (12%)
  other arithmetic  3.26 us (1%)
    all_to_all x3, blocking collectives, exchange(): return lax.all_to_all(value, axes, split_axis=0, concat_axis=0, tiled=True)  71.7 us
    ppermute x8, starting transfers between devices, ring(): lax.ppermute(value, axis, [(i, (i + hops) % length) for i in range(length)])  35.2 us
    ppermute x6, waiting for transfers between devices, across_sent(): lax.ppermute(shares[k], 'x', [(i, (i + k) % across) for i in range(across)])  25.1 us
    ppermute x6, starting transfers between devices, across_sent(): lax.ppermute(shares[k], 'x', [(i, (i + k) % across) for i in range(across)])  22.3 us
    ppermute x6, starting transfers between devices, swap(): return lax.ppermute(value, 'c', [(0, 1), (1, 0)])  21.4 us
    all_to_all x4, starting transfers between devices, exchange(): return lax.all_to_all(value, axes, split_axis=0, concat_axis=0, tiled=True)  19.4 us
    ppermute x4, starting transfers between devices, apart(): return lax.ppermute(value, PIV, pairs)  16.8 us
    ppermute x4, waiting for transfers between devices, apart(): return lax.ppermute(value, PIV, pairs)  11.5 us
  transfers between devices with their start and end apart: 28, of which 15 were waited for; matrix products, arithmetic and copies ran while one was open for 2% of the time, Pallas kernels for 8%

profile of v9, /device:TPU:1, one launch (start us, length us, event | category | flops | bytes accessed | tf_op | source)
XLA Modules:
  0.0 276.9 jit_solution(34851840660670492)
XLA Ops:
  2.6 5.0 %all-to-all-start = ((f32[4,200,384]{2,1,0:T(8,128)}), f32[4,200,384]{2,1,0:T(8,128)S(1)}, u32[]{:S(2)}, u32[]{:S(2)}) async-start(f32[4,200,384]{2,1,0:T(8,128)} %repeat.1), calls=%async_computation | async-start | bytes 2457600 | tf_op jit(solution)/shard_map/all_to_all | solution.py:21
  7.6 5.8 %collective-permute-start.3 = (f32[64,1024]{1,0:T(8,128)S(1)}, f32[64,1024]{1,0:T(8,128)S(1)}, u32[]{:S(2)}, u32[]{:S(2)}) collective-permute-start(f32[64,1024]{1,0:T(8,128)S(1)} %copy-done), channel_id=1, source_target_pairs={{0,128},{64,192},{128,256},{192,320},{256,384},{320,448},{384,0},{... | collective-permute-start | bytes 786440 | tf_op jit(solution)/shard_map/ppermute | solution.py:175
  13.4 6.8 %collective-permute-start.1 = (f32[64,1024]{1,0:T(8,128)S(1)}, f32[64,1024]{1,0:T(8,128)S(1)}, u32[]{:S(2)}, u32[]{:S(2)}) collective-permute-start(f32[64,1024]{1,0:T(8,128)S(1)} %copy-done), channel_id=1, source_target_pairs={{0,384},{64,448},{128,0},{192,64},{256,128},{320,192},{384,256},{4... | collective-permute-start | bytes 786440 | tf_op jit(solution)/shard_map/ppermute | solution.py:175
  20.1 4.3 %collective-permute-start = (f32[64,1024]{1,0:T(8,128)S(1)}, f32[64,1024]{1,0:T(8,128)S(1)}, u32[]{:S(2)}, u32[]{:S(2)}) collective-permute-start(f32[64,1024]{1,0:T(8,128)S(1)} %copy-done), channel_id=1, source_target_pairs={{0,448},{64,0},{128,64},{192,128},{256,192},{320,256},{384,320},{4... | collective-permute-start | bytes 786440 | tf_op jit(solution)/shard_map/ppermute | solution.py:175
  26.4 4.3 %collective-permute-start.6 = (f32[32,1024]{1,0:T(8,128)S(1)}, f32[32,1024]{1,0:T(8,128)S(1)}, u32[]{:S(2)}, u32[]{:S(2)}) collective-permute-start(f32[32,1024]{1,0:T(8,128)S(1)} %slice.16), channel_id=1, source_target_pairs={{0,128},{64,192},{128,256},{192,320},{256,384},{320,448},{384,0},{... | collective-permute-start | bytes 393224 | tf_op jit(solution)/shard_map/ppermute | solution.py:175
  31.6 5.0 %collective-permute-start.7 = (f32[32,1024]{1,0:T(8,128)}, f32[32,1024]{1,0:T(8,128)S(1)}, u32[]{:S(2)}, u32[]{:S(2)}) collective-permute-start(f32[32,1024]{1,0:T(8,128)} %slice.17), channel_id=1, source_target_pairs={{0,384},{64,448},{128,0},{192,64},{256,128},{320,192},{384,256},{4... | collective-permute-start | bytes 393224 | tf_op jit(solution)/shard_map/ppermute | solution.py:175
  36.5 5.2 %collective-permute-start.4 = (f32[64,1024]{1,0:T(8,128)S(1)}, f32[64,1024]{1,0:T(8,128)S(1)}, u32[]{:S(2)}, u32[]{:S(2)}) collective-permute-start(f32[64,1024]{1,0:T(8,128)S(1)} %collective-permute-done.3.refs_7_), channel_id=1, source_target_pairs={{0,64},{64,128},{128,192},{192,256},{256,320},{320,384},{384,448},... | collective-permute-start | bytes 786440 | tf_op jit(solution)/shard_map/ppermute | solution.py:175
  55.9 6.5 %copies.1 = f32[4,576,384]{2,1,0:T(8,128)} custom-call(f32[768,384]{1,0:T(8,128)} %inverse.2), custom_call_target="tpu_custom_call" | custom-call | flops 294912 | bytes 5898240 | tf_op jit(solution)/shard_map/copies/pallas_call | solution.py:208
  63.4 4.3 %halve.1 = (bf16[1024,768]{1,0:T(8,128)(2,1)}, bf16[1024,768]{1,0:T(8,128)(2,1)}) custom-call(f32[1024,768]{1,0:T(8,128)} %value), custom_call_target="tpu_custom_call" | custom-call | flops 3145728 | bytes 6291456 | tf_op jit(solution)/shard_map/halve/pallas_call | solution.py:220
  69.9 4.8 %collective-permute-start.8 = (f32[64,1024]{1,0:T(8,128)S(1)}, f32[64,1024]{1,0:T(8,128)S(1)}, u32[]{:S(2)}, u32[]{:S(2)}) collective-permute-start(f32[64,1024]{1,0:T(8,128)S(1)} %pick.1), channel_id=1, source_target_pairs={{0,1},{1,0},{2,3},{3,2},{4,5},{5,4},{6,7},{7,6},{8,9},{9,8},{10,11... | collective-permute-start | bytes 786440 | tf_op jit(solution)/shard_map/ppermute | solution.py:258
  74.7 4.7 %all-to-all-start.2 = ((f32[4,576,384]{2,1,0:T(8,128)}), f32[4,576,384]{2,1,0:T(8,128)}, u32[]{:S(2)}, u32[]{:S(2)}) async-start(f32[4,576,384]{2,1,0:T(8,128)} %copies.1), calls=%async_computation.2 | async-start | bytes 7077888 | tf_op jit(solution)/shard_map/all_to_all | solution.py:21
  79.5 5.9 %collective-permute-start.10 = (f32[2,64,1024]{2,1,0:T(8,128)S(1)}, f32[2,64,1024]{2,1,0:T(8,128)S(1)}, u32[]{:S(2)}, u32[]{:S(2)}) collective-permute-start(f32[2,64,1024]{2,1,0:T(8,128)S(1)} %pad_maximum_fusion.1), channel_id=1, source_target_pairs={{0,4},{1,13},{2,6},{3,15},{4,8},{5,1},{6,10},{7,3},{8,12},{9,5},{1... | collective-permute-start | bytes 1572872 | tf_op jit(solution)/shard_map/ppermute | solution.py:266
  88.4 8.7 %collective-permute-done.10 = f32[2,64,1024]{2,1,0:T(8,128)S(1)} collective-permute-done((f32[2,64,1024]{2,1,0:T(8,128)S(1)}, f32[2,64,1024]{2,1,0:T(8,128)S(1)}, u32[]{:S(2)}, u32[]{:S(2)}) %collective-permute-start.10) | collective-permute-done | bytes 524320 | tf_op jit(solution)/shard_map/ppermute | solution.py:266
  119.9 11.0 %couple.1 = (f32[256,384]{1,0:T(8,128)S(1)}, f32[256,384]{1,0:T(8,128)S(1)}, f32[256,384]{1,0:T(8,128)S(1)}, f32[256,384]{1,0:T(8,128)}, f32[256,384]{1,0:T(8,12...) custom-call(s32[4]{0:T(128)S(1)} %pad_add_fusion.refs_0_, ...), custom_call_target="tpu_custom_call" | custom-call | flops 4831838208 | bytes 10485760 | tf_op jit(solution)/shard_map/couple/pallas_call | solution.py:281
  134.7 4.3 %collective-permute-start.18 = (f32[256,384]{1,0:T(8,128)S(1)}, f32[256,384]{1,0:T(8,128)S(1)}, u32[]{:S(2)}, u32[]{:S(2)}) collective-permute-start(f32[256,384]{1,0:T(8,128)S(1)} %get-tuple-element.68), channel_id=1, source_target_pairs={{0,32},{16,48},{32,0},{48,16},{1,33},{17,49},{33,1},{49,17},{2,34}... | collective-permute-start | bytes 1179656 | tf_op jit(solution)/shard_map/ppermute | solution.py:316
  145.0 9.3 %collective-permute-done.18 = f32[256,384]{1,0:T(8,128)S(1)} collective-permute-done((f32[256,384]{1,0:T(8,128)S(1)}, f32[256,384]{1,0:T(8,128)S(1)}, u32[]{:S(2)}, u32[]{:S(2)}) %collective-permute-start.18) | collective-permute-done | bytes 393248 | tf_op jit(solution)/shard_map/ppermute | solution.py:316
  156.5 5.8 %all-to-all-start.3 = ((f32[8,32,384]{2,1,0:T(8,128)}), f32[8,32,384]{2,1,0:T(8,128)S(1)}, u32[]{:S(2)}, u32[]{:S(2)}) async-start(f32[8,32,384]{2,1,0:T(8,128)} %bitcast.20), calls=%async_computation.3 | async-start | bytes 786432 | tf_op jit(solution)/shard_map/all_to_all | solution.py:21
  162.3 5.0 %collective-permute-start.20 = (f32[256,384]{1,0:T(8,128)}, f32[256,384]{1,0:T(8,128)S(1)}, u32[]{:S(2)}, u32[]{:S(2)}) collective-permute-start(f32[256,384]{1,0:T(8,128)} %get-tuple-element.72), channel_id=1, source_target_pairs={{0,16},{16,32},{32,48},{48,0},{1,17},{17,33},{33,49},{49,1},{2,18}... | collective-permute-start | bytes 1179656 | tf_op jit(solution)/shard_map/ppermute | solution.py:316
  175.6 9.9 %collective-permute-done.21 = f32[256,384]{1,0:T(8,128)S(1)} collective-permute-done((f32[256,384]{1,0:T(8,128)S(1)}, f32[256,384]{1,0:T(8,128)S(1)}, u32[]{:S(2)}, u32[]{:S(2)}) %collective-permute-start.21) | collective-permute-done | bytes 393248 | tf_op jit(solution)/shard_map/ppermute | solution.py:316
  186.8 18.9 %all_to_all.35.pieces_b = f32[8,32,384]{2,1,0:T(8,128)S(1)} all-to-all(f32[8,32,384]{2,1,0:T(8,128)S(1)} %bitcast.43), channel_id=1, replica_groups=mesh['z'=8,'x'=4,'y'=8,'c'=2] {'z'}, dimensions={0} | all-to-all | bytes 786432 | tf_op jit(solution)/shard_map/all_to_all | solution.py:21
  205.8 22.6 %all_to_all.36 = f32[8,32,768]{2,1,0:T(8,128)} all-to-all(f32[8,32,768]{2,1,0:T(8,128)S(1)} %join.1), channel_id=1, replica_groups=mesh['z'=8,'x'=4,'y'=8,'c'=2] {'z'}, dimensions={0} | all-to-all | bytes 1572864 | tf_op jit(solution)/shard_map/all_to_all | solution.py:21
  228.4 6.9 %solve.1 = (f32[4,8,16,384]{3,2,1,0:T(8,128)}, f32[4,8,16,384]{3,2,1,0:T(8,128)}) custom-call(s32[1]{0:T(128)} %bitcast.core, f32[256,768]{1,0:T(8,128)} %bitcast.42, f32[4,200,384]{2,1,0:T(8,128)} %copy-done.3, f32[4,576,384]{2,1,0:T(8,128)} %all-to-all-done.2.inverse_hi), custom_call_target="tpu_custom_call" | custom-call | tf_op jit(solution)/shard_map/solve/pallas_call | solution.py:341
  235.3 6.6 %collective-permute-start.23 = (f32[4,8,16,384]{3,2,1,0:T(8,128)}, f32[4,8,16,384]{3,2,1,0:T(8,128)S(1)}, u32[]{:S(2)}, u32[]{:S(2)}) collective-permute-start(f32[4,8,16,384]{3,2,1,0:T(8,128)} %get-tuple-element.78), channel_id=1, source_target_pairs={{0,1},{1,0},{2,3},{3,2},{4,5},{5,4},{6,7},{7,6},{8,9},{9,8},{10,11... | collective-permute-start | bytes 2359304 | tf_op jit(solution)/shard_map/ppermute | solution.py:258
  245.2 30.3 %all_to_all.37 = f32[32,16,384]{2,1,0:T(8,128)S(1)} all-to-all(f32[32,16,384]{2,1,0:T(8,128)S(1)} %bitcast.41), channel_id=1, replica_groups=mesh['z'=8,'x'=4,'y'=8,'c'=2] {'x','y'}, dimensions={0} | all-to-all | bytes 1572864 | tf_op jit(solution)/shard_map/all_to_all | solution.py:21
  (86 shorter events, 74.7 us)
Async XLA Ops:
  2.6 41.1 %all-to-all-start = ((f32[4,200,384]{2,1,0:T(8,128)}), f32[4,200,384]{2,1,0:T(8,128)S(1)}, u32[]{:S(2)}, u32[]{:S(2)}) async-start(f32[4,200,384]{2,1,0:T(8,128)} %repeat.1), calls=%async_computation | async-start | bytes 2457600 | tf_op jit(solution)/shard_map/all_to_all | solution.py:21
  7.6 18.8 %collective-permute-start.3 = (f32[64,1024]{1,0:T(8,128)S(1)}, f32[64,1024]{1,0:T(8,128)S(1)}, u32[]{:S(2)}, u32[]{:S(2)}) collective-permute-start(f32[64,1024]{1,0:T(8,128)S(1)} %copy-done), channel_id=1, source_target_pairs={{0,128},{64,192},{128,256},{192,320},{256,384},{320,448},{384,0},{... | collective-permute-start | bytes 786440 | tf_op jit(solution)/shard_map/ppermute | solution.py:175
  13.4 17.5 %collective-permute-start.1 = (f32[64,1024]{1,0:T(8,128)S(1)}, f32[64,1024]{1,0:T(8,128)S(1)}, u32[]{:S(2)}, u32[]{:S(2)}) collective-permute-start(f32[64,1024]{1,0:T(8,128)S(1)} %copy-done), channel_id=1, source_target_pairs={{0,384},{64,448},{128,0},{192,64},{256,128},{320,192},{384,256},{4... | collective-permute-start | bytes 786440 | tf_op jit(solution)/shard_map/ppermute | solution.py:175
  20.1 21.6 %collective-permute-start = (f32[64,1024]{1,0:T(8,128)S(1)}, f32[64,1024]{1,0:T(8,128)S(1)}, u32[]{:S(2)}, u32[]{:S(2)}) collective-permute-start(f32[64,1024]{1,0:T(8,128)S(1)} %copy-done), channel_id=1, source_target_pairs={{0,448},{64,0},{128,64},{192,128},{256,192},{320,256},{384,320},{4... | collective-permute-start | bytes 786440 | tf_op jit(solution)/shard_map/ppermute | solution.py:175
  24.4 19.5 %collective-permute-start.5 = (f32[64,1024]{1,0:T(8,128)S(1)}, f32[64,1024]{1,0:T(8,128)S(1)}, u32[]{:S(2)}, u32[]{:S(2)}) collective-permute-start(f32[64,1024]{1,0:T(8,128)S(1)} %copy-done), channel_id=1, source_target_pairs={{0,64},{64,128},{128,192},{192,256},{256,320},{320,384},{384,448},... | collective-permute-start | bytes 786440 | tf_op jit(solution)/shard_map/ppermute | solution.py:175
  26.4 17.5 %collective-permute-start.6 = (f32[32,1024]{1,0:T(8,128)S(1)}, f32[32,1024]{1,0:T(8,128)S(1)}, u32[]{:S(2)}, u32[]{:S(2)}) collective-permute-start(f32[32,1024]{1,0:T(8,128)S(1)} %slice.16), channel_id=1, source_target_pairs={{0,128},{64,192},{128,256},{192,320},{256,384},{320,448},{384,0},{... | collective-permute-start | bytes 393224 | tf_op jit(solution)/shard_map/ppermute | solution.py:175
  31.6 12.4 %collective-permute-start.7 = (f32[32,1024]{1,0:T(8,128)}, f32[32,1024]{1,0:T(8,128)S(1)}, u32[]{:S(2)}, u32[]{:S(2)}) collective-permute-start(f32[32,1024]{1,0:T(8,128)} %slice.17), channel_id=1, source_target_pairs={{0,384},{64,448},{128,0},{192,64},{256,128},{320,192},{384,256},{4... | collective-permute-start | bytes 393224 | tf_op jit(solution)/shard_map/ppermute | solution.py:175
  36.5 9.7 %collective-permute-start.4 = (f32[64,1024]{1,0:T(8,128)S(1)}, f32[64,1024]{1,0:T(8,128)S(1)}, u32[]{:S(2)}, u32[]{:S(2)}) collective-permute-start(f32[64,1024]{1,0:T(8,128)S(1)} %collective-permute-done.3.refs_7_), channel_id=1, source_target_pairs={{0,64},{64,128},{128,192},{192,256},{256,320},{320,384},{384,448},... | collective-permute-start | bytes 786440 | tf_op jit(solution)/shard_map/ppermute | solution.py:175
  51.9 17.4 %all-to-all-start.1 = ((f32[4,64,1024]{2,1,0:T(8,128)}), f32[4,64,1024]{2,1,0:T(8,128)S(1)}, u32[]{:S(2)}, u32[]{:S(2)}) async-start(f32[4,64,1024]{2,1,0:T(8,128)} %pack.1), calls=%async_computation.1 | async-start | bytes 2097152 | tf_op jit(solution)/shard_map/all_to_all | solution.py:21
  69.9 9.6 %collective-permute-start.8 = (f32[64,1024]{1,0:T(8,128)S(1)}, f32[64,1024]{1,0:T(8,128)S(1)}, u32[]{:S(2)}, u32[]{:S(2)}) collective-permute-start(f32[64,1024]{1,0:T(8,128)S(1)} %pick.1), channel_id=1, source_target_pairs={{0,1},{1,0},{2,3},{3,2},{4,5},{5,4},{6,7},{7,6},{8,9},{9,8},{10,11... | collective-permute-start | bytes 786440 | tf_op jit(solution)/shard_map/ppermute | solution.py:258
  74.7 67.3 %all-to-all-start.2 = ((f32[4,576,384]{2,1,0:T(8,128)}), f32[4,576,384]{2,1,0:T(8,128)}, u32[]{:S(2)}, u32[]{:S(2)}) async-start(f32[4,576,384]{2,1,0:T(8,128)} %copies.1), calls=%async_computation.2 | async-start | bytes 7077888 | tf_op jit(solution)/shard_map/all_to_all | solution.py:21
  79.5 17.6 %collective-permute-start.10 = (f32[2,64,1024]{2,1,0:T(8,128)S(1)}, f32[2,64,1024]{2,1,0:T(8,128)S(1)}, u32[]{:S(2)}, u32[]{:S(2)}) collective-permute-start(f32[2,64,1024]{2,1,0:T(8,128)S(1)} %pad_maximum_fusion.1), channel_id=1, source_target_pairs={{0,4},{1,13},{2,6},{3,15},{4,8},{5,1},{6,10},{7,3},{8,12},{9,5},{1... | collective-permute-start | bytes 1572872 | tf_op jit(solution)/shard_map/ppermute | solution.py:266
  85.4 21.7 %collective-permute-start.9 = (f32[2,64,1024]{2,1,0:T(8,128)S(1)}, f32[2,64,1024]{2,1,0:T(8,128)S(1)}, u32[]{:S(2)}, u32[]{:S(2)}) collective-permute-start(f32[2,64,1024]{2,1,0:T(8,128)S(1)} %pad_maximum_fusion.1), channel_id=1, source_target_pairs={{0,2},{1,15},{2,4},{3,1},{4,6},{5,3},{6,8},{7,5},{8,10},{9,7},{10,... | collective-permute-start | bytes 1572872 | tf_op jit(solution)/shard_map/ppermute | solution.py:266
  97.2 12.7 %collective-permute-start.11 = (f32[2,64,1024]{2,1,0:T(8,128)S(1)}, f32[2,64,1024]{2,1,0:T(8,128)S(1)}, u32[]{:S(2)}, u32[]{:S(2)}) collective-permute-start(f32[2,64,1024]{2,1,0:T(8,128)S(1)} %collective-permute-done.10), channel_id=1, source_target_pairs={{0,2},{1,15},{2,4},{3,1},{4,6},{5,3},{6,8},{7,5},{8,10},{9,7},{10,... | collective-permute-start | bytes 1572872 | tf_op jit(solution)/shard_map/ppermute | solution.py:266
  101.4 12.8 %collective-permute-start.15 = (f32[64,1024]{1,0:T(8,128)S(1)}, f32[64,1024]{1,0:T(8,128)S(1)}, u32[]{:S(2)}, u32[]{:S(2)}) collective-permute-start(f32[64,1024]{1,0:T(8,128)S(1)} %slice_bitcast_fusion), channel_id=1, source_target_pairs={{0,4},{1,13},{2,6},{3,15},{4,8},{5,1},{6,10},{7,3},{8,12},{9,5},{1... | collective-permute-start | bytes 786440 | tf_op jit(solution)/shard_map/ppermute | solution.py:266
  105.1 13.9 %collective-permute-start.13 = (f32[2,64,1024]{2,1,0:T(8,128)S(1)}, f32[2,64,1024]{2,1,0:T(8,128)S(1)}, u32[]{:S(2)}, u32[]{:S(2)}) collective-permute-start(f32[2,64,1024]{2,1,0:T(8,128)S(1)} %collective-permute-done.10), channel_id=1, source_target_pairs={{0,1},{1,0},{2,3},{3,2},{4,5},{5,4},{6,7},{7,6},{8,9},{9,8},{10,11... | collective-permute-start | bytes 1572872 | tf_op jit(solution)/shard_map/ppermute | solution.py:258
  107.1 11.9 %collective-permute-start.12 = (f32[2,64,1024]{2,1,0:T(8,128)S(1)}, f32[2,64,1024]{2,1,0:T(8,128)}, u32[]{:S(2)}, u32[]{:S(2)}) collective-permute-start(f32[2,64,1024]{2,1,0:T(8,128)S(1)} %collective-permute-done.9), channel_id=1, source_target_pairs={{0,1},{1,0},{2,3},{3,2},{4,5},{5,4},{6,7},{7,6},{8,9},{9,8},{10,11... | collective-permute-start | bytes 1572872 | tf_op jit(solution)/shard_map/ppermute | solution.py:258
  130.9 14.1 %collective-permute-start.17 = (f32[256,384]{1,0:T(8,128)S(1)}, f32[256,384]{1,0:T(8,128)S(1)}, u32[]{:S(2)}, u32[]{:S(2)}) collective-permute-start(f32[256,384]{1,0:T(8,128)S(1)} %get-tuple-element.67), channel_id=1, source_target_pairs={{0,16},{16,32},{32,48},{48,0},{1,17},{17,33},{33,49},{49,1},{2,18}... | collective-permute-start | bytes 1179656 | tf_op jit(solution)/shard_map/ppermute | solution.py:316
  134.7 19.6 %collective-permute-start.18 = (f32[256,384]{1,0:T(8,128)S(1)}, f32[256,384]{1,0:T(8,128)S(1)}, u32[]{:S(2)}, u32[]{:S(2)}) collective-permute-start(f32[256,384]{1,0:T(8,128)S(1)} %get-tuple-element.68), channel_id=1, source_target_pairs={{0,32},{16,48},{32,0},{48,16},{1,33},{17,49},{33,1},{49,17},{2,34}... | collective-permute-start | bytes 1179656 | tf_op jit(solution)/shard_map/ppermute | solution.py:316
  139.0 16.7 %collective-permute-start.19 = (f32[256,384]{1,0:T(8,128)}, f32[256,384]{1,0:T(8,128)S(1)}, u32[]{:S(2)}, u32[]{:S(2)}) collective-permute-start(f32[256,384]{1,0:T(8,128)} %get-tuple-element.69), channel_id=1, source_target_pairs={{0,48},{16,0},{32,16},{48,32},{1,49},{17,1},{33,17},{49,33},{2,50}... | collective-permute-start | bytes 1179656 | tf_op jit(solution)/shard_map/ppermute | solution.py:316
  156.5 18.8 %all-to-all-start.3 = ((f32[8,32,384]{2,1,0:T(8,128)}), f32[8,32,384]{2,1,0:T(8,128)S(1)}, u32[]{:S(2)}, u32[]{:S(2)}) async-start(f32[8,32,384]{2,1,0:T(8,128)} %bitcast.20), calls=%async_computation.3 | async-start | bytes 786432 | tf_op jit(solution)/shard_map/all_to_all | solution.py:21
  162.3 13.3 %collective-permute-start.20 = (f32[256,384]{1,0:T(8,128)}, f32[256,384]{1,0:T(8,128)S(1)}, u32[]{:S(2)}, u32[]{:S(2)}) collective-permute-start(f32[256,384]{1,0:T(8,128)} %get-tuple-element.72), channel_id=1, source_target_pairs={{0,16},{16,32},{32,48},{48,0},{1,17},{17,33},{33,49},{49,1},{2,18}... | collective-permute-start | bytes 1179656 | tf_op jit(solution)/shard_map/ppermute | solution.py:316
  167.2 18.3 %collective-permute-start.21 = (f32[256,384]{1,0:T(8,128)S(1)}, f32[256,384]{1,0:T(8,128)S(1)}, u32[]{:S(2)}, u32[]{:S(2)}) collective-permute-start(f32[256,384]{1,0:T(8,128)S(1)} %copy-done.11), channel_id=1, source_target_pairs={{0,32},{16,48},{32,0},{48,16},{1,33},{17,49},{33,1},{49,17},{2,34}... | collective-permute-start | bytes 1179656 | tf_op jit(solution)/shard_map/ppermute | solution.py:316
  170.4 16.4 %collective-permute-start.22 = (f32[256,384]{1,0:T(8,128)S(1)}, f32[256,384]{1,0:T(8,128)S(1)}, u32[]{:S(2)}, u32[]{:S(2)}) collective-permute-start(f32[256,384]{1,0:T(8,128)S(1)} %copy-done.10), channel_id=1, source_target_pairs={{0,48},{16,0},{32,16},{48,32},{1,49},{17,1},{33,17},{49,33},{2,50}... | collective-permute-start | bytes 1179656 | tf_op jit(solution)/shard_map/ppermute | solution.py:316
  (17 other events, 307.5 us)

commit v10 on v9

--- a/solution.py
+++ b/solution.py
@@ -68,14 +68,15 @@
     repeated[0] = inverse[...]
 
 
-def halve_kernel(value, high, low):
-    high[...], low[...] = split(value[...])
-
-
 def couple_kernel(slots, where, *rest):
-    pieces, (high, low, placed) = rest[:9], rest[9:12]
-    shares, (rows, total) = rest[12 : 12 + slots], rest[12 + slots :]
+    pieces, (panel, placed) = rest[:10], rest[10:12]
+    shares, (rows, high, low, total) = rest[12 : 12 + slots], rest[12 + slots :]
     step = pl.program_id(0)
+
+    @pl.when(step == 0)
+    def _():
+        high[...], low[...] = split(panel[...])
+
     part = pieces[0].shape[2]
     tall = rows.shape[0] // (2 * part)
     level, core = where[2], where[3]
@@ -85,16 +86,16 @@
         at = lax.rem(level + distance + tall, tall)
         rows[pl.ds(pl.multiple_of((at * 2 + owner) * part, part), part)] = piece[entry, 0]
 
-    own, near, far = pieces[0], pieces[1:4], pieces[4:7]
-    put(own, 0, 0, core)
-    put(own, 1, 0, 1 - core)
+    near, far = pieces[2:5], pieces[5:8]
+    put(pieces[0], 0, 0, core)
+    put(pieces[1], 0, 0, 1 - core)
     for k in range(3):
         put(near[k], 0, -(k + 1) * way, core)
         put(near[k], 1, -(k + 1) * way, 1 - core)
         put(far[k], 0, (k + 1) * way, 1 - core)
         put(far[k], 1, (k + 1) * way, core)
-    put(pieces[7], 0, tall // 2, core)
-    put(pieces[8], 0, tall // 2, 1 - core)
+    put(pieces[8], 0, tall // 2, core)
+    put(pieces[9], 0, tall // 2, 1 - core)
     wide = placed.shape[2]
     total[...] = -product(split(rows[...]), (high[...], low[...]))
     window = pl.ds(pl.multiple_of(where[1] * BLK, BLK), wide)
@@ -201,8 +202,8 @@
         compiler_params=grant(12),
         name="pack",
     )(maps, lax.axis_index("z").reshape(1), *column)
-    sends, inverse_lo, inverse_factor, right_side, lower_panel = lax.optimization_barrier(
-        (sends, inverse_lo, inverse_factor, right_side, lower_panel)
+    sends, inverse_lo, inverse_factor, right_side = lax.optimization_barrier(
+        (sends, inverse_lo, inverse_factor, right_side)
     )
     arrived = exchange(sends, "x")
     rest = pl.pallas_call(
@@ -217,18 +218,6 @@
         ),
         name="copies",
     )(inverse_factor)
-    panel_high, panel_low = pl.pallas_call(
-        halve_kernel,
-        grid=(4,),
-        out_shape=(jax.ShapeDtypeStruct((width, pivots), jnp.bfloat16),) * 2,
-        in_specs=[pl.BlockSpec((width // 4, pivots), lambda i: (i, 0))],
-        out_specs=(pl.BlockSpec((width // 4, pivots), lambda i: (i, 0)),) * 2,
-        compiler_params=grant(60),
-        cost_estimate=pl.CostEstimate(
-            flops=4 * width * pivots, bytes_accessed=8 * width * pivots, transcendentals=0
-        ),
-        name="halve",
-    )(lower_panel)
     own_share = right_side.shape[1]
     tile = jnp.minimum(lax.div(me * own_share, BLK), pivots // BLK - 2)
     place = (
@@ -250,9 +239,7 @@
         compiler_params=grant(8),
         name="pick",
     )(front_map, arrived)
-    boundary, rest, placed, panel_high, panel_low = lax.optimization_barrier(
-        (boundary, rest, placed, panel_high, panel_low)
-    )
+    boundary, rest, placed = lax.optimization_barrier((boundary, rest, placed))
 
     def swap(value):
         return lax.ppermute(value, "c", [(0, 1), (1, 0)])
@@ -265,12 +252,13 @@
         ]
         return lax.ppermute(value, PIV, pairs)
 
-    chip = jnp.stack([boundary, swap(boundary)])
+    partner = swap(boundary)
+    chip = jnp.stack([boundary, partner])
     near_2, near_1 = apart(chip, 2), apart(chip, 1)
     inverse_hi = exchange(rest, "x")
     near_4, near_3 = apart(near_2[0], 2), apart(near_2, 1)
     far_2, far_1, far_4, far_3 = swap(near_2), swap(near_1), swap(near_4), swap(near_3)
-    pieces = (chip, near_1, near_2, near_3, far_1, far_2, far_3, near_4, far_4)
+    pieces = (boundary, partner, near_1, near_2, near_3, far_1, far_2, far_3, near_4, far_4)
     pieces = [piece.reshape(-1, across, part, width) for piece in pieces]
     few = quarter // deep
     where = jnp.stack([lax.axis_index("x"), tile, lax.axis_index("y"), core])
@@ -291,12 +279,13 @@
             ]
             + [
                 pl.BlockSpec((width, pivots), lambda i, at: (0, 0)),
-                pl.BlockSpec((width, pivots), lambda i, at: (0, 0)),
                 pl.BlockSpec((1, quarter, 2 * BLK), turn),
             ],
             out_specs=(pl.BlockSpec((quarter, half), lambda i, at: (0, 0)),) * (2 * across),
             scratch_shapes=[
                 pltpu.VMEM((quarter, width), jnp.float32),
+                pltpu.VMEM((width, pivots), jnp.bfloat16),
+                pltpu.VMEM((width, pivots), jnp.bfloat16),
                 pltpu.VMEM((quarter, pivots), jnp.float32),
             ],
         ),
@@ -308,7 +297,7 @@
             transcendentals=0,
         ),
         name="couple",
-    )(where, *pieces, panel_high, panel_low, placed)
+    )(where, *pieces, lower_panel, placed)
     shares_a, shares_b = shares[:across], shares[across:]
 
     def across_sent(shares):

time: 282 us -> 280 us (level)
  waiting for transfers between devices: 47 us -> 50.8 us
  Pallas kernels: 35.1 us -> 31.4 us
    pallas_call x1 -> x0, Pallas kernels: 4.31 us -> none  [body(): pl.pallas_call(halve_kernel, grid=(4,), out_shape=(jax.ShapeDtypeStruct((...]
  transfers between devices with their start and end apart: 28 -> 28, of which waited for: 15 -> 16; matrix products, arithmetic and copies ran while one was open for 2% -> 1% of each run, Pallas kernels for 8% -> 7%
where the time goes in v10:
time: 280 us; the launch traced here: 275 us
  starting transfers between devices  114 us (41%)
  blocking collectives  71.7 us (26%)
  waiting for transfers between devices  50.8 us (18%)
  Pallas kernels  31.4 us (11%)
    all_to_all x3, blocking collectives, exchange(): return lax.all_to_all(value, axes, split_axis=0, concat_axis=0, tiled=True)  71.7 us
    ppermute x8, starting transfers between devices, ring(): lax.ppermute(value, axis, [(i, (i + hops) % length) for i in range(length)])  35.2 us
    ppermute x6, waiting for transfers between devices, across_sent(): lax.ppermute(shares[k], 'x', [(i, (i + k) % across) for i in range(across)])  25.3 us
    ppermute x6, starting transfers between devices, swap(): return lax.ppermute(value, 'c', [(0, 1), (1, 0)])  22.5 us
    ppermute x6, starting transfers between devices, across_sent(): lax.ppermute(shares[k], 'x', [(i, (i + k) % across) for i in range(across)])  22.2 us
    all_to_all x4, starting transfers between devices, exchange(): return lax.all_to_all(value, axes, split_axis=0, concat_axis=0, tiled=True)  17.7 us
    ppermute x4, starting transfers between devices, apart(): return lax.ppermute(value, PIV, pairs)  16.8 us
    pallas_call x1, Pallas kernels, body(): pl.pallas_call(lambda *refs: couple_kernel(2 * across, *refs), grid_spec=...  11.5 us
  transfers between devices with their start and end apart: 28, of which 16 were waited for; matrix products, arithmetic and copies ran while one was open for 1% of the time, Pallas kernels for 7%

profile of v10, /device:TPU:1, one launch (start us, length us, event | category | flops | bytes accessed | tf_op | source)
XLA Modules:
  0.0 275.3 jit_solution(2818689877541840674)
XLA Ops:
  2.6 5.0 %all-to-all-start = ((f32[4,200,384]{2,1,0:T(8,128)}), f32[4,200,384]{2,1,0:T(8,128)S(1)}, u32[]{:S(2)}, u32[]{:S(2)}) async-start(f32[4,200,384]{2,1,0:T(8,128)} %repeat.1), calls=%async_computation | async-start | bytes 2457600 | tf_op jit(solution)/shard_map/all_to_all | solution.py:21
  7.6 5.8 %collective-permute-start.3 = (f32[64,1024]{1,0:T(8,128)S(1)}, f32[64,1024]{1,0:T(8,128)S(1)}, u32[]{:S(2)}, u32[]{:S(2)}) collective-permute-start(f32[64,1024]{1,0:T(8,128)S(1)} %copy-done), channel_id=1, source_target_pairs={{0,128},{64,192},{128,256},{192,320},{256,384},{320,448},{384,0},{... | collective-permute-start | bytes 786440 | tf_op jit(solution)/shard_map/ppermute | solution.py:176
  13.4 6.8 %collective-permute-start.1 = (f32[64,1024]{1,0:T(8,128)S(1)}, f32[64,1024]{1,0:T(8,128)S(1)}, u32[]{:S(2)}, u32[]{:S(2)}) collective-permute-start(f32[64,1024]{1,0:T(8,128)S(1)} %copy-done), channel_id=1, source_target_pairs={{0,384},{64,448},{128,0},{192,64},{256,128},{320,192},{384,256},{4... | collective-permute-start | bytes 786440 | tf_op jit(solution)/shard_map/ppermute | solution.py:176
  20.2 4.3 %collective-permute-start = (f32[64,1024]{1,0:T(8,128)S(1)}, f32[64,1024]{1,0:T(8,128)S(1)}, u32[]{:S(2)}, u32[]{:S(2)}) collective-permute-start(f32[64,1024]{1,0:T(8,128)S(1)} %copy-done), channel_id=1, source_target_pairs={{0,448},{64,0},{128,64},{192,128},{256,192},{320,256},{384,320},{4... | collective-permute-start | bytes 786440 | tf_op jit(solution)/shard_map/ppermute | solution.py:176
  26.4 4.3 %collective-permute-start.6 = (f32[32,1024]{1,0:T(8,128)S(1)}, f32[32,1024]{1,0:T(8,128)S(1)}, u32[]{:S(2)}, u32[]{:S(2)}) collective-permute-start(f32[32,1024]{1,0:T(8,128)S(1)} %slice.16), channel_id=1, source_target_pairs={{0,128},{64,192},{128,256},{192,320},{256,384},{320,448},{384,0},{... | collective-permute-start | bytes 393224 | tf_op jit(solution)/shard_map/ppermute | solution.py:176
  31.6 5.0 %collective-permute-start.7 = (f32[32,1024]{1,0:T(8,128)}, f32[32,1024]{1,0:T(8,128)S(1)}, u32[]{:S(2)}, u32[]{:S(2)}) collective-permute-start(f32[32,1024]{1,0:T(8,128)} %slice.17), channel_id=1, source_target_pairs={{0,384},{64,448},{128,0},{192,64},{256,128},{320,192},{384,256},{4... | collective-permute-start | bytes 393224 | tf_op jit(solution)/shard_map/ppermute | solution.py:176
  36.6 5.2 %collective-permute-start.4 = (f32[64,1024]{1,0:T(8,128)S(1)}, f32[64,1024]{1,0:T(8,128)S(1)}, u32[]{:S(2)}, u32[]{:S(2)}) collective-permute-start(f32[64,1024]{1,0:T(8,128)S(1)} %collective-permute-done.3.refs_7_), channel_id=1, source_target_pairs={{0,64},{64,128},{128,192},{192,256},{256,320},{320,384},{384,448},... | collective-permute-start | bytes 786440 | tf_op jit(solution)/shard_map/ppermute | solution.py:176
  55.9 6.5 %copies.1 = f32[4,576,384]{2,1,0:T(8,128)} custom-call(f32[768,384]{1,0:T(8,128)} %inverse.2), custom_call_target="tpu_custom_call" | custom-call | flops 294912 | bytes 5898240 | tf_op jit(solution)/shard_map/copies/pallas_call | solution.py:209
  68.5 6.0 %collective-permute-start.8 = (f32[64,1024]{1,0:T(8,128)S(1)}, f32[64,1024]{1,0:T(8,128)S(1)}, u32[]{:S(2)}, u32[]{:S(2)}) collective-permute-start(f32[64,1024]{1,0:T(8,128)S(1)} %pick.1), channel_id=1, source_target_pairs={{0,1},{1,0},{2,3},{3,2},{4,5},{5,4},{6,7},{7,6},{8,9},{9,8},{10,11... | collective-permute-start | bytes 786440 | tf_op jit(solution)/shard_map/ppermute | solution.py:245
  74.4 4.7 %all-to-all-start.2 = ((f32[4,576,384]{2,1,0:T(8,128)}), f32[4,576,384]{2,1,0:T(8,128)}, u32[]{:S(2)}, u32[]{:S(2)}) async-start(f32[4,576,384]{2,1,0:T(8,128)} %copies.1), calls=%async_computation.2 | async-start | bytes 7077888 | tf_op jit(solution)/shard_map/all_to_all | solution.py:21
  79.2 5.9 %collective-permute-start.10 = (f32[2,64,1024]{2,1,0:T(8,128)S(1)}, f32[2,64,1024]{2,1,0:T(8,128)S(1)}, u32[]{:S(2)}, u32[]{:S(2)}) collective-permute-start(f32[2,64,1024]{2,1,0:T(8,128)S(1)} %pad_maximum_fusion), channel_id=1, source_target_pairs={{0,4},{1,13},{2,6},{3,15},{4,8},{5,1},{6,10},{7,3},{8,12},{9,5},{1... | collective-permute-start | bytes 1572872 | tf_op jit(solution)/shard_map/ppermute | solution.py:253
  88.1 8.7 %collective-permute-done.10 = f32[2,64,1024]{2,1,0:T(8,128)S(1)} collective-permute-done((f32[2,64,1024]{2,1,0:T(8,128)S(1)}, f32[2,64,1024]{2,1,0:T(8,128)S(1)}, u32[]{:S(2)}, u32[]{:S(2)}) %collective-permute-start.10) | collective-permute-done | bytes 524320 | tf_op jit(solution)/shard_map/ppermute | solution.py:253
  96.9 4.2 %collective-permute-start.11 = (f32[2,64,1024]{2,1,0:T(8,128)S(1)}, f32[2,64,1024]{2,1,0:T(8,128)S(1)}, u32[]{:S(2)}, u32[]{:S(2)}) collective-permute-start(f32[2,64,1024]{2,1,0:T(8,128)S(1)} %collective-permute-done.10), channel_id=1, source_target_pairs={{0,2},{1,15},{2,4},{3,1},{4,6},{5,3},{6,8},{7,5},{8,10},{9,7},{10,... | collective-permute-start | bytes 1572872 | tf_op jit(solution)/shard_map/ppermute | solution.py:253
  119.5 11.5 %couple.1 = (f32[256,384]{1,0:T(8,128)S(1)}, f32[256,384]{1,0:T(8,128)S(1)}, f32[256,384]{1,0:T(8,128)}, f32[256,384]{1,0:T(8,128)}, f32[256,384]{1,0:T(8,128)},...) custom-call(s32[4]{0:T(128)S(1)} %pad_add_fusion.refs_0_, f32[1,4,16,1024]{3,2,1,0:T(8,128)S(1)} %bitcast.37, ...), custom_call_target="tpu_custom_call" | custom-call | flops 4831838208 | bytes 10485760 | tf_op jit(solution)/shard_map/couple/pallas_call | solution.py:269
  134.7 4.3 %collective-permute-start.18 = (f32[256,384]{1,0:T(8,128)}, f32[256,384]{1,0:T(8,128)S(1)}, u32[]{:S(2)}, u32[]{:S(2)}) collective-permute-start(f32[256,384]{1,0:T(8,128)} %get-tuple-element.58), channel_id=1, source_target_pairs={{0,32},{16,48},{32,0},{48,16},{1,33},{17,49},{33,1},{49,17},{2,34}... | collective-permute-start | bytes 1179656 | tf_op jit(solution)/shard_map/ppermute | solution.py:305
  144.9 9.4 %collective-permute-done.18 = f32[256,384]{1,0:T(8,128)S(1)} collective-permute-done((f32[256,384]{1,0:T(8,128)}, f32[256,384]{1,0:T(8,128)S(1)}, u32[]{:S(2)}, u32[]{:S(2)}) %collective-permute-start.18) | collective-permute-done | bytes 393248 | tf_op jit(solution)/shard_map/ppermute | solution.py:305
  156.6 4.0 %all-to-all-start.3 = ((f32[8,32,384]{2,1,0:T(8,128)}), f32[8,32,384]{2,1,0:T(8,128)S(1)}, u32[]{:S(2)}, u32[]{:S(2)}) async-start(f32[8,32,384]{2,1,0:T(8,128)} %bitcast.20), calls=%async_computation.3 | async-start | bytes 786432 | tf_op jit(solution)/shard_map/all_to_all | solution.py:21
  160.7 5.0 %collective-permute-start.20 = (f32[256,384]{1,0:T(8,128)}, f32[256,384]{1,0:T(8,128)S(1)}, u32[]{:S(2)}, u32[]{:S(2)}) collective-permute-start(f32[256,384]{1,0:T(8,128)} %get-tuple-element.62), channel_id=1, source_target_pairs={{0,16},{16,32},{32,48},{48,0},{1,17},{17,33},{33,49},{49,1},{2,18}... | collective-permute-start | bytes 1179656 | tf_op jit(solution)/shard_map/ppermute | solution.py:305
  174.0 9.9 %collective-permute-done.21 = f32[256,384]{1,0:T(8,128)S(1)} collective-permute-done((f32[256,384]{1,0:T(8,128)S(1)}, f32[256,384]{1,0:T(8,128)S(1)}, u32[]{:S(2)}, u32[]{:S(2)}) %collective-permute-start.21) | collective-permute-done | bytes 393248 | tf_op jit(solution)/shard_map/ppermute | solution.py:305
  185.2 18.9 %all_to_all.35.pieces_b = f32[8,32,384]{2,1,0:T(8,128)S(1)} all-to-all(f32[8,32,384]{2,1,0:T(8,128)S(1)} %bitcast.45), channel_id=1, replica_groups=mesh['z'=8,'x'=4,'y'=8,'c'=2] {'z'}, dimensions={0} | all-to-all | bytes 786432 | tf_op jit(solution)/shard_map/all_to_all | solution.py:21
  204.2 22.6 %all_to_all.36 = f32[8,32,768]{2,1,0:T(8,128)} all-to-all(f32[8,32,768]{2,1,0:T(8,128)S(1)} %join.1), channel_id=1, replica_groups=mesh['z'=8,'x'=4,'y'=8,'c'=2] {'z'}, dimensions={0} | all-to-all | bytes 1572864 | tf_op jit(solution)/shard_map/all_to_all | solution.py:21
  226.8 6.9 %solve.1 = (f32[4,8,16,384]{3,2,1,0:T(8,128)}, f32[4,8,16,384]{3,2,1,0:T(8,128)}) custom-call(s32[1]{0:T(128)} %bitcast.core, f32[256,768]{1,0:T(8,128)} %bitcast.44, f32[4,200,384]{2,1,0:T(8,128)} %copy-done.3, f32[4,576,384]{2,1,0:T(8,128)} %all-to-all-done.2.inverse_hi), custom_call_target="tpu_custom_call" | custom-call | tf_op jit(solution)/shard_map/solve/pallas_call | solution.py:330
  233.7 6.6 %collective-permute-start.23 = (f32[4,8,16,384]{3,2,1,0:T(8,128)}, f32[4,8,16,384]{3,2,1,0:T(8,128)S(1)}, u32[]{:S(2)}, u32[]{:S(2)}) collective-permute-start(f32[4,8,16,384]{3,2,1,0:T(8,128)} %get-tuple-element.68), channel_id=1, source_target_pairs={{0,1},{1,0},{2,3},{3,2},{4,5},{5,4},{6,7},{7,6},{8,9},{9,8},{10,11... | collective-permute-start | bytes 2359304 | tf_op jit(solution)/shard_map/ppermute | solution.py:245
  243.6 30.2 %all_to_all.37 = f32[32,16,384]{2,1,0:T(8,128)S(1)} all-to-all(f32[32,16,384]{2,1,0:T(8,128)S(1)} %bitcast.43), channel_id=1, replica_groups=mesh['z'=8,'x'=4,'y'=8,'c'=2] {'x','y'}, dimensions={0} | all-to-all | bytes 1572864 | tf_op jit(solution)/shard_map/all_to_all | solution.py:21
  (84 shorter events, 73.1 us)
Async XLA Ops:
  2.6 41.1 %all-to-all-start = ((f32[4,200,384]{2,1,0:T(8,128)}), f32[4,200,384]{2,1,0:T(8,128)S(1)}, u32[]{:S(2)}, u32[]{:S(2)}) async-start(f32[4,200,384]{2,1,0:T(8,128)} %repeat.1), calls=%async_computation | async-start | bytes 2457600 | tf_op jit(solution)/shard_map/all_to_all | solution.py:21
  7.6 18.8 %collective-permute-start.3 = (f32[64,1024]{1,0:T(8,128)S(1)}, f32[64,1024]{1,0:T(8,128)S(1)}, u32[]{:S(2)}, u32[]{:S(2)}) collective-permute-start(f32[64,1024]{1,0:T(8,128)S(1)} %copy-done), channel_id=1, source_target_pairs={{0,128},{64,192},{128,256},{192,320},{256,384},{320,448},{384,0},{... | collective-permute-start | bytes 786440 | tf_op jit(solution)/shard_map/ppermute | solution.py:176
  13.4 17.5 %collective-permute-start.1 = (f32[64,1024]{1,0:T(8,128)S(1)}, f32[64,1024]{1,0:T(8,128)S(1)}, u32[]{:S(2)}, u32[]{:S(2)}) collective-permute-start(f32[64,1024]{1,0:T(8,128)S(1)} %copy-done), channel_id=1, source_target_pairs={{0,384},{64,448},{128,0},{192,64},{256,128},{320,192},{384,256},{4... | collective-permute-start | bytes 786440 | tf_op jit(solution)/shard_map/ppermute | solution.py:176
  20.2 21.6 %collective-permute-start = (f32[64,1024]{1,0:T(8,128)S(1)}, f32[64,1024]{1,0:T(8,128)S(1)}, u32[]{:S(2)}, u32[]{:S(2)}) collective-permute-start(f32[64,1024]{1,0:T(8,128)S(1)} %copy-done), channel_id=1, source_target_pairs={{0,448},{64,0},{128,64},{192,128},{256,192},{320,256},{384,320},{4... | collective-permute-start | bytes 786440 | tf_op jit(solution)/shard_map/ppermute | solution.py:176
  24.4 19.5 %collective-permute-start.5 = (f32[64,1024]{1,0:T(8,128)S(1)}, f32[64,1024]{1,0:T(8,128)S(1)}, u32[]{:S(2)}, u32[]{:S(2)}) collective-permute-start(f32[64,1024]{1,0:T(8,128)S(1)} %copy-done), channel_id=1, source_target_pairs={{0,64},{64,128},{128,192},{192,256},{256,320},{320,384},{384,448},... | collective-permute-start | bytes 786440 | tf_op jit(solution)/shard_map/ppermute | solution.py:176
  26.4 17.5 %collective-permute-start.6 = (f32[32,1024]{1,0:T(8,128)S(1)}, f32[32,1024]{1,0:T(8,128)S(1)}, u32[]{:S(2)}, u32[]{:S(2)}) collective-permute-start(f32[32,1024]{1,0:T(8,128)S(1)} %slice.16), channel_id=1, source_target_pairs={{0,128},{64,192},{128,256},{192,320},{256,384},{320,448},{384,0},{... | collective-permute-start | bytes 393224 | tf_op jit(solution)/shard_map/ppermute | solution.py:176
  31.6 12.4 %collective-permute-start.7 = (f32[32,1024]{1,0:T(8,128)}, f32[32,1024]{1,0:T(8,128)S(1)}, u32[]{:S(2)}, u32[]{:S(2)}) collective-permute-start(f32[32,1024]{1,0:T(8,128)} %slice.17), channel_id=1, source_target_pairs={{0,384},{64,448},{128,0},{192,64},{256,128},{320,192},{384,256},{4... | collective-permute-start | bytes 393224 | tf_op jit(solution)/shard_map/ppermute | solution.py:176
  36.6 9.7 %collective-permute-start.4 = (f32[64,1024]{1,0:T(8,128)S(1)}, f32[64,1024]{1,0:T(8,128)S(1)}, u32[]{:S(2)}, u32[]{:S(2)}) collective-permute-start(f32[64,1024]{1,0:T(8,128)S(1)} %collective-permute-done.3.refs_7_), channel_id=1, source_target_pairs={{0,64},{64,128},{128,192},{192,256},{256,320},{320,384},{384,448},... | collective-permute-start | bytes 786440 | tf_op jit(solution)/shard_map/ppermute | solution.py:176
  51.9 16.0 %all-to-all-start.1 = ((f32[4,64,1024]{2,1,0:T(8,128)}), f32[4,64,1024]{2,1,0:T(8,128)S(1)}, u32[]{:S(2)}, u32[]{:S(2)}) async-start(f32[4,64,1024]{2,1,0:T(8,128)} %pack.1), calls=%async_computation.1 | async-start | bytes 2097152 | tf_op jit(solution)/shard_map/all_to_all | solution.py:21
  68.5 10.7 %collective-permute-start.8 = (f32[64,1024]{1,0:T(8,128)S(1)}, f32[64,1024]{1,0:T(8,128)S(1)}, u32[]{:S(2)}, u32[]{:S(2)}) collective-permute-start(f32[64,1024]{1,0:T(8,128)S(1)} %pick.1), channel_id=1, source_target_pairs={{0,1},{1,0},{2,3},{3,2},{4,5},{5,4},{6,7},{7,6},{8,9},{9,8},{10,11... | collective-permute-start | bytes 786440 | tf_op jit(solution)/shard_map/ppermute | solution.py:245
  74.4 67.6 %all-to-all-start.2 = ((f32[4,576,384]{2,1,0:T(8,128)}), f32[4,576,384]{2,1,0:T(8,128)}, u32[]{:S(2)}, u32[]{:S(2)}) async-start(f32[4,576,384]{2,1,0:T(8,128)} %copies.1), calls=%async_computation.2 | async-start | bytes 7077888 | tf_op jit(solution)/shard_map/all_to_all | solution.py:21
  79.2 17.6 %collective-permute-start.10 = (f32[2,64,1024]{2,1,0:T(8,128)S(1)}, f32[2,64,1024]{2,1,0:T(8,128)S(1)}, u32[]{:S(2)}, u32[]{:S(2)}) collective-permute-start(f32[2,64,1024]{2,1,0:T(8,128)S(1)} %pad_maximum_fusion), channel_id=1, source_target_pairs={{0,4},{1,13},{2,6},{3,15},{4,8},{5,1},{6,10},{7,3},{8,12},{9,5},{1... | collective-permute-start | bytes 1572872 | tf_op jit(solution)/shard_map/ppermute | solution.py:253
  85.1 21.6 %collective-permute-start.9 = (f32[2,64,1024]{2,1,0:T(8,128)S(1)}, f32[2,64,1024]{2,1,0:T(8,128)S(1)}, u32[]{:S(2)}, u32[]{:S(2)}) collective-permute-start(f32[2,64,1024]{2,1,0:T(8,128)S(1)} %pad_maximum_fusion), channel_id=1, source_target_pairs={{0,2},{1,15},{2,4},{3,1},{4,6},{5,3},{6,8},{7,5},{8,10},{9,7},{10,... | collective-permute-start | bytes 1572872 | tf_op jit(solution)/shard_map/ppermute | solution.py:253
  96.9 12.7 %collective-permute-start.11 = (f32[2,64,1024]{2,1,0:T(8,128)S(1)}, f32[2,64,1024]{2,1,0:T(8,128)S(1)}, u32[]{:S(2)}, u32[]{:S(2)}) collective-permute-start(f32[2,64,1024]{2,1,0:T(8,128)S(1)} %collective-permute-done.10), channel_id=1, source_target_pairs={{0,2},{1,15},{2,4},{3,1},{4,6},{5,3},{6,8},{7,5},{8,10},{9,7},{10,... | collective-permute-start | bytes 1572872 | tf_op jit(solution)/shard_map/ppermute | solution.py:253
  101.1 12.8 %collective-permute-start.15 = (f32[64,1024]{1,0:T(8,128)S(1)}, f32[64,1024]{1,0:T(8,128)S(1)}, u32[]{:S(2)}, u32[]{:S(2)}) collective-permute-start(f32[64,1024]{1,0:T(8,128)S(1)} %slice_bitcast_fusion), channel_id=1, source_target_pairs={{0,4},{1,13},{2,6},{3,15},{4,8},{5,1},{6,10},{7,3},{8,12},{9,5},{1... | collective-permute-start | bytes 786440 | tf_op jit(solution)/shard_map/ppermute | solution.py:253
  104.8 13.9 %collective-permute-start.13 = (f32[2,64,1024]{2,1,0:T(8,128)S(1)}, f32[2,64,1024]{2,1,0:T(8,128)S(1)}, u32[]{:S(2)}, u32[]{:S(2)}) collective-permute-start(f32[2,64,1024]{2,1,0:T(8,128)S(1)} %collective-permute-done.10), channel_id=1, source_target_pairs={{0,1},{1,0},{2,3},{3,2},{4,5},{5,4},{6,7},{7,6},{8,9},{9,8},{10,11... | collective-permute-start | bytes 1572872 | tf_op jit(solution)/shard_map/ppermute | solution.py:245
  106.8 11.9 %collective-permute-start.12 = (f32[2,64,1024]{2,1,0:T(8,128)S(1)}, f32[2,64,1024]{2,1,0:T(8,128)}, u32[]{:S(2)}, u32[]{:S(2)}) collective-permute-start(f32[2,64,1024]{2,1,0:T(8,128)S(1)} %collective-permute-done.9), channel_id=1, source_target_pairs={{0,1},{1,0},{2,3},{3,2},{4,5},{5,4},{6,7},{7,6},{8,9},{9,8},{10,11... | collective-permute-start | bytes 1572872 | tf_op jit(solution)/shard_map/ppermute | solution.py:245
  131.1 13.8 %collective-permute-start.17 = (f32[256,384]{1,0:T(8,128)S(1)}, f32[256,384]{1,0:T(8,128)S(1)}, u32[]{:S(2)}, u32[]{:S(2)}) collective-permute-start(f32[256,384]{1,0:T(8,128)S(1)} %get-tuple-element.57), channel_id=1, source_target_pairs={{0,16},{16,32},{32,48},{48,0},{1,17},{17,33},{33,49},{49,1},{2,18}... | collective-permute-start | bytes 1179656 | tf_op jit(solution)/shard_map/ppermute | solution.py:305
  134.7 19.6 %collective-permute-start.18 = (f32[256,384]{1,0:T(8,128)}, f32[256,384]{1,0:T(8,128)S(1)}, u32[]{:S(2)}, u32[]{:S(2)}) collective-permute-start(f32[256,384]{1,0:T(8,128)} %get-tuple-element.58), channel_id=1, source_target_pairs={{0,32},{16,48},{32,0},{48,16},{1,33},{17,49},{33,1},{49,17},{2,34}... | collective-permute-start | bytes 1179656 | tf_op jit(solution)/shard_map/ppermute | solution.py:305
  139.0 16.9 %collective-permute-start.19 = (f32[256,384]{1,0:T(8,128)}, f32[256,384]{1,0:T(8,128)S(1)}, u32[]{:S(2)}, u32[]{:S(2)}) collective-permute-start(f32[256,384]{1,0:T(8,128)} %get-tuple-element.59), channel_id=1, source_target_pairs={{0,48},{16,0},{32,16},{48,32},{1,49},{17,1},{33,17},{49,33},{2,50}... | collective-permute-start | bytes 1179656 | tf_op jit(solution)/shard_map/ppermute | solution.py:305
  156.6 16.9 %all-to-all-start.3 = ((f32[8,32,384]{2,1,0:T(8,128)}), f32[8,32,384]{2,1,0:T(8,128)S(1)}, u32[]{:S(2)}, u32[]{:S(2)}) async-start(f32[8,32,384]{2,1,0:T(8,128)} %bitcast.20), calls=%async_computation.3 | async-start | bytes 786432 | tf_op jit(solution)/shard_map/all_to_all | solution.py:21
  160.7 13.3 %collective-permute-start.20 = (f32[256,384]{1,0:T(8,128)}, f32[256,384]{1,0:T(8,128)S(1)}, u32[]{:S(2)}, u32[]{:S(2)}) collective-permute-start(f32[256,384]{1,0:T(8,128)} %get-tuple-element.62), channel_id=1, source_target_pairs={{0,16},{16,32},{32,48},{48,0},{1,17},{17,33},{33,49},{49,1},{2,18}... | collective-permute-start | bytes 1179656 | tf_op jit(solution)/shard_map/ppermute | solution.py:305
  165.7 18.3 %collective-permute-start.21 = (f32[256,384]{1,0:T(8,128)S(1)}, f32[256,384]{1,0:T(8,128)S(1)}, u32[]{:S(2)}, u32[]{:S(2)}) collective-permute-start(f32[256,384]{1,0:T(8,128)S(1)} %copy-done.11), channel_id=1, source_target_pairs={{0,32},{16,48},{32,0},{48,16},{1,33},{17,49},{33,1},{49,17},{2,34}... | collective-permute-start | bytes 1179656 | tf_op jit(solution)/shard_map/ppermute | solution.py:305
  168.8 16.4 %collective-permute-start.22 = (f32[256,384]{1,0:T(8,128)S(1)}, f32[256,384]{1,0:T(8,128)S(1)}, u32[]{:S(2)}, u32[]{:S(2)}) collective-permute-start(f32[256,384]{1,0:T(8,128)S(1)} %copy-done.10), channel_id=1, source_target_pairs={{0,48},{16,0},{32,16},{48,32},{1,49},{17,1},{33,17},{49,33},{2,50}... | collective-permute-start | bytes 1179656 | tf_op jit(solution)/shard_map/ppermute | solution.py:305
  (17 other events, 266.5 us)

commit v11 on v10

--- a/solution.py
+++ b/solution.py
@@ -100,7 +100,7 @@
     total[...] = -product(split(rows[...]), (high[...], low[...]))
     window = pl.ds(pl.multiple_of(where[1] * BLK, BLK), wide)
     total[:, window] = total[:, window] + placed[0]
-    half = total.shape[1] // 2
+    half = shares[0].shape[1]
     across = slots // 2
     for slot in range(across):
 
@@ -166,7 +166,6 @@
     quarter = total // across
     me = lax.axis_index(ROWS)
 
-    half = pivots // 2
     cut = pivots // 4
     core = lax.axis_index("c")
     first = child_start - me * span
@@ -261,6 +260,7 @@
     pieces = (boundary, partner, near_1, near_2, near_3, far_1, far_2, far_3, near_4, far_4)
     pieces = [piece.reshape(-1, across, part, width) for piece in pieces]
     few = quarter // deep
+    sizes = [pivots // 3] * across + [pivots - pivots // 3] * across
     where = jnp.stack([lax.axis_index("x"), tile, lax.axis_index("y"), core])
 
     def turn(i, at):
@@ -281,7 +281,7 @@
                 pl.BlockSpec((width, pivots), lambda i, at: (0, 0)),
                 pl.BlockSpec((1, quarter, 2 * BLK), turn),
             ],
-            out_specs=(pl.BlockSpec((quarter, half), lambda i, at: (0, 0)),) * (2 * across),
+            out_specs=[pl.BlockSpec((quarter, size), lambda i, at: (0, 0)) for size in sizes],
             scratch_shapes=[
                 pltpu.VMEM((quarter, width), jnp.float32),
                 pltpu.VMEM((width, pivots), jnp.bfloat16),
@@ -289,7 +289,7 @@
                 pltpu.VMEM((quarter, pivots), jnp.float32),
             ],
         ),
-        out_shape=(jax.ShapeDtypeStruct((quarter, half), jnp.float32),) * (2 * across),
+        out_shape=[jax.ShapeDtypeStruct((quarter, size), jnp.float32) for size in sizes],
         compiler_params=grant(52),
         cost_estimate=pl.CostEstimate(
             flops=6 * total * width * pivots,
@@ -308,7 +308,7 @@
 
     def nearer(shares, arrived):
         summed = shares[0] + sum(arrived[1:], arrived[0])
-        return exchange(summed.reshape(deep, few, half), "z")
+        return exchange(summed.reshape(deep, few, -1), "z")
 
     arrived_a = across_sent(shares_a)
     arrived_b = across_sent(shares_b)

time: 280 us -> 268 us (0.957)
  waiting for transfers between devices: 50.8 us -> 32.7 us
  blocking collectives: 71.7 us -> 84.5 us
  starting transfers between devices: 114 us -> 108 us
    ppermute x6, waiting for transfers between devices: 25.3 us -> 8.69 us  [across_sent(): lax.ppermute(shares[k], 'x', [(i, (i + k) % across) for i in range(across)])]
    all_to_all x3 -> x4, blocking collectives: 71.7 us -> 84.5 us  [exchange(): return lax.all_to_all(value, axes, split_axis=0, concat_axis=0, tiled=True)]
    all_to_all x4 -> x3, starting transfers between devices: 17.7 us -> 13.7 us  [exchange(): return lax.all_to_all(value, axes, split_axis=0, concat_axis=0, tiled=True)]
  transfers between devices with their start and end apart: 28 -> 27, of which waited for: 16 -> 11; matrix products, arithmetic and copies ran while one was open for 1% -> 1% of each run, Pallas kernels for 7% -> 7%
where the time goes in v11:
time: 268 us; the launch traced here: 263 us
  starting transfers between devices  108 us (40%)
  blocking collectives  84.5 us (32%)
  waiting for transfers between devices  32.7 us (12%)
  Pallas kernels  31.5 us (12%)
  local copies, waits for them, and re-layouts  2.68 us (1%)
    all_to_all x4, blocking collectives, exchange(): return lax.all_to_all(value, axes, split_axis=0, concat_axis=0, tiled=True)  84.5 us
    ppermute x8, starting transfers between devices, ring(): lax.ppermute(value, axis, [(i, (i + hops) % length) for i in range(length)])  35.2 us
    ppermute x6, starting transfers between devices, swap(): return lax.ppermute(value, 'c', [(0, 1), (1, 0)])  22.8 us
    ppermute x6, starting transfers between devices, across_sent(): lax.ppermute(shares[k], 'x', [(i, (i + k) % across) for i in range(across)])  19.5 us
    ppermute x4, starting transfers between devices, apart(): return lax.ppermute(value, PIV, pairs)  16.8 us
    all_to_all x3, starting transfers between devices, exchange(): return lax.all_to_all(value, axes, split_axis=0, concat_axis=0, tiled=True)  13.7 us
    pallas_call x1, Pallas kernels, body(): pl.pallas_call(lambda *refs: couple_kernel(2 * across, *refs), grid_spec=...  11.6 us
    ppermute x4, waiting for transfers between devices, apart(): return lax.ppermute(value, PIV, pairs)  11.5 us
  transfers between devices with their start and end apart: 27, of which 11 were waited for; matrix products, arithmetic and copies ran while one was open for 1% of the time, Pallas kernels for 7%

profile of v11, /device:TPU:1, one launch (start us, length us, event | category | flops | bytes accessed | tf_op | source)
XLA Modules:
  0.0 263.2 jit_solution(497564299186208433)
XLA Ops:
  2.6 5.0 %all-to-all-start = ((f32[4,200,384]{2,1,0:T(8,128)}), f32[4,200,384]{2,1,0:T(8,128)S(1)}, u32[]{:S(2)}, u32[]{:S(2)}) async-start(f32[4,200,384]{2,1,0:T(8,128)} %repeat.1), calls=%async_computation | async-start | bytes 2457600 | tf_op jit(solution)/shard_map/all_to_all | solution.py:21
  7.6 5.8 %collective-permute-start.3 = (f32[64,1024]{1,0:T(8,128)S(1)}, f32[64,1024]{1,0:T(8,128)S(1)}, u32[]{:S(2)}, u32[]{:S(2)}) collective-permute-start(f32[64,1024]{1,0:T(8,128)S(1)} %copy-done), channel_id=1, source_target_pairs={{0,128},{64,192},{128,256},{192,320},{256,384},{320,448},{384,0},{... | collective-permute-start | bytes 786440 | tf_op jit(solution)/shard_map/ppermute | solution.py:175
  13.4 6.8 %collective-permute-start.1 = (f32[64,1024]{1,0:T(8,128)S(1)}, f32[64,1024]{1,0:T(8,128)S(1)}, u32[]{:S(2)}, u32[]{:S(2)}) collective-permute-start(f32[64,1024]{1,0:T(8,128)S(1)} %copy-done), channel_id=1, source_target_pairs={{0,384},{64,448},{128,0},{192,64},{256,128},{320,192},{384,256},{4... | collective-permute-start | bytes 786440 | tf_op jit(solution)/shard_map/ppermute | solution.py:175
  20.1 4.3 %collective-permute-start = (f32[64,1024]{1,0:T(8,128)S(1)}, f32[64,1024]{1,0:T(8,128)S(1)}, u32[]{:S(2)}, u32[]{:S(2)}) collective-permute-start(f32[64,1024]{1,0:T(8,128)S(1)} %copy-done), channel_id=1, source_target_pairs={{0,448},{64,0},{128,64},{192,128},{256,192},{320,256},{384,320},{4... | collective-permute-start | bytes 786440 | tf_op jit(solution)/shard_map/ppermute | solution.py:175
  26.4 4.3 %collective-permute-start.6 = (f32[32,1024]{1,0:T(8,128)S(1)}, f32[32,1024]{1,0:T(8,128)S(1)}, u32[]{:S(2)}, u32[]{:S(2)}) collective-permute-start(f32[32,1024]{1,0:T(8,128)S(1)} %slice.16), channel_id=1, source_target_pairs={{0,128},{64,192},{128,256},{192,320},{256,384},{320,448},{384,0},{... | collective-permute-start | bytes 393224 | tf_op jit(solution)/shard_map/ppermute | solution.py:175
  31.6 5.0 %collective-permute-start.7 = (f32[32,1024]{1,0:T(8,128)}, f32[32,1024]{1,0:T(8,128)S(1)}, u32[]{:S(2)}, u32[]{:S(2)}) collective-permute-start(f32[32,1024]{1,0:T(8,128)} %slice.17), channel_id=1, source_target_pairs={{0,384},{64,448},{128,0},{192,64},{256,128},{320,192},{384,256},{4... | collective-permute-start | bytes 393224 | tf_op jit(solution)/shard_map/ppermute | solution.py:175
  36.5 5.2 %collective-permute-start.4 = (f32[64,1024]{1,0:T(8,128)S(1)}, f32[64,1024]{1,0:T(8,128)S(1)}, u32[]{:S(2)}, u32[]{:S(2)}) collective-permute-start(f32[64,1024]{1,0:T(8,128)S(1)} %collective-permute-done.3.refs_7_), channel_id=1, source_target_pairs={{0,64},{64,128},{128,192},{192,256},{256,320},{320,384},{384,448},... | collective-permute-start | bytes 786440 | tf_op jit(solution)/shard_map/ppermute | solution.py:175
  46.2 3.8 %collective-permute-done.2.refs_5_ = f32[64,1024]{1,0:T(8,128)S(1)} collective-permute-done((f32[64,1024]{1,0:T(8,128)S(1)}, f32[64,1024]{1,0:T(8,128)S(1)}, u32[]{:S(2)}, u32[]{:S(2)}) %collective-permute-start.2) | collective-permute-done | bytes 262176 | tf_op jit(solution)/shard_map/ppermute | solution.py:175
  51.9 4.0 %all-to-all-start.1 = ((f32[4,64,1024]{2,1,0:T(8,128)}), f32[4,64,1024]{2,1,0:T(8,128)S(1)}, u32[]{:S(2)}, u32[]{:S(2)}) async-start(f32[4,64,1024]{2,1,0:T(8,128)} %pack.1), calls=%async_computation.1 | async-start | bytes 2097152 | tf_op jit(solution)/shard_map/all_to_all | solution.py:21
  55.9 6.5 %copies.1 = f32[4,576,384]{2,1,0:T(8,128)} custom-call(f32[768,384]{1,0:T(8,128)} %inverse.2), custom_call_target="tpu_custom_call" | custom-call | flops 294912 | bytes 5898240 | tf_op jit(solution)/shard_map/copies/pallas_call | solution.py:208
  68.4 6.0 %collective-permute-start.8 = (f32[64,1024]{1,0:T(8,128)S(1)}, f32[64,1024]{1,0:T(8,128)S(1)}, u32[]{:S(2)}, u32[]{:S(2)}) collective-permute-start(f32[64,1024]{1,0:T(8,128)S(1)} %pick.1), channel_id=1, source_target_pairs={{0,1},{1,0},{2,3},{3,2},{4,5},{5,4},{6,7},{7,6},{8,9},{9,8},{10,11... | collective-permute-start | bytes 786440 | tf_op jit(solution)/shard_map/ppermute | solution.py:244
  74.4 4.7 %all-to-all-start.2 = ((f32[4,576,384]{2,1,0:T(8,128)}), f32[4,576,384]{2,1,0:T(8,128)}, u32[]{:S(2)}, u32[]{:S(2)}) async-start(f32[4,576,384]{2,1,0:T(8,128)} %copies.1), calls=%async_computation.2 | async-start | bytes 7077888 | tf_op jit(solution)/shard_map/all_to_all | solution.py:21
  79.2 5.9 %collective-permute-start.10 = (f32[2,64,1024]{2,1,0:T(8,128)S(1)}, f32[2,64,1024]{2,1,0:T(8,128)S(1)}, u32[]{:S(2)}, u32[]{:S(2)}) collective-permute-start(f32[2,64,1024]{2,1,0:T(8,128)S(1)} %pad_maximum_fusion), channel_id=1, source_target_pairs={{0,4},{1,13},{2,6},{3,15},{4,8},{5,1},{6,10},{7,3},{8,12},{9,5},{1... | collective-permute-start | bytes 1572872 | tf_op jit(solution)/shard_map/ppermute | solution.py:252
  88.1 8.7 %collective-permute-done.10 = f32[2,64,1024]{2,1,0:T(8,128)S(1)} collective-permute-done((f32[2,64,1024]{2,1,0:T(8,128)S(1)}, f32[2,64,1024]{2,1,0:T(8,128)S(1)}, u32[]{:S(2)}, u32[]{:S(2)}) %collective-permute-start.10) | collective-permute-done | bytes 524320 | tf_op jit(solution)/shard_map/ppermute | solution.py:252
  96.8 4.2 %collective-permute-start.11 = (f32[2,64,1024]{2,1,0:T(8,128)S(1)}, f32[2,64,1024]{2,1,0:T(8,128)S(1)}, u32[]{:S(2)}, u32[]{:S(2)}) collective-permute-start(f32[2,64,1024]{2,1,0:T(8,128)S(1)} %collective-permute-done.10), channel_id=1, source_target_pairs={{0,2},{1,15},{2,4},{3,1},{4,6},{5,3},{6,8},{7,5},{8,10},{9,7},{10,... | collective-permute-start | bytes 1572872 | tf_op jit(solution)/shard_map/ppermute | solution.py:252
  119.8 11.6 %couple.1 = (f32[256,256]{1,0:T(8,128)S(1)}, f32[256,256]{1,0:T(8,128)S(1)}, f32[256,256]{1,0:T(8,128)S(1)}, f32[256,256]{1,0:T(8,128)S(1)}, f32[256,512]{1,0:T(...) custom-call(s32[4]{0:T(128)S(1)} %pad_add_fusion.refs_0_, f32[1,4,16,1024]{3,2,1,0:T(8,128)S(1)} %bitcast.37, ...), custom_call_target="tpu_custom_call" | custom-call | flops 4831838208 | bytes 10485760 | tf_op jit(solution)/shard_map/couple/pallas_call | solution.py:269
  135.2 4.3 %collective-permute-start.18 = (f32[256,256]{1,0:T(8,128)S(1)}, f32[256,256]{1,0:T(8,128)S(1)}, u32[]{:S(2)}, u32[]{:S(2)}) collective-permute-start(f32[256,256]{1,0:T(8,128)S(1)} %get-tuple-element.58), channel_id=1, source_target_pairs={{0,32},{16,48},{32,0},{48,16},{1,33},{17,49},{33,1},{49,17},{2,34}... | collective-permute-start | bytes 786440 | tf_op jit(solution)/shard_map/ppermute | solution.py:305
  151.1 13.0 %all_to_all.35.pieces_a = f32[8,32,256]{2,1,0:T(8,128)S(1)} all-to-all(f32[8,32,256]{2,1,0:T(8,128)S(1)} %bitcast.45), channel_id=1, replica_groups=mesh['z'=8,'x'=4,'y'=8,'c'=2] {'z'}, dimensions={0} | all-to-all | bytes 524288 | tf_op jit(solution)/shard_map/all_to_all | solution.py:21
  164.1 7.5 %collective-permute-done.21 = f32[256,512]{1,0:T(8,128)S(1)} collective-permute-done((f32[256,512]{1,0:T(8,128)}, f32[256,512]{1,0:T(8,128)S(1)}, u32[]{:S(2)}, u32[]{:S(2)}) %collective-permute-start.21) | collective-permute-done | bytes 524320 | tf_op jit(solution)/shard_map/ppermute | solution.py:305
  173.0 18.9 %all_to_all.36.pieces_b = f32[8,32,512]{2,1,0:T(8,128)S(1)} all-to-all(f32[8,32,512]{2,1,0:T(8,128)S(1)} %bitcast.44), channel_id=1, replica_groups=mesh['z'=8,'x'=4,'y'=8,'c'=2] {'z'}, dimensions={0} | all-to-all | bytes 1048576 | tf_op jit(solution)/shard_map/all_to_all | solution.py:21
  192.0 22.3 %all_to_all.37 = f32[8,32,768]{2,1,0:T(8,128)} all-to-all(f32[8,32,768]{2,1,0:T(8,128)S(1)} %join.1), channel_id=1, replica_groups=mesh['z'=8,'x'=4,'y'=8,'c'=2] {'z'}, dimensions={0} | all-to-all | bytes 1572864 | tf_op jit(solution)/shard_map/all_to_all | solution.py:21
  214.3 6.9 %solve.1 = (f32[4,8,16,384]{3,2,1,0:T(8,128)}, f32[4,8,16,384]{3,2,1,0:T(8,128)}) custom-call(s32[1]{0:T(128)} %bitcast.core, f32[256,768]{1,0:T(8,128)} %bitcast.43, f32[4,200,384]{2,1,0:T(8,128)} %copy-done.3, f32[4,576,384]{2,1,0:T(8,128)} %all-to-all-done.2.inverse_hi), custom_call_target="tpu_custom_call" | custom-call | tf_op jit(solution)/shard_map/solve/pallas_call | solution.py:330
  221.2 6.9 %collective-permute-start.23 = (f32[4,8,16,384]{3,2,1,0:T(8,128)}, f32[4,8,16,384]{3,2,1,0:T(8,128)S(1)}, u32[]{:S(2)}, u32[]{:S(2)}) collective-permute-start(f32[4,8,16,384]{3,2,1,0:T(8,128)} %get-tuple-element.68), channel_id=1, source_target_pairs={{0,1},{1,0},{2,3},{3,2},{4,5},{5,4},{6,7},{7,6},{8,9},{9,8},{10,11... | collective-permute-start | bytes 2359304 | tf_op jit(solution)/shard_map/ppermute | solution.py:244
  231.5 30.3 %all_to_all.38 = f32[32,16,384]{2,1,0:T(8,128)S(1)} all-to-all(f32[32,16,384]{2,1,0:T(8,128)S(1)} %bitcast.42), channel_id=1, replica_groups=mesh['z'=8,'x'=4,'y'=8,'c'=2] {'x','y'}, dimensions={0} | all-to-all | bytes 1572864 | tf_op jit(solution)/shard_map/all_to_all | solution.py:21
  (81 shorter events, 60.9 us)
Async XLA Ops:
  2.6 41.1 %all-to-all-start = ((f32[4,200,384]{2,1,0:T(8,128)}), f32[4,200,384]{2,1,0:T(8,128)S(1)}, u32[]{:S(2)}, u32[]{:S(2)}) async-start(f32[4,200,384]{2,1,0:T(8,128)} %repeat.1), calls=%async_computation | async-start | bytes 2457600 | tf_op jit(solution)/shard_map/all_to_all | solution.py:21
  7.6 18.8 %collective-permute-start.3 = (f32[64,1024]{1,0:T(8,128)S(1)}, f32[64,1024]{1,0:T(8,128)S(1)}, u32[]{:S(2)}, u32[]{:S(2)}) collective-permute-start(f32[64,1024]{1,0:T(8,128)S(1)} %copy-done), channel_id=1, source_target_pairs={{0,128},{64,192},{128,256},{192,320},{256,384},{320,448},{384,0},{... | collective-permute-start | bytes 786440 | tf_op jit(solution)/shard_map/ppermute | solution.py:175
  13.4 17.5 %collective-permute-start.1 = (f32[64,1024]{1,0:T(8,128)S(1)}, f32[64,1024]{1,0:T(8,128)S(1)}, u32[]{:S(2)}, u32[]{:S(2)}) collective-permute-start(f32[64,1024]{1,0:T(8,128)S(1)} %copy-done), channel_id=1, source_target_pairs={{0,384},{64,448},{128,0},{192,64},{256,128},{320,192},{384,256},{4... | collective-permute-start | bytes 786440 | tf_op jit(solution)/shard_map/ppermute | solution.py:175
  20.1 21.6 %collective-permute-start = (f32[64,1024]{1,0:T(8,128)S(1)}, f32[64,1024]{1,0:T(8,128)S(1)}, u32[]{:S(2)}, u32[]{:S(2)}) collective-permute-start(f32[64,1024]{1,0:T(8,128)S(1)} %copy-done), channel_id=1, source_target_pairs={{0,448},{64,0},{128,64},{192,128},{256,192},{320,256},{384,320},{4... | collective-permute-start | bytes 786440 | tf_op jit(solution)/shard_map/ppermute | solution.py:175
  24.4 19.5 %collective-permute-start.5 = (f32[64,1024]{1,0:T(8,128)S(1)}, f32[64,1024]{1,0:T(8,128)S(1)}, u32[]{:S(2)}, u32[]{:S(2)}) collective-permute-start(f32[64,1024]{1,0:T(8,128)S(1)} %copy-done), channel_id=1, source_target_pairs={{0,64},{64,128},{128,192},{192,256},{256,320},{320,384},{384,448},... | collective-permute-start | bytes 786440 | tf_op jit(solution)/shard_map/ppermute | solution.py:175
  26.4 17.5 %collective-permute-start.6 = (f32[32,1024]{1,0:T(8,128)S(1)}, f32[32,1024]{1,0:T(8,128)S(1)}, u32[]{:S(2)}, u32[]{:S(2)}) collective-permute-start(f32[32,1024]{1,0:T(8,128)S(1)} %slice.16), channel_id=1, source_target_pairs={{0,128},{64,192},{128,256},{192,320},{256,384},{320,448},{384,0},{... | collective-permute-start | bytes 393224 | tf_op jit(solution)/shard_map/ppermute | solution.py:175
  31.6 12.4 %collective-permute-start.7 = (f32[32,1024]{1,0:T(8,128)}, f32[32,1024]{1,0:T(8,128)S(1)}, u32[]{:S(2)}, u32[]{:S(2)}) collective-permute-start(f32[32,1024]{1,0:T(8,128)} %slice.17), channel_id=1, source_target_pairs={{0,384},{64,448},{128,0},{192,64},{256,128},{320,192},{384,256},{4... | collective-permute-start | bytes 393224 | tf_op jit(solution)/shard_map/ppermute | solution.py:175
  36.5 9.7 %collective-permute-start.4 = (f32[64,1024]{1,0:T(8,128)S(1)}, f32[64,1024]{1,0:T(8,128)S(1)}, u32[]{:S(2)}, u32[]{:S(2)}) collective-permute-start(f32[64,1024]{1,0:T(8,128)S(1)} %collective-permute-done.3.refs_7_), channel_id=1, source_target_pairs={{0,64},{64,128},{128,192},{192,256},{256,320},{320,384},{384,448},... | collective-permute-start | bytes 786440 | tf_op jit(solution)/shard_map/ppermute | solution.py:175
  51.9 16.0 %all-to-all-start.1 = ((f32[4,64,1024]{2,1,0:T(8,128)}), f32[4,64,1024]{2,1,0:T(8,128)S(1)}, u32[]{:S(2)}, u32[]{:S(2)}) async-start(f32[4,64,1024]{2,1,0:T(8,128)} %pack.1), calls=%async_computation.1 | async-start | bytes 2097152 | tf_op jit(solution)/shard_map/all_to_all | solution.py:21
  68.4 10.7 %collective-permute-start.8 = (f32[64,1024]{1,0:T(8,128)S(1)}, f32[64,1024]{1,0:T(8,128)S(1)}, u32[]{:S(2)}, u32[]{:S(2)}) collective-permute-start(f32[64,1024]{1,0:T(8,128)S(1)} %pick.1), channel_id=1, source_target_pairs={{0,1},{1,0},{2,3},{3,2},{4,5},{5,4},{6,7},{7,6},{8,9},{9,8},{10,11... | collective-permute-start | bytes 786440 | tf_op jit(solution)/shard_map/ppermute | solution.py:244
  74.4 73.2 %all-to-all-start.2 = ((f32[4,576,384]{2,1,0:T(8,128)}), f32[4,576,384]{2,1,0:T(8,128)}, u32[]{:S(2)}, u32[]{:S(2)}) async-start(f32[4,576,384]{2,1,0:T(8,128)} %copies.1), calls=%async_computation.2 | async-start | bytes 7077888 | tf_op jit(solution)/shard_map/all_to_all | solution.py:21
  79.2 17.6 %collective-permute-start.10 = (f32[2,64,1024]{2,1,0:T(8,128)S(1)}, f32[2,64,1024]{2,1,0:T(8,128)S(1)}, u32[]{:S(2)}, u32[]{:S(2)}) collective-permute-start(f32[2,64,1024]{2,1,0:T(8,128)S(1)} %pad_maximum_fusion), channel_id=1, source_target_pairs={{0,4},{1,13},{2,6},{3,15},{4,8},{5,1},{6,10},{7,3},{8,12},{9,5},{1... | collective-permute-start | bytes 1572872 | tf_op jit(solution)/shard_map/ppermute | solution.py:252
  85.1 21.6 %collective-permute-start.9 = (f32[2,64,1024]{2,1,0:T(8,128)S(1)}, f32[2,64,1024]{2,1,0:T(8,128)S(1)}, u32[]{:S(2)}, u32[]{:S(2)}) collective-permute-start(f32[2,64,1024]{2,1,0:T(8,128)S(1)} %pad_maximum_fusion), channel_id=1, source_target_pairs={{0,2},{1,15},{2,4},{3,1},{4,6},{5,3},{6,8},{7,5},{8,10},{9,7},{10,... | collective-permute-start | bytes 1572872 | tf_op jit(solution)/shard_map/ppermute | solution.py:252
  96.8 12.7 %collective-permute-start.11 = (f32[2,64,1024]{2,1,0:T(8,128)S(1)}, f32[2,64,1024]{2,1,0:T(8,128)S(1)}, u32[]{:S(2)}, u32[]{:S(2)}) collective-permute-start(f32[2,64,1024]{2,1,0:T(8,128)S(1)} %collective-permute-done.10), channel_id=1, source_target_pairs={{0,2},{1,15},{2,4},{3,1},{4,6},{5,3},{6,8},{7,5},{8,10},{9,7},{10,... | collective-permute-start | bytes 1572872 | tf_op jit(solution)/shard_map/ppermute | solution.py:252
  101.1 12.8 %collective-permute-start.15 = (f32[64,1024]{1,0:T(8,128)S(1)}, f32[64,1024]{1,0:T(8,128)S(1)}, u32[]{:S(2)}, u32[]{:S(2)}) collective-permute-start(f32[64,1024]{1,0:T(8,128)S(1)} %slice_bitcast_fusion), channel_id=1, source_target_pairs={{0,4},{1,13},{2,6},{3,15},{4,8},{5,1},{6,10},{7,3},{8,12},{9,5},{1... | collective-permute-start | bytes 786440 | tf_op jit(solution)/shard_map/ppermute | solution.py:252
  104.8 14.0 %collective-permute-start.13 = (f32[2,64,1024]{2,1,0:T(8,128)S(1)}, f32[2,64,1024]{2,1,0:T(8,128)S(1)}, u32[]{:S(2)}, u32[]{:S(2)}) collective-permute-start(f32[2,64,1024]{2,1,0:T(8,128)S(1)} %collective-permute-done.10), channel_id=1, source_target_pairs={{0,1},{1,0},{2,3},{3,2},{4,5},{5,4},{6,7},{7,6},{8,9},{9,8},{10,11... | collective-permute-start | bytes 1572872 | tf_op jit(solution)/shard_map/ppermute | solution.py:244
  106.8 12.1 %collective-permute-start.12 = (f32[2,64,1024]{2,1,0:T(8,128)S(1)}, f32[2,64,1024]{2,1,0:T(8,128)S(1)}, u32[]{:S(2)}, u32[]{:S(2)}) collective-permute-start(f32[2,64,1024]{2,1,0:T(8,128)S(1)} %collective-permute-done.9), channel_id=1, source_target_pairs={{0,1},{1,0},{2,3},{3,2},{4,5},{5,4},{6,7},{7,6},{8,9},{9,8},{10,11... | collective-permute-start | bytes 1572872 | tf_op jit(solution)/shard_map/ppermute | solution.py:244
  109.5 9.3 %collective-permute-start.14 = (f32[2,64,1024]{2,1,0:T(8,128)S(1)}, f32[2,64,1024]{2,1,0:T(8,128)}, u32[]{:S(2)}, u32[]{:S(2)}) collective-permute-start(f32[2,64,1024]{2,1,0:T(8,128)S(1)} %collective-permute-done.11), channel_id=1, source_target_pairs={{0,1},{1,0},{2,3},{3,2},{4,5},{5,4},{6,7},{7,6},{8,9},{9,8},{10,11... | collective-permute-start | bytes 1572872 | tf_op jit(solution)/shard_map/ppermute | solution.py:244
  131.5 16.2 %collective-permute-start.17 = (f32[256,256]{1,0:T(8,128)S(1)}, f32[256,256]{1,0:T(8,128)S(1)}, u32[]{:S(2)}, u32[]{:S(2)}) collective-permute-start(f32[256,256]{1,0:T(8,128)S(1)} %get-tuple-element.57), channel_id=1, source_target_pairs={{0,16},{16,32},{32,48},{48,0},{1,17},{17,33},{33,49},{49,1},{2,18}... | collective-permute-start | bytes 786440 | tf_op jit(solution)/shard_map/ppermute | solution.py:305
  135.2 15.9 %collective-permute-start.18 = (f32[256,256]{1,0:T(8,128)S(1)}, f32[256,256]{1,0:T(8,128)S(1)}, u32[]{:S(2)}, u32[]{:S(2)}) collective-permute-start(f32[256,256]{1,0:T(8,128)S(1)} %get-tuple-element.58), channel_id=1, source_target_pairs={{0,32},{16,48},{32,0},{48,16},{1,33},{17,49},{33,1},{49,17},{2,34}... | collective-permute-start | bytes 786440 | tf_op jit(solution)/shard_map/ppermute | solution.py:305
  139.5 11.6 %collective-permute-start.19 = (f32[256,256]{1,0:T(8,128)S(1)}, f32[256,256]{1,0:T(8,128)S(1)}, u32[]{:S(2)}, u32[]{:S(2)}) collective-permute-start(f32[256,256]{1,0:T(8,128)S(1)} %get-tuple-element.59), channel_id=1, source_target_pairs={{0,48},{16,0},{32,16},{48,32},{1,49},{17,1},{33,17},{49,33},{2,50}... | collective-permute-start | bytes 786440 | tf_op jit(solution)/shard_map/ppermute | solution.py:305
  142.6 21.5 %collective-permute-start.20 = (f32[256,512]{1,0:T(8,128)}, f32[256,512]{1,0:T(8,128)S(1)}, u32[]{:S(2)}, u32[]{:S(2)}) collective-permute-start(f32[256,512]{1,0:T(8,128)} %get-tuple-element.62), channel_id=1, source_target_pairs={{0,16},{16,32},{32,48},{48,0},{1,17},{17,33},{33,49},{49,1},{2,18}... | collective-permute-start | bytes 1572872 | tf_op jit(solution)/shard_map/ppermute | solution.py:305
  144.8 26.9 %collective-permute-start.21 = (f32[256,512]{1,0:T(8,128)}, f32[256,512]{1,0:T(8,128)S(1)}, u32[]{:S(2)}, u32[]{:S(2)}) collective-permute-start(f32[256,512]{1,0:T(8,128)} %get-tuple-element.63), channel_id=1, source_target_pairs={{0,32},{16,48},{32,0},{48,16},{1,33},{17,49},{33,1},{49,17},{2,34}... | collective-permute-start | bytes 1572872 | tf_op jit(solution)/shard_map/ppermute | solution.py:305
  147.6 25.2 %collective-permute-start.22 = (f32[256,512]{1,0:T(8,128)}, f32[256,512]{1,0:T(8,128)S(1)}, u32[]{:S(2)}, u32[]{:S(2)}) collective-permute-start(f32[256,512]{1,0:T(8,128)} %get-tuple-element.64), channel_id=1, source_target_pairs={{0,48},{16,0},{32,16},{48,32},{1,49},{17,1},{33,17},{49,33},{2,50}... | collective-permute-start | bytes 1572872 | tf_op jit(solution)/shard_map/ppermute | solution.py:305
  (15 other events, 207.7 us)
